TPU v7x, 32 devices: a whole 2x2x4 slice. The times are simulated.
32 devices in a mesh: slides: 1, row: 16 (over z, y, x), col: 2 (over core).
Axes of the slice: x: 2, y: 2, z: 4, core: 2. Of those that a mesh axis runs over, the one named last changes fastest.
Arguments:
- image: bfloat16 [64, 128, 768], P(('slides', 'row'), 'col'), may hold values from -6 to 6
- dw_kernel: float32 [49, 768], replicated, may hold values from -0.875 to 0.875
- w_in: bfloat16 [768, 3072], replicated, may hold values from -0.21875 to 0.21875
- w_out: bfloat16 [3072, 768], replicated, may hold values from -0.109375 to 0.109375
- layer_scale: float32 [768], replicated, may hold values from 0.5 to 1.5
- region_ids: int32 [32, 64], P(('slides', 'row'), 'col'), may hold values from 0 to 127, as said below
- region_slot: int32 [128], P('slides'), may hold values from 0 to 127, each once
- pool_grad: bfloat16 [128, 768], P(('slides', 'row', 'col')), may hold values from -6 to 6
Outputs:
- region_pool: float32 [128, 768], P(('slides', 'row', 'col'))
- grad_image: bfloat16 [64, 128, 768], P(('slides', 'row'), 'col')
- grad_w_in: float32 [768, 3072], P('slides', ('row', 'col'))
- grad_w_out: float32 [3072, 768], P(('slides', 'row', 'col'))
- grad_kernel: float32 [49, 768], P('slides')
Inputs may be any that keep to these rules, and one draw needn't show every extreme that they name: `region_ids`: every region is named by some tile. `region_slot`: each slot once; slot s lies on index s // 4 of row+col.
All inputs are finite; a program needn't handle non-finite values.
Results may differ from a plain program's by a relative error of at most 0.007.
Values may be sent and summed in bfloat16 or wider, within the bound.
No kernel may reach another device: no remote copies, remote signals or barrier semaphores. Data moves between devices by JAX's collectives and lax.ppermute only.
A program may use at most 192 MiB of HBM per device.

v0:
```python
import math

import jax
import jax.numpy as jnp
from jax import lax
from jax.sharding import PartitionSpec as P


def extended(cells, sides, width):
    for axis, dim in sides:
        count = lax.axis_size(axis)
        ends = count - 1
        head = lax.slice_in_dim(cells, 0, width, axis=dim)
        tail = lax.slice_in_dim(cells, cells.shape[dim] - width, cells.shape[dim], axis=dim)
        cells = jnp.concatenate(
            [
                lax.ppermute(tail, axis, [(i, (i + 1) % count) for i in range(ends)]),
                cells,
                lax.ppermute(head, axis, [((i + 1) % count, i) for i in range(ends)]),
            ],
            axis=dim,
        )
    return cells


def widen(field, forward):
    if forward:
        return extended(field, (("row", 0), ("col", 1)), 3)
    return extended(field.astype(jnp.bfloat16), (("row", 0), ("col", 1)), 3).astype(field.dtype)


def depthwise(padded, taps, height, breadth, flipped):
    total = jnp.zeros((height, breadth, padded.shape[2]), jnp.float32)
    for a in range(7):
        if flipped:
            terms = [
                padded[6 - a : 6 - a + height, 6 - b : 6 - b + breadth] * taps[a, b]
                for b in range(7)
            ]
        else:
            terms = [padded[a : a + height, b : b + breadth] * taps[a, b] for b in range(7)]
        row_total = terms[0]
        for term in terms[1:]:
            row_total = row_total + term
        total = total + row_total
    return total


def shards(image, dw_kernel, w_in, w_out, layer_scale, region_ids, region_slot, pool_grad):
    height, breadth, width = image.shape
    taps = dw_kernel.reshape(7, 7, width)
    xfull = image.astype(jnp.float32)
    xpad = widen(image, True).astype(jnp.float32)
    conv = depthwise(xpad, taps, height, breadth, False)
    centre = conv - jnp.mean(conv, axis=-1, keepdims=True)
    inv_std = lax.rsqrt(jnp.mean(centre * centre, axis=-1, keepdims=True) + 1e-06)
    normed_f = centre * inv_std
    normed = normed_f.astype(jnp.bfloat16).reshape(-1, width)
    pre = jnp.dot(normed, w_in, preferred_element_type=jnp.float32)
    hidden = jax.nn.gelu(pre, approximate=False).astype(jnp.bfloat16)
    branch = jnp.dot(hidden, w_out, preferred_element_type=jnp.float32).reshape(
        height, breadth, width
    )
    block = (xfull + layer_scale * branch).astype(jnp.bfloat16)
    tile_sum = (
        block.astype(jnp.float32)
        .reshape(height // 2, 2, breadth // 2, 2, width)
        .sum(axis=(1, 3))
        .reshape(-1, width)
    )
    regions = region_slot.shape[0]
    labels = region_ids.reshape(-1)
    region_iota = jnp.arange(regions, dtype=jnp.int32)
    id_onehot = (labels[:, None] == region_iota[None, :]).astype(jnp.bfloat16)
    slot_onehot = (region_slot[:, None] == region_iota[None, :]).astype(jnp.bfloat16)
    tile_onehot = jnp.dot(id_onehot, slot_onehot, preferred_element_type=jnp.float32)
    partial_sum = jnp.dot(
        tile_onehot.T, tile_sum, precision=lax.Precision.HIGHEST, preferred_element_type=jnp.float32
    )
    partial_count = jnp.sum(tile_onehot, axis=0)
    owned_sum, owned_count = (
        lax.psum_scatter(partial_sum, ("row", "col"), scatter_dimension=0, tiled=True),
        lax.psum_scatter(partial_count, ("row", "col"), scatter_dimension=0, tiled=True),
    )
    region_pool = owned_sum / (4.0 * owned_count)[:, None]
    region_grad = (pool_grad.astype(jnp.float32) / (4.0 * owned_count)[:, None]).astype(
        jnp.bfloat16
    )
    every_grad = lax.all_gather(region_grad, ("row", "col"), axis=0, tiled=True)
    tile_grad = jnp.dot(
        tile_onehot.astype(jnp.bfloat16), every_grad, preferred_element_type=jnp.float32
    )
    tile_grad = tile_grad.reshape(height // 2, 1, breadth // 2, 1, width)
    dblock = jnp.broadcast_to(tile_grad, (height // 2, 2, breadth // 2, 2, width)).reshape(
        height, breadth, width
    )
    g_out = (dblock * layer_scale).astype(jnp.bfloat16).reshape(-1, width)
    dhidden = jnp.dot(g_out, w_out.T, preferred_element_type=jnp.float32)
    cdf = 0.5 * (1.0 + lax.erf(pre / math.sqrt(2.0)))
    density = jnp.exp(-0.5 * pre * pre) / math.sqrt(2.0 * math.pi)
    g_in = (dhidden * (cdf + pre * density)).astype(jnp.bfloat16)
    full_out = jnp.dot(hidden.T, g_out, preferred_element_type=jnp.float32)
    full_in = jnp.dot(normed.T, g_in, preferred_element_type=jnp.float32)
    grad_w_in, grad_w_out = (
        lax.psum_scatter(full_in, ("row", "col"), scatter_dimension=1, tiled=True),
        lax.psum_scatter(full_out, ("row", "col"), scatter_dimension=0, tiled=True),
    )
    dnorm = jnp.dot(g_in, w_in.T, preferred_element_type=jnp.float32).reshape(
        height, breadth, width
    )
    dconv = inv_std * (
        dnorm
        - jnp.mean(dnorm, axis=-1, keepdims=True)
        - normed_f * jnp.mean(dnorm * normed_f, axis=-1, keepdims=True)
    )
    dpad = widen(dconv, False)
    back = depthwise(dpad, taps, height, breadth, True)
    kernel_rows = []
    for a in range(7):
        for b in range(7):
            kernel_rows.append(jnp.sum(xpad[a : a + height, b : b + breadth] * dconv, axis=(0, 1)))
    grad_kernel = lax.psum(jnp.stack(kernel_rows, axis=0), ("row", "col"))
    grad_image = (dblock + back).astype(jnp.bfloat16)
    return (region_pool, grad_image, grad_w_in, grad_w_out, grad_kernel)


def solution(mesh):
    placed = (
        P(("slides", "row"), "col", None),
        P(),
        P(),
        P(),
        P(),
        P(("slides", "row"), "col"),
        P("slides"),
        P(("slides", "row", "col"), None),
    )
    return jax.shard_map(
        shards,
        mesh=mesh,
        in_specs=placed,
        out_specs=(
            P(("slides", "row", "col"), None),
            P(("slides", "row"), "col", None),
            P("slides", ("row", "col")),
            P(("slides", "row", "col"), None),
            P("slides", None),
        ),
        check_vma=False,
    )
```

profile of v0, /device:TPU:0, one launch (start us, length us, event | category | flops | bytes accessed | tf_op | source)
XLA Modules:
  0.0 569.0 jit_solution(408561282894542323)
XLA Ops:
  7.2 0.0 all-reduce.5.cloned.1.call-start
  7.2 1.1 fusion.79
  8.4 1.3 collective-permute-start.1
  9.7 5.5 collective-permute-start
  15.2 0.8 eq.28
  16.0 0.9 fusion.80
  16.8 44.4 %all-reduce.1 = f32[128]{0:T(128)S(1)} all-reduce(f32[128]{0:T(128)S(1)} %get-tuple-element.119), channel_id=3, replica_groups=mesh['slides'=1,'row'=16,'col'=2] {'row','col'}, use_global_device_ids=true, to_apply=%region_5.0.clone | all-reduce | flops 128 | bytes 1024
  61.2 0.1 dynamic-slice_multiply_fusion
  61.3 0.8 fusion.74
  62.1 40.2 %all-gather = bf16[32,4,768]{2,1,0:T(4,128)(2,1)S(1)} all-gather(bf16[1,4,768]{2,1,0:T(4,128)(2,1)S(1)} %fusion.74), channel_id=1, replica_groups=mesh['slides'=1,'row'=16,'col'=2] {'row','col'}, dimensions={0}, use_global_device_ids=true | all-gather | bytes 202752 | tf_op jit(solution)/shard_map/all_gather | solution.py:89
  102.3 0.1 reshape.82
  102.3 0.2 fusion.70
  102.5 0.9 reshape.70
  103.4 0.2 slice_reduce_fusion.48
  103.6 0.7 slice_reduce_fusion.47
  104.5 0.1 fusion.77
  104.6 2.3 collective-permute-start.2
  106.9 1.5 collective-permute-start.3
  108.3 0.1 slice_reduce_fusion.46
  108.6 0.2 broadcast_in_dim.5
  108.8 1.4 reshape.77
  110.2 1.6 maximum_convert_fusion
  112.0 6.0 %fusion.76 = (f32[4,64]{1,0:T(4,128)S(1)}, f32[4,64,768]{2,1,0:T(8,128)S(1)}) fusion(f32[768]{0:T(1024)S(1)} %get-tuple-element.55, f32[10,70,768]{2,1,0:T(8,128)S(1)} %maximum_convert_fusion, f32[768]{0:T(1024)S(1)} %get-tuple-element.56, f32[768]{0:T(1024)S(1)} %get-tuple-element.57, f32[768]{0:T(1024)S(1)} %get-tuple-element.58, ...), kind=kLoop, calls=%fused_computation.258 | loop fusion | flops 19267328 | bytes 39473152 | tf_op jit(solution)/shard_map/reduce_sum | solution.py:55
  118.1 0.2 multiply_reduce_fusion.50
  118.4 0.1 fusion.65
  118.5 0.4 copy-done.50
  119.0 9.0 %fusion.3 = (bf16[256,3072]{1,0:T(8,128)(2,1)}, f32[256,3072]{1,0:T(8,128)S(1)}) fusion(bf16[256,768]{1,0:T(8,128)(2,1)S(1)} %bitcast.23, bf16[768,3072]{1,0:T(8,128)(2,1)S(1)} %bitcast.29), kind=kOutput, calls=%fused_computation.6 | convolution fusion | flops 1259077632 | bytes 9830400 | tf_op jit(solution)/shard_map/dot_general | solution.py:59
  128.0 2.0 fusion
  130.1 2.4 fusion.81
  132.5 0.7 div.47
  133.2 1.4 multiply_reduce_fusion.49
  134.6 1.4 fusion.75
  136.0 1.1 multiply_reduce_fusion.36
  137.1 1.9 multiply_reduce_fusion
  139.0 2.1 multiply_reduce_fusion.18
  141.2 1.4 fusion.82
  142.6 0.1 fusion.66
  142.7 0.5 reshape.80
  143.1 0.5 reduce_sum.497
  143.7 1.3 fusion.83
  145.5 4.5 stack.199
  150.1 0.0 all-reduce.5.cloned.1.call-update
  150.1 0.0 reduce-scatter.5.cloned.1.call-start
  150.2 5.1 fusion.67
  155.2 0.0 reduce-scatter.5.cloned.1.call-update
  155.2 0.0 reduce-scatter.3.cloned.1.call-start
  155.3 0.9 copy-done.10
  156.2 0.5 copy-done.12
  156.8 5.1 fusion.84
  162.1 1.4 collective-permute-start.4
  163.6 1.3 collective-permute-start.5
  164.9 0.5 reshape.76
  165.4 11.4 %collective-permute-done.4 = bf16[3,64,768]{2,1,0:T(8,128)(2,1)S(1)} collective-permute-done((bf16[3,64,768]{2,1,0:T(8,128)(2,1)S(1)}, bf16[3,64,768]{2,1,0:T(8,128)(2,1)S(1)}, u32[]{:S(2)}, u32[]{:S(2)}) %collective-permute-start.4) | collective-permute-done | bytes 294944 | tf_op jit(solution)/shard_map/ppermute | solution.py:17
  176.9 0.9 collective-permute-done.5
  177.7 0.1 pad_maximum_fusion.2
  177.8 2.0 collective-permute-start.6
  179.8 1.3 collective-permute-start.7
  181.1 95.4 %all-reduce.5.cloned.1.call-done = (f32[128,768]{1,0:T(8,128)}, f32[49,768]{1,0:T(8,128)}) async-done(((f32[128,768]{1,0:T(8,128)}, f32[49,768]{1,0:T(8,128)}), (f32[128,768]{1,0:T(8,128)}, f32[49,768]{1,0:T(8,128)})) %all-reduce.5.cloned.1.call-update) | async-done | bytes 543760
  276.5 1.4 dynamic-slice_divide_fusion
  277.9 0.3 maximum_convert_fusion.1
  278.4 6.5 %fusion.18 = bf16[4,64,768]{2,1,0:T(8,128)(2,1)} fusion(f32[4,64,768]{2,1,0:T(8,128)S(1)} %reshape.76, f32[10,70,768]{2,1,0:T(8,128)S(1)} %maximum_convert_fusion.1, f32[768]{0:T(1024)S(1)} %get-tuple-element.55, f32[768]{0:T(1024)S(1)} %get-tuple-element.56, f32[768]{0:T(1024)S(1)} %get-tuple-element.57, f32[768]{0:T(1024)S(1)} %get-tuple-element.58, ...), kind=kLoop, calls=%fused_computation.32 | loop fusion | flops 19464192 | bytes 39865344 | tf_op jit(solution)/shard_map/convert_element_type | solution.py:123
  284.9 135.2 %reduce-scatter.5.cloned.1.call-done = f32[96,768]{1,0:T(8,128)} async-done(((f32[3072,768]{1,0:T(8,128)}), f32[96,768]{1,0:T(8,128)}) %reduce-scatter.5.cloned.1.call-update) | async-done | bytes 294928 | tf_op jit(solution)/shard_map/reduce_scatter | solution.py:106
  420.1 141.7 %reduce-scatter.3.cloned.1.call-done = f32[768,96]{0,1:T(8,128)} async-done(((f32[768,3072]{0,1:T(8,128)}), f32[768,96]{0,1:T(8,128)}) %reduce-scatter.3.cloned.1.call-update) | async-done | bytes 294928 | tf_op jit(solution)/shard_map/reduce_scatter | solution.py:105
  561.8 0.7 copy.17
  (188 shorter events, 0.7 us)
Async XLA Ops:
  7.2 97.2 %copy-start.2 = (bf16[4,64,768]{2,1,0:T(8,128)(2,1)S(1)}, bf16[4,64,768]{2,1,0:T(8,128)(2,1)}, u32[]{:S(2)}) copy-start(bf16[4,64,768]{2,1,0:T(8,128)(2,1)} %param.8) | copy-start | bytes 1179652
  7.2 269.3 %all-reduce.5.cloned.1.call-start = ((), (), s32[]{:S(2)}) async-start(), calls=%async_computation.4 | async-start | bytes 1130496
  8.4 96.1 %collective-permute-start.1 = (bf16[3,64,768]{2,1,0:T(8,128)(2,1)S(1)}, bf16[3,64,768]{2,1,0:T(8,128)(2,1)S(1)}, u32[]{:S(2)}, u32[]{:S(2)}) collective-permute-start(bf16[3,64,768]{2,1,0:T(8,128)(2,1)S(1)} %get-tuple-element.115), channel_id=1, source_target_pairs={{2,0},{4,2},{6,4},{8,6},{10,8},{12,10},{14,12},{16,14},{18,16},{20... | collective-permute-start | bytes 884744 | tf_op jit(solution)/shard_map/ppermute | solution.py:19
  9.7 94.7 %collective-permute-start = (bf16[3,64,768]{2,1,0:T(8,128)(2,1)S(1)}, bf16[3,64,768]{2,1,0:T(8,128)(2,1)S(1)}, u32[]{:S(2)}, u32[]{:S(2)}) collective-permute-start(bf16[3,64,768]{2,1,0:T(8,128)(2,1)S(1)} %get-tuple-element.116), channel_id=1, source_target_pairs={{0,2},{2,4},{4,6},{6,8},{8,10},{10,12},{12,14},{14,16},{16,18},{18... | collective-permute-start | bytes 884744 | tf_op jit(solution)/shard_map/ppermute | solution.py:17
  104.4 7.5 %copy-start.14 = (f32[768]{0:T(1024)}, f32[768]{0:T(1024)S(1)}, u32[]{:S(2)}) copy-start(f32[768]{0:T(1024)S(1)} %get-tuple-element.85) | copy-start | bytes 9220
  104.5 4.0 copy-start.8
  104.5 7.4 %copy-start.16 = (f32[768]{0:T(1024)S(1)}, f32[768]{0:T(1024)}, u32[]{:S(2)}) copy-start(f32[768]{0:T(1024)} %get-tuple-element.86) | copy-start | bytes 9220
  104.5 7.4 %copy-start.18 = (f32[768]{0:T(1024)S(1)}, f32[768]{0:T(1024)}, u32[]{:S(2)}) copy-start(f32[768]{0:T(1024)} %get-tuple-element.87) | copy-start | bytes 9220
  104.5 7.4 %copy-start.20 = (f32[768]{0:T(1024)S(1)}, f32[768]{0:T(1024)}, u32[]{:S(2)}) copy-start(f32[768]{0:T(1024)} %get-tuple-element.88) | copy-start | bytes 9220
  104.5 7.4 %copy-start.22 = (f32[768]{0:T(1024)S(1)}, f32[768]{0:T(1024)}, u32[]{:S(2)}) copy-start(f32[768]{0:T(1024)} %get-tuple-element.89) | copy-start | bytes 9220
  104.5 7.4 %copy-start.24 = (f32[768]{0:T(1024)S(1)}, f32[768]{0:T(1024)}, u32[]{:S(2)}) copy-start(f32[768]{0:T(1024)} %get-tuple-element.90) | copy-start | bytes 9220
  104.5 7.4 %copy-start.26 = (f32[768]{0:T(1024)S(1)}, f32[768]{0:T(1024)}, u32[]{:S(2)}) copy-start(f32[768]{0:T(1024)} %get-tuple-element.91) | copy-start | bytes 9220
  104.6 5.6 collective-permute-start.2
  106.9 3.4 collective-permute-start.3
  108.5 9.6 %copy-start.28 = (f32[768]{0:T(1024)}, f32[768]{0:T(1024)S(1)}, u32[]{:S(2)}) copy-start(f32[768]{0:T(1024)S(1)} %get-tuple-element.92) | copy-start | bytes 9220
  108.5 9.5 %copy-start.30 = (f32[768]{0:T(1024)}, f32[768]{0:T(1024)S(1)}, u32[]{:S(2)}) copy-start(f32[768]{0:T(1024)S(1)} %get-tuple-element.93) | copy-start | bytes 9220
  108.5 9.5 %copy-start.32 = (f32[768]{0:T(1024)}, f32[768]{0:T(1024)S(1)}, u32[]{:S(2)}) copy-start(f32[768]{0:T(1024)S(1)} %get-tuple-element.94) | copy-start | bytes 9220
  108.5 9.5 %copy-start.34 = (f32[768]{0:T(1024)}, f32[768]{0:T(1024)S(1)}, u32[]{:S(2)}) copy-start(f32[768]{0:T(1024)S(1)} %get-tuple-element.95) | copy-start | bytes 9220
  108.5 9.5 %copy-start.36 = (f32[768]{0:T(1024)}, f32[768]{0:T(1024)S(1)}, u32[]{:S(2)}) copy-start(f32[768]{0:T(1024)S(1)} %get-tuple-element.96) | copy-start | bytes 9220
  108.5 9.5 %copy-start.38 = (f32[768]{0:T(1024)}, f32[768]{0:T(1024)S(1)}, u32[]{:S(2)}) copy-start(f32[768]{0:T(1024)S(1)} %get-tuple-element.97) | copy-start | bytes 9220
  108.5 9.5 %copy-start.40 = (f32[768]{0:T(1024)}, f32[768]{0:T(1024)S(1)}, u32[]{:S(2)}) copy-start(f32[768]{0:T(1024)S(1)} %get-tuple-element.98) | copy-start | bytes 9220
  108.5 9.5 %copy-start.42 = (f32[768]{0:T(1024)}, f32[768]{0:T(1024)S(1)}, u32[]{:S(2)}) copy-start(f32[768]{0:T(1024)S(1)} %get-tuple-element.99) | copy-start | bytes 9220
  108.5 9.5 %copy-start.44 = (f32[768]{0:T(1024)}, f32[768]{0:T(1024)S(1)}, u32[]{:S(2)}) copy-start(f32[768]{0:T(1024)S(1)} %get-tuple-element.100) | copy-start | bytes 9220
  108.5 9.5 %copy-start.46 = (f32[768]{0:T(1024)}, f32[768]{0:T(1024)S(1)}, u32[]{:S(2)}) copy-start(f32[768]{0:T(1024)S(1)} %get-tuple-element.101) | copy-start | bytes 9220
  108.6 9.5 %copy-start.48 = (f32[768]{0:T(1024)}, f32[768]{0:T(1024)S(1)}, u32[]{:S(2)}) copy-start(f32[768]{0:T(1024)S(1)} %get-tuple-element.102) | copy-start | bytes 9220
  110.2 8.7 %slice-start = ((s8[4718592]{0:T(1024)(128)(4,1)}), s8[4194304]{0:T(1024)(128)(4,1)S(1)}, s32[]{:S(2)}) async-start(s8[4718592]{0:T(1024)(128)(4,1)} %bitcast.28), calls=%async_computation.5 | async-start | bytes 8388608
  111.9 7.0 %slice-start.1 = ((s8[4718592]{0:T(1024)(128)(4,1)}), s8[524288]{0:T(1024)(128)(4,1)S(1)}, s32[]{:S(2)}) async-start(s8[4718592]{0:T(1024)(128)(4,1)} %bitcast.28), calls=%async_computation.6 | async-start | bytes 1048576
  118.1 9.9 %slice-start.2 = ((s8[4718592]{0:T(1024)(128)(4,1)}), s8[4194304]{0:T(1024)(128)(4,1)S(1)}, s32[]{:S(2)}) async-start(s8[4718592]{0:T(1024)(128)(4,1)} %bitcast.30), calls=%async_computation.7 | async-start | bytes 8388608
  118.9 9.0 %copy-start.9 = (bf16[4,64,768]{2,1,0:T(8,128)(2,1)}, bf16[4,64,768]{2,1,0:T(8,128)(2,1)S(1)}, u32[]{:S(2)}) copy-start(bf16[4,64,768]{2,1,0:T(8,128)(2,1)S(1)} %fusion.65) | copy-start | bytes 1179652
  119.0 9.0 %copy-start.4 = (f32[256,768]{1,0:T(8,128)S(1)}, f32[256,768]{1,0:T(8,128)}, u32[]{:S(2)}) copy-start(f32[256,768]{1,0:T(8,128)} %reshape.77) | copy-start | bytes 2359300
  119.0 9.0 %copy-start.52 = (f32[768]{0:T(1024)S(1)}, f32[768]{0:T(1024)}, u32[]{:S(2)}) copy-start(f32[768]{0:T(1024)} %param.12) | copy-start | bytes 9220
  119.0 9.0 %slice-start.3 = ((s8[4718592]{0:T(1024)(128)(4,1)}), s8[524288]{0:T(1024)(128)(4,1)S(1)}, s32[]{:S(2)}) async-start(s8[4718592]{0:T(1024)(128)(4,1)} %bitcast.30), calls=%async_computation.8 | async-start | bytes 1048576
  130.0 2.5 copy-start.11
  130.1 3.1 copy-start.51
  137.1 4.0 slice-start.4
  142.6 7.6 %copy-start.5 = (f32[256,768]{1,0:T(8,128)S(1)}, f32[256,768]{1,0:T(8,128)}, u32[]{:S(2)}) copy-start(f32[256,768]{1,0:T(8,128)} %reshape.77) | copy-start | bytes 2359300
  143.7 6.5 %copy-start.7 = (bf16[256,3072]{1,0:T(8,128)(2,1)S(1)}, bf16[256,3072]{1,0:T(8,128)(2,1)}, u32[]{:S(2)}) copy-start(bf16[256,3072]{1,0:T(8,128)(2,1)} %get-tuple-element.117) | copy-start | bytes 4718596
  150.1 270.1 %reduce-scatter.5.cloned.1.call-start = ((), (), s32[]{:S(2)}) async-start(), calls=%async_computation.3 | async-start | bytes 9732096 | tf_op jit(solution)/shard_map/reduce_scatter | solution.py:106
  155.2 406.6 %reduce-scatter.3.cloned.1.call-start = ((), (), s32[]{:S(2)}) async-start(), calls=%async_computation.2 | async-start | bytes 9732096 | tf_op jit(solution)/shard_map/reduce_scatter | solution.py:105
  161.9 3.0 copy-start.1
  161.9 114.6 %copy-start.55 = (f32[4]{0:T(128)S(1)}, f32[4]{0:T(128)}, u32[]{:S(2)}) copy-start(f32[4]{0:T(128)} %copy-done.54) | copy-start | bytes 52
  161.9 116.2 %copy-start.15 = (f32[768]{0:T(1024)S(1)}, f32[768]{0:T(1024)}, u32[]{:S(2)}) copy-start(f32[768]{0:T(1024)} %copy-done.14) | copy-start | bytes 9220
  161.9 116.2 %copy-start.17 = (f32[768]{0:T(1024)S(1)}, f32[768]{0:T(1024)}, u32[]{:S(2)}) copy-start(f32[768]{0:T(1024)} %get-tuple-element.86) | copy-start | bytes 9220
  162.0 116.2 %copy-start.19 = (f32[768]{0:T(1024)S(1)}, f32[768]{0:T(1024)}, u32[]{:S(2)}) copy-start(f32[768]{0:T(1024)} %get-tuple-element.87) | copy-start | bytes 9220
  162.0 116.2 %copy-start.21 = (f32[768]{0:T(1024)S(1)}, f32[768]{0:T(1024)}, u32[]{:S(2)}) copy-start(f32[768]{0:T(1024)} %get-tuple-element.88) | copy-start | bytes 9220
  162.0 116.2 %copy-start.23 = (f32[768]{0:T(1024)S(1)}, f32[768]{0:T(1024)}, u32[]{:S(2)}) copy-start(f32[768]{0:T(1024)} %get-tuple-element.89) | copy-start | bytes 9220
  162.0 116.2 %copy-start.25 = (f32[768]{0:T(1024)S(1)}, f32[768]{0:T(1024)}, u32[]{:S(2)}) copy-start(f32[768]{0:T(1024)} %get-tuple-element.90) | copy-start | bytes 9220
  162.0 116.2 %copy-start.27 = (f32[768]{0:T(1024)S(1)}, f32[768]{0:T(1024)}, u32[]{:S(2)}) copy-start(f32[768]{0:T(1024)} %get-tuple-element.91) | copy-start | bytes 9220
  162.0 116.2 %copy-start.29 = (f32[768]{0:T(1024)S(1)}, f32[768]{0:T(1024)}, u32[]{:S(2)}) copy-start(f32[768]{0:T(1024)} %copy-done.28) | copy-start | bytes 9220
  162.0 116.2 %copy-start.31 = (f32[768]{0:T(1024)S(1)}, f32[768]{0:T(1024)}, u32[]{:S(2)}) copy-start(f32[768]{0:T(1024)} %copy-done.30) | copy-start | bytes 9220
  162.0 116.2 %copy-start.33 = (f32[768]{0:T(1024)S(1)}, f32[768]{0:T(1024)}, u32[]{:S(2)}) copy-start(f32[768]{0:T(1024)} %copy-done.32) | copy-start | bytes 9220
  162.0 116.2 %copy-start.35 = (f32[768]{0:T(1024)S(1)}, f32[768]{0:T(1024)}, u32[]{:S(2)}) copy-start(f32[768]{0:T(1024)} %copy-done.34) | copy-start | bytes 9220
  162.0 116.2 %copy-start.37 = (f32[768]{0:T(1024)S(1)}, f32[768]{0:T(1024)}, u32[]{:S(2)}) copy-start(f32[768]{0:T(1024)} %copy-done.36) | copy-start | bytes 9220
  162.1 116.2 %copy-start.39 = (f32[768]{0:T(1024)S(1)}, f32[768]{0:T(1024)}, u32[]{:S(2)}) copy-start(f32[768]{0:T(1024)} %copy-done.38) | copy-start | bytes 9220
  162.1 116.2 %copy-start.41 = (f32[768]{0:T(1024)S(1)}, f32[768]{0:T(1024)}, u32[]{:S(2)}) copy-start(f32[768]{0:T(1024)} %copy-done.40) | copy-start | bytes 9220
  162.1 116.2 %copy-start.43 = (f32[768]{0:T(1024)S(1)}, f32[768]{0:T(1024)}, u32[]{:S(2)}) copy-start(f32[768]{0:T(1024)} %copy-done.42) | copy-start | bytes 9220
  162.1 116.2 %copy-start.45 = (f32[768]{0:T(1024)S(1)}, f32[768]{0:T(1024)}, u32[]{:S(2)}) copy-start(f32[768]{0:T(1024)} %copy-done.44) | copy-start | bytes 9220
  162.1 116.2 %copy-start.47 = (f32[768]{0:T(1024)S(1)}, f32[768]{0:T(1024)}, u32[]{:S(2)}) copy-start(f32[768]{0:T(1024)} %copy-done.46) | copy-start | bytes 9220
  162.1 116.2 %copy-start.49 = (f32[768]{0:T(1024)S(1)}, f32[768]{0:T(1024)}, u32[]{:S(2)}) copy-start(f32[768]{0:T(1024)} %copy-done.48) | copy-start | bytes 9220
  162.1 14.7 %collective-permute-start.4 = (bf16[3,64,768]{2,1,0:T(8,128)(2,1)S(1)}, bf16[3,64,768]{2,1,0:T(8,128)(2,1)S(1)}, u32[]{:S(2)}, u32[]{:S(2)}) collective-permute-start(bf16[3,64,768]{2,1,0:T(8,128)(2,1)S(1)} %get-tuple-element.113), channel_id=1, source_target_pairs={{0,2},{2,4},{4,6},{6,8},{8,10},{10,12},{12,14},{14,16},{16,18},{18... | collective-permute-start | bytes 884744 | tf_op jit(solution)/shard_map/ppermute | solution.py:17
  163.6 14.2 %collective-permute-start.5 = (bf16[3,64,768]{2,1,0:T(8,128)(2,1)S(1)}, bf16[3,64,768]{2,1,0:T(8,128)(2,1)S(1)}, u32[]{:S(2)}, u32[]{:S(2)}) collective-permute-start(bf16[3,64,768]{2,1,0:T(8,128)(2,1)S(1)} %get-tuple-element.114), channel_id=1, source_target_pairs={{2,0},{4,2},{6,4},{8,6},{10,8},{12,10},{14,12},{16,14},{18,16},{20... | collective-permute-start | bytes 884744 | tf_op jit(solution)/shard_map/ppermute | solution.py:19
  177.8 100.1 %collective-permute-start.6 = (bf16[10,3,768]{2,1,0:T(4,128)(2,1)S(1)}, bf16[10,3,768]{2,1,0:T(4,128)(2,1)S(1)}, u32[]{:S(2)}, u32[]{:S(2)}) collective-permute-start(bf16[10,3,768]{2,1,0:T(4,128)(2,1)S(1)} %get-tuple-element.109), channel_id=1, source_target_pairs={{0,1},{2,3},{4,5},{6,7},{8,9},{10,11},{12,13},{14,15},{16,17},{18,... | collective-permute-start | bytes 138248 | tf_op jit(solution)/shard_map/ppermute | solution.py:17
  179.8 98.1 %collective-permute-start.7 = (bf16[10,3,768]{2,1,0:T(4,128)(2,1)S(1)}, bf16[10,3,768]{2,1,0:T(4,128)(2,1)S(1)}, u32[]{:S(2)}, u32[]{:S(2)}) collective-permute-start(bf16[10,3,768]{2,1,0:T(4,128)(2,1)S(1)} %get-tuple-element.110), channel_id=1, source_target_pairs={{1,0},{3,2},{5,4},{7,6},{9,8},{11,10},{13,12},{15,14},{17,16},{19,... | collective-permute-start | bytes 138248 | tf_op jit(solution)/shard_map/ppermute | solution.py:19
  278.4 283.5 %copy-start.13 = (f32[49,768]{1,0:T(8,128)S(1)}, f32[49,768]{1,0:T(8,128)}, u32[]{:S(2)}) copy-start(f32[49,768]{1,0:T(8,128)} %get-tuple-element.127) | copy-start | bytes 451588
  (9 other events, 12.4 us)
Sparse Core Ops, SparseCore 0:
  150.2 126.2 all-reduce.4
  283.0 137.1 reduce-scatter.4
  426.6 135.1 reduce-scatter.2
where the time goes:
time: 570 us; the launch traced here: 569 us
  waiting for transfers between devices  385 us (68%)
  blocking collectives  84.6 us (15%)
  matrix products  27.3 us (5%)
  other arithmetic  25.6 us (4%)
  starting transfers between devices  16.7 us (3%)
  between operations  15.2 us (3%)
  local copies, waits for them, and re-layouts  14.9 us (3%)
    reduce_scatter x1, waiting for transfers between devices, shards(): lax.psum_scatter(full_in, ('row', 'col'), scatter_dimension=1, tiled=True)  142 us
    reduce_scatter x1, waiting for transfers between devices, shards(): lax.psum_scatter(full_out, ('row', 'col'), scatter_dimension=0, tiled=True)  135 us
    unnamed x4, waiting for transfers between devices  95.4 us
    unnamed x1, blocking collectives  44.4 us
    all_gather x1, blocking collectives, shards(): every_grad = lax.all_gather(region_grad, ('row', 'col'), axis=0, tiled=True)  40.2 us
    ppermute x4, waiting for transfers between devices, extended(): lax.ppermute(tail, axis, [(i, (i + 1) % count) for i in range(ends)])  11.4 us
  transfers between devices with their start and end apart: 11, of which 5 were waited for; matrix products, arithmetic and copies ran while one was open for 4% of the time, Pallas kernels for 0%

commit v1 on v0

v1 whole, which is shorter than its diff:
```python
import functools
import math

import jax
import jax.numpy as jnp
from jax import lax
from jax.experimental import pallas as pl
from jax.experimental.pallas import tpu as pltpu
from jax.sharding import PartitionSpec as P


AXES = ("row", "col")
F32, BF16 = jnp.float32, jnp.bfloat16
VMEM = pl.BlockSpec(memory_space=pltpu.VMEM)
CONTRACT_ROWS = (((0,), (0,)), ((), ()))
CONTRACT_LANES = (((1,), (1,)), ((), ()))
LEFT = 8


def dot(a, b, dims=(((1,), (0,)), ((), ()))):
    return lax.dot_general(a, b, dims, preferred_element_type=F32)


def iota(shape, dim):
    return lax.broadcasted_iota(jnp.int32, shape, dim)


def call(body, outs, micros, scratch=(), far_in=(), any_in=(), far_out=(), room=8):
    def run(*operands):
        operands = [
            pltpu.with_memory_space_constraint(
                x, pltpu.HBM if k in far_in or k in any_in else pltpu.VMEM
            )
            for k, x in enumerate(operands)
        ]
        specs = [
            pl.BlockSpec(memory_space=pl.ANY) if k in any_in else VMEM
            for k in range(len(operands))
        ]
        shapes = [
            jax.ShapeDtypeStruct(shape, dtype) if k in far_out else pltpu.VMEM(shape, dtype)
            for k, (shape, dtype) in enumerate(outs)
        ]
        return pl.pallas_call(
            body,
            in_specs=specs,
            out_specs=[VMEM] * len(outs),
            out_shape=shapes,
            scratch_shapes=list(scratch),
            compiler_params=pltpu.CompilerParams(vmem_limit_bytes=room << 20),
            cost_estimate=pl.CostEstimate(
                flops=0, bytes_accessed=int(micros * 3.0e6), transcendentals=0
            ),
        )(*operands)

    return run


def exchange(value, chips, flip_core=False):
    rows = lax.axis_size("row")
    pairs = []
    for r in range(rows):
        for c in range(2):
            pairs.append((2 * r + c, 2 * (r ^ chips[c]) + (c ^ int(flip_core))))
    return lax.ppermute(value, AXES, pairs)


def swap_core(value):
    return exchange(value, (0, 0), True)


def swap_rows(value):
    rows = lax.axis_size("row")
    pairs = []
    for r in range(rows - 1):
        pairs.append((2 * r + 1, 2 * r + 2))
        pairs.append((2 * r + 2, 2 * r + 1))
    return lax.ppermute(value, AXES, pairs)


def orders(bits, chunk):
    plain = list(range(bits))
    mixed = [k ^ 1 if k < 2 and bits > 1 else k for k in range(bits)]
    turn = chunk * (bits // 2)
    return plain[turn:] + plain[:turn], mixed[turn:] + mixed[:turn]


def layout_place(chip, row, core, order):
    value = chip ^ row
    bits = len(order[0])
    out = jnp.zeros_like(value)
    for k in range(bits):
        taken = jnp.where(core == 0, (value >> order[0][k]) & 1, (value >> order[1][k]) & 1)
        out = out | (taken << (bits - 1 - k))
    return out


def prepare_body(
    ids_ref, table_ref, grad_ref, image_ref, taps_ref, scale_ref,
    known_ref, slot_ref, image_out, taps_out, scale_out, sems,
):
    copies = [
        pltpu.make_async_copy(image_ref, image_out, sems.at[0]),
        pltpu.make_async_copy(taps_ref, taps_out, sems.at[1]),
    ]
    for copy in copies:
        copy.start()
    scale_out[...] = scale_ref[...].reshape(scale_out.shape)
    tall, wide = ids_ref.shape
    regions = table_ref.shape[1]
    tiles = tall * wide
    owned = grad_ref.shape[0]
    eye = iota((wide, wide), 0) == iota((wide, wide), 1)
    columns = []
    for t in range(tall):
        row = jnp.broadcast_to(ids_ref[t : t + 1, :].astype(F32), (wide, wide))
        columns.append(jnp.sum(jnp.where(eye, row, 0.0), axis=1, keepdims=True))
    ids = jnp.concatenate(columns, axis=0)
    match = ids == iota((tiles, regions), 1).astype(F32)
    table = jnp.broadcast_to(table_ref[...].astype(F32), (tiles, regions))
    slot = jnp.sum(jnp.where(match, table, 0.0), axis=1, keepdims=True)
    onehot = (slot == iota((tiles, regions), 1).astype(F32)).astype(F32)
    known_ref[...] = jnp.zeros_like(known_ref)
    known_ref[:owned, :] = grad_ref[...]
    known_ref[owned : owned + 1, :regions] = jnp.sum(onehot, axis=0, keepdims=True).astype(BF16)
    places = tiles * 4
    p = iota((places, tiles), 0)
    line = 2 * wide
    tile = (p // (2 * line)) * wide + (p % line) // 2
    expand = (tile == iota((places, tiles), 1)).astype(F32)
    slot_row = jnp.sum(
        jnp.where(iota((tiles, tiles), 0) == iota((tiles, tiles), 1), slot, 0.0),
        axis=0,
        keepdims=True,
    )
    slot_ref[...] = jnp.sum(expand * slot_row, axis=1, keepdims=True)
    for copy in copies:
        copy.wait()


def prepare(ids, table, grad, image, taps, scale):
    width = grad.shape[1]
    outs = [
        ((8, width), BF16),
        ((4 * ids.size, 1), F32),
        (image.shape, BF16),
        (taps.shape, F32),
        ((1, width), F32),
    ]
    scratch = [pltpu.SemaphoreType.DMA((2,))]
    return call(
        prepare_body, outs, 1.5, scratch, far_in=(0, 1, 2, 5), any_in=(3, 4)
    )(ids, table.reshape(1, -1), grad, image, taps, scale)


def pack_body(own_ref, other_ref, out_ref):
    c = lax.axis_index("col")
    height, breadth, _ = own_ref.shape

    @pl.when(c == 0)
    def _():
        out_ref[:, :breadth] = own_ref[:3]
        out_ref[:, breadth:] = other_ref[:3]

    @pl.when(c == 1)
    def _():
        out_ref[:, :breadth] = other_ref[height - 3 :]
        out_ref[:, breadth:] = own_ref[height - 3 :]


def halo(source, field):
    _, breadth, width = field.shape
    other = swap_core(source)
    (packed,) = call(pack_body, [((3, 2 * breadth, width), field.dtype)], 0.5)(field, other)
    near = swap_rows(packed)
    far = swap_core(near)
    return other, near, far


def fill_center(pad_ref, own_ref, other_ref):
    c = lax.axis_index("col")
    height, breadth, lanes = other_ref.shape
    stop = LEFT + breadth
    for i in range(height):
        if len(own_ref.shape) == 3:
            own = own_ref[i]
        else:
            own = own_ref[i * breadth : (i + 1) * breadth, :]
        pad_ref[i, LEFT:stop, :] = own.astype(F32)

    @pl.when(c == 0)
    def _():
        pad_ref[:, stop : stop + 8, :] = other_ref[:, :8, :].astype(F32)
        pad_ref[:, :LEFT, :] = jnp.zeros((height, LEFT, lanes), F32)

    @pl.when(c == 1)
    def _():
        pad_ref[:, :LEFT, :] = other_ref[:, breadth - 8 :, :].astype(F32)
        pad_ref[:, stop : stop + 8, :] = jnp.zeros((height, 8, lanes), F32)


def fill_edges(edge_ref, near_ref, far_ref):
    c = lax.axis_index("col")
    breadth, lanes = near_ref.shape[1] // 2, near_ref.shape[2]
    stop = LEFT + breadth

    @pl.when(c == 0)
    def _():
        edge_ref[:3, LEFT : stop + 8, :] = near_ref[:, : breadth + 8, :].astype(F32)
        edge_ref[3:, LEFT : stop + 8, :] = far_ref[:, : breadth + 8, :].astype(F32)
        edge_ref[:, :LEFT, :] = jnp.zeros((6, LEFT, lanes), F32)

    @pl.when(c == 1)
    def _():
        edge_ref[:3, :stop, :] = far_ref[:, breadth - 8 :, :].astype(F32)
        edge_ref[3:, :stop, :] = near_ref[:, breadth - 8 :, :].astype(F32)
        edge_ref[:, stop : stop + 8, :] = jnp.zeros((6, 8, lanes), F32)


def convolve(lines, sums, taps_ref, breadth, lanes, flipped):
    sums = list(sums)
    height = len(sums)
    for b in range(7):
        start = LEFT - 3 + b
        for ref, at, i in lines:
            line = ref[at, start : start + breadth, lanes]
            for a in range(7):
                row = i - a
                if 0 <= row < height:
                    tap = 48 - (7 * a + b) if flipped else 7 * a + b
                    term = line * taps_ref[tap : tap + 1, lanes]
                    sums[row] = term if sums[row] is None else sums[row] + term
    return sums


def center_lines(ref):
    return [(ref, i, i + 3) for i in range(ref.shape[0])]


def edge_lines(ref, height):
    return [(ref, i, i) for i in range(3)] + [(ref, i + 3, i + height + 3) for i in range(3)]


def lane_block(k):
    return pl.ds(pl.multiple_of(k * 128, 128), 128)


def local_body(flipped, copied, *refs):
    own_ref, other_ref, taps_ref = refs[:3]
    sources = refs[3 : 3 + copied]
    pad_ref, sum_ref = refs[3 + copied : 5 + copied]
    targets = refs[5 + copied : 5 + 2 * copied]
    copies = []
    for k in range(copied):
        copies.append(pltpu.make_async_copy(sources[k], targets[k], refs[-1].at[k]))
        copies[k].start()
    height, breadth, width = other_ref.shape
    fill_center(pad_ref, own_ref, other_ref)

    def block(k, carry):
        lanes = lane_block(k)
        sums = convolve(
            center_lines(pad_ref), [None] * height, taps_ref, breadth, lanes, flipped
        )
        for i, row in enumerate(sums):
            sum_ref[i * breadth : (i + 1) * breadth, lanes] = row
        return carry

    lax.fori_loop(0, width // 128, block, 0)
    for copy in copies:
        copy.wait()


def local_convolution(own, other, taps, flipped=False, copied=()):
    height, breadth, width = other.shape
    outs = [((height, breadth + 16, width), F32), ((height * breadth, width), F32)]
    outs += [(x.shape, x.dtype) for x in copied]
    scratch = [pltpu.SemaphoreType.DMA((len(copied),))] if copied else []
    return call(
        functools.partial(local_body, flipped, len(copied)),
        outs,
        4.0,
        scratch,
        any_in=tuple(range(3, 3 + len(copied))),
    )(own, other, taps, *copied)


def conv_norm_body(
    near_ref, far_ref, taps_ref, sum_ref, edge_ref, normed_ref, send_ref, full_ref, inv_ref
):
    places, width = sum_ref.shape
    breadth = near_ref.shape[1] // 2
    height = places // breadth
    steps, half = width // 128, width // 2
    fill_edges(edge_ref, near_ref, far_ref)

    def block(k, carry):
        lanes = lane_block(k)
        sums = [sum_ref[i * breadth : (i + 1) * breadth, lanes] for i in range(height)]
        sums = convolve(edge_lines(edge_ref, height), sums, taps_ref, breadth, lanes, False)
        for i, row in enumerate(sums):
            full_ref[i * breadth : (i + 1) * breadth, lanes] = row
        return carry

    lax.fori_loop(0, steps, block, 0)

    def chunk(i, carry):
        rows = pl.ds(pl.multiple_of(i * 16, 16), 16)
        parts = [full_ref[rows, s * 128 : (s + 1) * 128] for s in range(steps)]
        mean = jnp.sum(functools.reduce(jnp.add, parts), axis=1, keepdims=True) * (1.0 / width)
        parts = [p - mean for p in parts]
        total = functools.reduce(jnp.add, [p * p for p in parts])
        var = jnp.sum(total, axis=1, keepdims=True) * (1.0 / width)
        inv = lax.rsqrt(var + 1e-06)
        inv_ref[rows, :] = jnp.broadcast_to(inv, (16, 128))
        for s, p in enumerate(parts):
            value = p * inv
            full_ref[rows, s * 128 : (s + 1) * 128] = value
            normed_ref[rows, s * 128 : (s + 1) * 128] = value.astype(BF16)
        return carry

    lax.fori_loop(0, places // 16, chunk, 0, unroll=4)
    c = lax.axis_index("col")
    send_ref[...] = normed_ref[:, pl.ds(pl.multiple_of((1 - c) * half, 128), half)]


def conv_norm(near, far, taps, sums):
    places, width = sums.shape
    outs = [
        ((6, near.shape[1] // 2 + 16, width), F32),
        ((places, width), BF16),
        ((places, width // 2), BF16),
        ((places, width), F32),
        ((places, 128), F32),
    ]
    return call(conv_norm_body, outs, 5.0)(near, far, taps, sums)


def lane_pack(rows, stack):
    _, wide = rows.shape
    tall = jnp.concatenate([rows[:, s : s + 128] for s in range(0, wide, 128)], axis=0)
    each = tall.shape[0] // stack
    return jnp.concatenate([tall[s * each : (s + 1) * each] for s in range(stack)], axis=1)


def lane_unpack(packed, n):
    _, wide = packed.shape
    tall = jnp.concatenate([packed[:, s : s + 128] for s in range(0, wide, 128)], axis=0)
    count = tall.shape[0] // n
    return jnp.concatenate([tall[s * n : (s + 1) * n] for s in range(count)], axis=1)


UNITS = 768


def unit_block(f):
    return pl.ds(pl.multiple_of(f * UNITS, UNITS), UNITS)


def forward_body(
    rows, normed_ref, w_in_ref, w_out_ref, slot_ref, image_ref, scale_ref,
    slope_ref, h_mine_ref, h_send_ref, s_mine_ref, s_send_ref, pre, hidden, branch, block,
):
    c = lax.axis_index("col")
    places, width = branch.shape
    total = w_in_ref.shape[1]
    regions = s_mine_ref.shape[0]
    half = width // 2
    per_chip = total // rows
    per_core = per_chip // 2
    slot = slot_ref[...]
    select = (slot == iota((places, regions), 1).astype(F32)).astype(BF16)
    branch[...] = jnp.zeros_like(branch)

    def units(f, carry):
        at = unit_block(f)
        pre[...] = dot(normed_ref[...], w_in_ref[:, at])

        def chunk(i, inner):
            line = pl.ds(pl.multiple_of(i * 16, 16), 16)
            for start in range(0, UNITS, 256):
                lanes = slice(start, start + 256)
                value = pre[line, lanes]
                cdf = 0.5 * (1.0 + lax.erf(value * (1.0 / math.sqrt(2.0))))
                density = jnp.exp(-0.5 * value * value) * (1.0 / math.sqrt(2.0 * math.pi))
                hidden[line, lanes] = (value * cdf).astype(BF16)
                out = pl.ds(pl.multiple_of(f * UNITS + start, 256), 256)
                slope_ref[line, out] = cdf + value * density
            return inner

        lax.fori_loop(0, places // 16, chunk, 0)
        branch[...] += dot(hidden[...], w_out_ref[at, :])
        by_region = dot(hidden[...], select, CONTRACT_ROWS)
        for t in range(UNITS // per_chip):
            q = f * (UNITS // per_chip) + t
            low = by_region[t * per_chip : t * per_chip + per_core]
            high = by_region[t * per_chip + per_core : (t + 1) * per_chip]
            h_mine_ref[q] = lane_pack(jnp.where(c == 0, low, high), half // 128)
            h_send_ref[q] = lane_pack(jnp.where(c == 0, high, low), half // 128).astype(BF16)
        return carry

    lax.fori_loop(0, total // UNITS, units, 0)
    block[...] = (image_ref[...].astype(F32) + scale_ref[...] * branch[...]).astype(BF16)
    for at, out in ((c, s_mine_ref), (1 - c, s_send_ref)):
        columns = block[:, pl.ds(pl.multiple_of(at * half, 128), half)]
        out[...] = dot(select, columns, CONTRACT_ROWS)


def mlp_forward(normed, w_in, w_out, slot, image, scale, regions, rows):
    places, width = normed.shape
    total, half = w_in.shape[1], width // 2
    packed = total // rows // 2 * regions // half
    outs = [
        ((places, total), F32),
        ((rows, packed, half), F32),
        ((rows, packed, half), BF16),
        ((regions, half), F32),
        ((regions, half), F32),
    ]
    scratch = [
        pltpu.VMEM((places, UNITS), F32),
        pltpu.VMEM((places, UNITS), BF16),
        pltpu.VMEM((places, width), F32),
        pltpu.VMEM((places, width), BF16),
    ]
    return call(functools.partial(forward_body, rows), outs, 9.0, scratch, room=12)(
        normed, w_in, w_out, slot, image, scale
    )


def backward_body(
    *refs,
):
    known_refs = refs[:4]
    slot_ref, scale_ref, w_out_ref, slope_ref = refs[4:8]
    g_in_ref, region_ref, dblock_ref, count_ref, g_out, known_all = refs[8:]
    r, c = lax.axis_index("row"), lax.axis_index("col")
    me = 2 * r + c
    places, units = slope_ref.shape
    regions = region_ref.shape[0]
    piece = known_refs[0].shape[0]
    for k in range(4):
        known_all[k * piece : (k + 1) * piece, :] = known_refs[k][...]
    total = 4 * piece
    owned = regions * 8 // total
    known = known_all[...]
    is_count = (iota((total, 128), 0) & 7) == owned
    count = dot(known[:, :regions], is_count.astype(BF16), CONTRACT_ROWS)
    count_ref[...] = count
    line = iota((regions, total), 1)
    source = (me ^ (line >> 3)) * owned + (line & 7)
    place = ((line & 7) < owned) & (source == iota((regions, total), 0))
    pooled = dot(place.astype(BF16), known)
    region_grad = (pooled / (4.0 * count[:, :1])).astype(BF16)
    g_region = (region_grad.astype(F32) * scale_ref[...]).astype(BF16)
    region_ref[...] = g_region
    select = (slot_ref[...] == iota((places, regions), 1).astype(F32)).astype(BF16)
    g_out[...] = dot(select, g_region).astype(BF16)
    dblock_ref[...] = dot(select, region_grad).astype(BF16)

    def block(f, carry):
        at = unit_block(f)
        dhidden = dot(g_out[...], w_out_ref[at, :], CONTRACT_LANES)
        g_in_ref[:, at] = (dhidden * slope_ref[:, at]).astype(BF16)
        return carry

    lax.fori_loop(0, units // UNITS, block, 0)


def mlp_backward(known, slot, scale, w_out, slope, regions):
    places, total = slope.shape
    width = w_out.shape[1]
    outs = [
        ((places, total), BF16),
        ((regions, width), BF16),
        ((places, width), BF16),
        ((regions, 128), F32),
    ]
    scratch = [
        pltpu.VMEM((places, width), BF16),
        pltpu.VMEM((4 * known[0].shape[0], width), BF16),
    ]
    return call(backward_body, outs, 4.0, scratch)(*known, slot, scale, w_out, slope)


def norm_backward_body(g_in_ref, w_in_ref, full_ref, inv_ref, dconv_ref, narrow_ref):
    places, width = dconv_ref.shape
    dconv_ref[...] = dot(g_in_ref[:, :UNITS], w_in_ref[:, :UNITS], CONTRACT_LANES)

    def block(f, carry):
        at = unit_block(f)
        dconv_ref[...] += dot(g_in_ref[:, at], w_in_ref[:, at], CONTRACT_LANES)
        return carry

    lax.fori_loop(1, w_in_ref.shape[1] // UNITS, block, 0)

    def chunk(i, carry):
        rows = pl.ds(pl.multiple_of(i * 16, 16), 16)
        lanes = [slice(s, s + 128) for s in range(0, width, 128)]
        grads = [dconv_ref[rows, at] for at in lanes]
        fulls = [full_ref[rows, at] for at in lanes]
        mean = jnp.sum(functools.reduce(jnp.add, grads), axis=1, keepdims=True) * (1.0 / width)
        total = functools.reduce(jnp.add, [g * n for g, n in zip(grads, fulls)])
        along = jnp.sum(total, axis=1, keepdims=True) * (1.0 / width)
        inv = inv_ref[rows, :]
        for at, g, n in zip(lanes, grads, fulls):
            value = inv * (g - mean - n * along)
            dconv_ref[rows, at] = value
            narrow_ref[rows, at] = value.astype(BF16)
        return carry

    lax.fori_loop(0, places // 16, chunk, 0, unroll=4)


def norm_backward(g_in, w_in, full, inv):
    places, width = full.shape
    outs = [((places, width), F32), ((places, width), BF16)]
    return call(norm_backward_body, outs, 4.0)(g_in, w_in, full, inv)


def split_high_low(value):
    high = value.astype(BF16)
    return high, (value - high.astype(F32)).astype(BF16)


CHUNKS = ((0, 256), (256, 128))


def weight_body(
    rows, own_ref, other_ref, normed_ref, normed_other_ref, h_mine_ref, h_got_ref, s_mine_ref,
    s_got_ref, *out_refs,
):
    r, c = lax.axis_index("row"), lax.axis_index("col")
    bits = rows.bit_length() - 1
    half = h_mine_ref.shape[2]
    total = own_ref.shape[1]
    count = rows // 2
    per_chip = total // rows
    packed = h_mine_ref.shape[1]
    per = s_mine_ref.shape[0] // rows
    columns = pl.ds(pl.multiple_of(c * half, 128), half)

    def store(q, value, first, split):
        for k, (lane, wide) in enumerate(CHUNKS):
            keep_ref, send_ref = out_refs[2 * k : 2 * k + 2]
            j = layout_place(q, r, c, orders(bits, k))
            part = value[:, lane : lane + wide]

            @pl.when(j < count)
            def _():
                keep_ref[j, first : first + value.shape[0], :] = part

            @pl.when(j >= count)
            def _():
                if split:
                    tail = jnp.concatenate(split_high_low(part), axis=0)
                else:
                    tail = part.astype(BF16)
                send_ref[j - count, first : first + tail.shape[0], :] = tail

    def block(f, carry):
        at = unit_block(f)
        grad = dot(own_ref[:, at], normed_ref[:, columns], CONTRACT_ROWS)
        grad += dot(other_ref[:, at], normed_other_ref[...], CONTRACT_ROWS)
        for t in range(UNITS // per_chip):
            q = f * (UNITS // per_chip) + t
            store(q, grad[t * per_chip : (t + 1) * per_chip], 0, False)
        return carry

    lax.fori_loop(0, total // UNITS, block, 0)

    def chip(q, carry):
        store(q, h_mine_ref[q] + h_got_ref[q].astype(F32), per_chip, False)
        at = pl.ds(pl.multiple_of(q * per, per), per)
        store(q, s_mine_ref[at, :] + s_got_ref[at, :], per_chip + packed, True)
        return carry

    lax.fori_loop(0, rows, chip, 0)


def weight_gradient(g_in, g_other, normed, normed_other, h_mine, h_got, s_mine, s_got):
    total = g_in.shape[1]
    rows, packed, _ = h_mine.shape
    per = s_mine.shape[0] // rows
    height = total // rows + packed + per
    outs = []
    for _, wide in CHUNKS:
        outs.append(((rows // 2, height, wide), F32))
        outs.append(((rows // 2, height + per, wide), BF16))
    return call(functools.partial(weight_body, rows), outs, 5.0, room=12)(
        g_in, g_other, normed, normed_other, h_mine, h_got, s_mine, s_got
    )


def merged(keep, got, per):
    body = keep.shape[0] - per
    plain = keep[:body] + got[:body].astype(F32)
    sums = keep[body:] + (got[body : body + per].astype(F32) + got[body + per :].astype(F32))
    return plain, sums


def round_body(per, old_ref, got_ref, keep_ref, send_ref):
    left = keep_ref.shape[0]
    body = keep_ref.shape[1] - per

    def near(i, carry):
        plain, sums = merged(old_ref[i], got_ref[i], per)
        keep_ref[i, :body, :] = plain
        keep_ref[i, body:, :] = sums
        return carry

    def far(i, carry):
        plain, sums = merged(old_ref[i + left], got_ref[i + left], per)
        send_ref[i, :body, :] = plain.astype(BF16)
        send_ref[i, body:, :] = jnp.concatenate(split_high_low(sums), axis=0)
        return carry

    lax.fori_loop(0, left, far, 0)
    lax.fori_loop(0, left, near, 0)


def halving_round(keep, got, per):
    count, height, wide = keep.shape
    left = count // 2
    outs = [((left, height, wide), F32), ((left, height + per, wide), BF16)]
    return call(functools.partial(round_body, per), outs, 0.5)(keep, got)


def finish_body(per, *refs):
    parts = refs[: 2 * len(CHUNKS)]
    region_ref, count_ref, out_ref, mine_ref, send_ref = refs[2 * len(CHUNKS) :]
    r, c = lax.axis_index("row"), lax.axis_index("col")
    done = [merged(parts[2 * k][0], parts[2 * k + 1][0], per) for k in range(len(CHUNKS))]
    plain = jnp.concatenate([d[0] for d in done], axis=1)
    sums = jnp.concatenate([d[1] for d in done], axis=1)
    per_core = out_ref.shape[0]
    first, second = plain[:per_core], plain[per_core : 2 * per_core]
    high, low = split_high_low(lane_unpack(plain[2 * per_core :], per_core))
    out_ref[...] = dot(high, region_ref[...]) + dot(low, region_ref[...])
    mine_ref[:per_core, :] = jnp.where(c == 0, first, second)
    send_ref[:per_core, :] = jnp.where(c == 0, second, first)
    start = pl.multiple_of(r * per, per)
    pooled = sums / (4.0 * count_ref[pl.ds(start, per), :1])
    mine_ref[per_core:, :] = pooled
    send_ref[per_core:, :] = pooled


def finish(parts, region, count, per, per_core):
    width = region.shape[1]
    part = ((per_core + per, width // 2), F32)
    outs = [((per_core, width), F32), part, part]
    return call(functools.partial(finish_body, per), outs, 1.0, far_out=(0,))(*parts, region, count)


def place_body(mine_ref, got_ref, grad_ref, pool_ref):
    c = lax.axis_index("col")
    per_core, width = grad_ref.shape
    half = width // 2
    owned = pool_ref.shape[0]
    for core in range(2):

        @pl.when(c == core)
        def _():
            left, right = (mine_ref, got_ref) if core == 0 else (got_ref, mine_ref)
            grad_ref[:, :half] = left[:per_core, :]
            grad_ref[:, half:] = right[:per_core, :]
            rows = slice(per_core + core * owned, per_core + (core + 1) * owned)
            pool_ref[:, :half] = left[rows, :]
            pool_ref[:, half:] = right[rows, :]


def place_outputs(mine, got, per_core, owned):
    width = 2 * mine.shape[1]
    outs = [((per_core, width), F32), ((owned, width), F32)]
    return call(place_body, outs, 0.5, far_out=(0, 1))(mine, got)


def kernel_gradient_body(pad_ref, edge_ref, dconv_ref, mine_ref, send_ref):
    c = lax.axis_index("col")
    height, wide, width = pad_ref.shape
    breadth = wide - 16

    def block(k, carry):
        lanes = lane_block(k)
        sums = {}
        grads = [dconv_ref[i * breadth : (i + 1) * breadth, lanes] for i in range(height)]
        for b in range(7):
            start = LEFT - 3 + b
            for ref, at, i in center_lines(pad_ref) + edge_lines(edge_ref, height):
                line = ref[at, start : start + breadth, lanes]
                for a in range(7):
                    row = i - a
                    if 0 <= row < height:
                        term = (line * grads[row]).reshape(breadth // 8, 8, 128).sum(axis=0)
                        sums[a, b] = sums[a, b] + term if (a, b) in sums else term
            for a in range(7):
                sums[a, b] = jnp.sum(sums[a, b], axis=0, keepdims=True)

        def put(ref, first, last):
            ref[24:, lanes] = jnp.zeros((8, 128), F32)
            for a in range(first, last):
                for b in range(7):
                    at = (a - first) * 7 + b
                    ref[at : at + 1, lanes] = sums[a, b]

        @pl.when(c == 0)
        def _():
            put(mine_ref, 0, 4)
            put(send_ref, 4, 7)

        @pl.when(c == 1)
        def _():
            put(mine_ref, 4, 7)
            put(send_ref, 0, 4)

        return carry

    lax.fori_loop(0, width // 128, block, 0)


def kernel_gradient(padded, edges, dconv):
    width = dconv.shape[1]
    outs = [((32, width), F32)] * 2
    return call(kernel_gradient_body, outs, 5.0)(padded, edges, dconv)


def back_body(near_ref, far_ref, taps_ref, sum_ref, dblock_ref, out_ref, edge_ref):
    height, breadth, width = out_ref.shape
    fill_edges(edge_ref, near_ref, far_ref)

    def block(k, carry):
        lanes = lane_block(k)
        sums = [sum_ref[i * breadth : (i + 1) * breadth, lanes] for i in range(height)]
        sums = convolve(edge_lines(edge_ref, height), sums, taps_ref, breadth, lanes, True)
        for i, row in enumerate(sums):
            rows = slice(i * breadth, (i + 1) * breadth)
            out_ref[i, :, lanes] = (dblock_ref[rows, lanes].astype(F32) + row).astype(BF16)
        return carry

    lax.fori_loop(0, width // 128, block, 0)


def back_convolution(near, far, taps, sums, dblock):
    places, width = sums.shape
    breadth = near.shape[1] // 2
    outs = [((places // breadth, breadth, width), BF16)]
    scratch = [pltpu.VMEM((6, breadth + 16, width), F32)]
    (out,) = call(back_body, outs, 3.0, scratch, far_out=(0,))(near, far, taps, sums, dblock)
    return out


def gather_known(known):
    bits = lax.axis_size("row").bit_length() - 1
    pieces = [known, swap_core(known)]
    for low in range(0, bits, 2):
        known = jnp.concatenate(pieces, axis=0)
        pieces = [known]
        for mask in (1 << low, 2 << low, 3 << low):
            pieces.append(exchange(known, (mask, mask)))
    return pieces


def compute(image, dw_kernel, w_in, w_out, layer_scale, region_ids, region_slot, pool_grad):
    height, breadth, width = image.shape
    total = w_in.shape[1]
    rows = lax.axis_size("row")
    bits = rows.bit_length() - 1
    c = lax.axis_index("col")
    regions = region_slot.shape[0]
    owned = pool_grad.shape[0]
    known, slot, own, taps, scale = prepare(
        region_ids, region_slot, pool_grad, image, dw_kernel, layer_scale
    )
    other, near, far = halo(image, own)
    known = gather_known(known)

    padded, sums, w_in, w_out = local_convolution(own, other, taps, copied=(w_in, w_out))
    edges, normed, normed_send, full, inv = conv_norm(near, far, taps, sums)
    normed_other = swap_core(normed_send)
    slope, h_mine, h_send, s_mine, s_send = mlp_forward(
        normed, w_in, w_out, slot, own.reshape(-1, width), scale, regions, rows
    )
    h_got = swap_core(h_send)
    s_got = swap_core(s_send)
    g_in, g_region, dblock, count = mlp_backward(known, slot, scale, w_out, slope, regions)
    g_other = swap_core(g_in)
    dconv, narrow = norm_backward(g_in, w_in, full, inv)
    halves = weight_gradient(g_in, g_other, normed, normed_other, h_mine, h_got, s_mine, s_got)
    per = regions // rows
    parts = []
    for k in range(len(CHUNKS)):
        keep, send = halves[2 * k : 2 * k + 2]
        order = orders(bits, k)
        for step in range(bits):
            got = exchange(send, (1 << order[0][step], 1 << order[1][step]))
            if step < bits - 1:
                keep, send = halving_round(keep, got, per)
        parts += [keep, got]

    part, part_send = kernel_gradient(padded, edges, dconv)
    part = part + swap_core(part_send)
    order = orders(bits, 1)
    for step in range(bits):
        part = part + exchange(part, (1 << order[0][step], 1 << order[1][step]))
    part_other = swap_core(part)
    grad_kernel = jnp.concatenate(
        [
            jnp.where(c == 0, part, part_other)[:28],
            jnp.where(c == 0, part_other, part)[:21],
        ],
        axis=0,
    )

    narrow = narrow.reshape(height, breadth, width)
    d_other, d_near, d_far = halo(narrow, narrow)
    _, back = local_convolution(dconv, d_other, taps, flipped=True)
    grad_image = back_convolution(d_near, d_far, taps, back, dblock)

    per_core = total // rows // 2
    grad_w_out, mine, send = finish(parts, g_region, count, per, per_core)
    got = swap_core(send)
    grad_w_in, region_pool = place_outputs(mine, got, per_core, owned)
    return (region_pool, grad_image, grad_w_in.T, grad_w_out, grad_kernel)


def solution(mesh):
    placed = (
        P(("slides", "row"), "col", None),
        P(),
        P(),
        P(),
        P(),
        P(("slides", "row"), "col"),
        P("slides"),
        P(("slides", "row", "col"), None),
    )
    return jax.shard_map(
        compute,
        mesh=mesh,
        in_specs=placed,
        out_specs=(
            P(("slides", "row", "col"), None),
            P(("slides", "row"), "col", None),
            P("slides", ("row", "col")),
            P(("slides", "row", "col"), None),
            P("slides", None),
        ),
        check_vma=False,
    )
```

time: 570 us -> 142 us (0.25)
  waiting for transfers between devices: 385 us -> 38.5 us
  blocking collectives: 84.6 us -> 0 us
  Pallas kernels: 0 us -> 46.6 us
  starting transfers between devices: 16.7 us -> 49.5 us
  matrix products: 27.3 us -> 0 us
  other arithmetic: 25.6 us -> 3.27 us
  between operations: 15.2 us -> 0.86 us
  local copies, waits for them, and re-layouts: 14.9 us -> 3.34 us
    reduce_scatter x2 -> x0, waiting for transfers between devices: 277 us -> none  [the longest x1 142 us: shards(): lax.psum_scatter(full_in, ('row', 'col'), scatter_dimension=1, tiled=True)]
    unnamed x4 -> x0, waiting for transfers between devices: 95.4 us -> none
    pallas_call x0 -> x20, Pallas kernels: none -> 46.6 us  [run(): pl.pallas_call(body, in_specs=specs, out_specs=[VMEM] * len(outs), out_sh...]
    unnamed x1 -> x0, blocking collectives: 44.4 us -> none
    all_gather x1 -> x0, blocking collectives: 40.2 us -> none  [shards(): every_grad = lax.all_gather(region_grad, ('row', 'col'), axis=0, tiled=True)]
    ppermute x8 -> x32, starting transfers between devices: 16.6 us -> 49.5 us  [the longest x30 48.1 us: exchange(): return lax.ppermute(value, AXES, pairs)]
    dot_general x9 -> x0, matrix products: 27.3 us -> none  [the longest x1 9 us: shards(): pre = jnp.dot(normed, w_in, preferred_element_type=jnp.float32)]
    ppermute x8 -> x32, waiting for transfers between devices: 12.3 us -> 38.5 us  [the longest x30 38.5 us: exchange(): return lax.ppermute(value, AXES, pairs)]
  transfers between devices with their start and end apart: 11 -> 32, of which waited for: 5 -> 12; matrix products, arithmetic and copies ran while one was open for 4% -> 2% of each run, Pallas kernels for 0% -> 28%
where the time goes in v1:
time: 142 us
  starting transfers between devices  49.5 us (35%)
  Pallas kernels  46.6 us (33%)
  waiting for transfers between devices  38.5 us (27%)
  local copies, waits for them, and re-layouts  3.34 us (2%)
  other arithmetic  3.27 us (2%)
    ppermute x30, starting transfers between devices, exchange(): return lax.ppermute(value, AXES, pairs)  48.1 us
    pallas_call x20, Pallas kernels, run(): pl.pallas_call(body, in_specs=specs, out_specs=[VMEM] * len(outs), out_sh...  46.6 us
    ppermute x30, waiting for transfers between devices, exchange(): return lax.ppermute(value, AXES, pairs)  38.5 us
    unnamed x15, local copies, waits for them, and re-layouts  3.33 us
  transfers between devices with their start and end apart: 32, of which 12 were waited for; matrix products, arithmetic and copies ran while one was open for 2% of the time, Pallas kernels for 28%

profile of v1, /device:TPU:0, one launch (start us, length us, event | category | flops | bytes accessed | tf_op | source)
XLA Modules:
  0.0 142.1 jit_solution(14724257181138014804)
XLA Ops:
  0.6 0.6 collective-permute-start.7
  1.2 1.8 %shard_map.119 = (bf16[8,768]{1,0:T(8,128)(2,1)S(1)}, f32[256,1]{1,0:T(8,128)S(1)}, bf16[4,64,768]{2,1,0:T(8,128)(2,1)S(1)}, f32[49,768]{1,0:T(8,128)S(1)}, f32[1,768]{1,0:T(1,128)S(1)}) custom-call(s32[2,32]{1,0:T(2,128)} %ids_ref.1, s32[1,128]{1,0:T(1,128)} %bitcast.7, bf16[4,768]{1,0:T(4,128)(2,1)} %grad_ref.1, bf16[4,64,768]{2,1,0:T(8,128)(2,1)} %image_ref.1, ...), custom_call_target="tpu_custom_call" | custom-call | bytes 4500000 | tf_op jit(solution)/shard_map/pallas_call | solution.py:44
  3.1 0.7 collective-permute-start.8
  3.8 4.0 %collective-permute-start = (bf16[8,768]{1,0:T(8,128)(2,1)S(1)}, bf16[8,768]{1,0:T(8,128)(2,1)S(1)}, u32[]{:S(2)}, u32[]{:S(2)}) collective-permute-start(bf16[8,768]{1,0:T(8,128)(2,1)S(1)} %get-tuple-element.54), channel_id=1, source_target_pairs={{0,1},{1,0},{2,3},{3,2},{4,5},{5,4},{6,7},{7,6},{8,9},{9,8},{10,11... | collective-permute-start | bytes 36872 | tf_op jit(solution)/shard_map/ppermute | solution.py:65
  7.7 13.1 %collective-permute-start.9 = (bf16[3,128,768]{2,1,0:T(8,128)(2,1)S(1)}, bf16[3,128,768]{2,1,0:T(8,128)(2,1)S(1)}, u32[]{:S(2)}, u32[]{:S(2)}) collective-permute-start(bf16[3,128,768]{2,1,0:T(8,128)(2,1)S(1)} %collective-permute-done.8.near_ref), channel_id=1, source_target_pairs={{0,1},{1,0},{2,3},{3,2},{4,5},{5,4},{6,7},{7,6},{8,9},{9,8},{10,11... | collective-permute-start | bytes 1769480 | tf_op jit(solution)/shard_map/ppermute | solution.py:65
  20.8 3.2 %collective-permute-start.1 = (bf16[16,768]{1,0:T(8,128)(2,1)S(1)}, bf16[16,768]{1,0:T(8,128)(2,1)S(1)}, u32[]{:S(2)}, u32[]{:S(2)}) collective-permute-start(bf16[16,768]{1,0:T(8,128)(2,1)S(1)} %get-tuple-element.103), channel_id=1, source_target_pairs={{0,2},{1,3},{2,0},{3,1},{4,6},{5,7},{6,4},{7,5},{8,10},{9,11},{10,... | collective-permute-start | bytes 73736 | tf_op jit(solution)/shard_map/ppermute | solution.py:65
  24.0 0.2 collective-permute-start.2
  24.3 1.3 collective-permute-start.3
  25.6 0.3 collective-permute-done.1
  25.8 2.3 %collective-permute-done.2 = bf16[16,768]{1,0:T(8,128)(2,1)S(1)} collective-permute-done((bf16[16,768]{1,0:T(8,128)(2,1)S(1)}, bf16[16,768]{1,0:T(8,128)(2,1)S(1)}, u32[]{:S(2)}, u32[]{:S(2)}) %collective-permute-start.2) | collective-permute-done | bytes 24608 | tf_op jit(solution)/shard_map/ppermute | solution.py:65
  28.1 0.9 collective-permute-done.3
  29.0 1.6 %collective-permute-start.4 = (bf16[64,768]{1,0:T(8,128)(2,1)S(1)}, bf16[64,768]{1,0:T(8,128)(2,1)S(1)}, u32[]{:S(2)}, u32[]{:S(2)}) collective-permute-start(bf16[64,768]{1,0:T(8,128)(2,1)S(1)} %constant_dynamic-update-slice_fusion.2.refs_0_), channel_id=1, source_target_pairs={{0,8},{1,9},{2,10},{3,11},{4,12},{5,13},{6,14},{7,15},{8,0},{9,1},... | collective-permute-start | bytes 294920 | tf_op jit(solution)/shard_map/ppermute | solution.py:65
  30.6 2.6 %collective-permute-start.5 = (bf16[64,768]{1,0:T(8,128)(2,1)S(1)}, bf16[64,768]{1,0:T(8,128)(2,1)S(1)}, u32[]{:S(2)}, u32[]{:S(2)}) collective-permute-start(bf16[64,768]{1,0:T(8,128)(2,1)S(1)} %constant_dynamic-update-slice_fusion.2.refs_0_), channel_id=1, source_target_pairs={{0,16},{1,17},{2,18},{3,19},{4,20},{5,21},{6,22},{7,23},{8,24},{9,... | collective-permute-start | bytes 294920 | tf_op jit(solution)/shard_map/ppermute | solution.py:65
  33.2 0.2 collective-permute-start.6
  33.4 3.8 %shard_map.120 = (f32[4,80,768]{2,1,0:T(8,128)S(1)}, f32[256,768]{1,0:T(8,128)S(1)}, bf16[768,3072]{1,0:T(8,128)(2,1)S(1)}, bf16[3072,768]{1,0:T(8,128)(2,1)S(1)}) custom-call(bf16[4,64,768]{2,1,0:T(8,128)(2,1)S(1)} %get-tuple-element.57.refs_0_.own_ref, bf16[4,64,768]{2,1,0:T(8,128)(2,1)S(1)} %collective-permute-done.7.refs_1_.other_ref, ...), custom_call_target="tpu_custom_call" | custom-call | bytes 12000000 | tf_op jit(solution)/shard_map/pallas_call | solution.py:44
  37.2 5.5 %shard_map.122 = (f32[6,80,768]{2,1,0:T(8,128)S(1)}, bf16[256,768]{1,0:T(8,128)(2,1)S(1)}, bf16[256,384]{1,0:T(8,128)(2,1)S(1)}, f32[256,768]{1,0:T(8,128)S(1)}, f32[256,128]{1,0:T(8,128)S(1)}) custom-call(bf16[3,128,768]{2,1,0:T(8,128)(2,1)S(1)} %collective-permute-done.8.near_ref, bf16[3,128,768]{2,1,0:T(8,128)(2,1)S(1)} %collective-permute-done.9.far_ref, ...), custom_call_target="tpu_custom_call" | custom-call | bytes 15000000 | tf_op jit(solution)/shard_map/pallas_call | solution.py:44
  42.7 7.4 %shard_map.123 = (f32[256,3072]{1,0:T(8,128)S(1)}, f32[16,32,384]{2,1,0:T(8,128)S(1)}, bf16[16,32,384]{2,1,0:T(8,128)(2,1)S(1)}, f32[128,384]{1,0:T(8,128)S(1)}, f32[128,384]{1,0:T(8,128)S(1)}) custom-call(bf16[256,768]{1,0:T(8,128)(2,1)S(1)} %get-tuple-element.61.normed_ref, bf16[768,3072]{1,0:T(8,128)(2,1)S(1)} %get-tuple-element.62.w_in_ref, ...), custom_call_target="tpu_custom_call" | custom-call | bytes 27000000 | tf_op jit(solution)/shard_map/pallas_call | solution.py:44
  50.2 2.7 %shard_map.124 = (bf16[256,3072]{1,0:T(8,128)(2,1)S(1)}, bf16[128,768]{1,0:T(8,128)(2,1)S(1)}, bf16[256,768]{1,0:T(8,128)(2,1)S(1)}, f32[128,128]{1,0:T(8,128)S(1)}) custom-call(bf16[64,768]{1,0:T(8,128)(2,1)S(1)} %constant_dynamic-update-slice_fusion.2.refs_0_, bf16[64,768]{1,0:T(8,128)(2,1)S(1)} %collective-permute-done.4.refs_1_, ...), custom_call_target="tpu_custom_call" | custom-call | bytes 12000000 | tf_op jit(solution)/shard_map/pallas_call | solution.py:44
  52.9 0.6 copy-done.4
  53.6 0.5 collective-permute-start.12
  54.1 0.5 collective-permute-start.11
  54.6 3.2 %collective-permute-done.13.s_got_ref = f32[128,384]{1,0:T(8,128)S(1)} collective-permute-done((f32[128,384]{1,0:T(8,128)S(1)}, f32[128,384]{1,0:T(8,128)S(1)}, u32[]{:S(2)}, u32[]{:S(2)}) %collective-permute-start.13) | collective-permute-done | bytes 196640 | tf_op jit(solution)/shard_map/ppermute | solution.py:65
  57.8 0.3 collective-permute-done.11.normed_other_ref
  58.1 3.9 %shard_map.125 = (f32[8,232,256]{2,1,0:T(8,128)S(1)}, bf16[8,240,256]{2,1,0:T(8,128)(2,1)S(1)}, f32[8,232,128]{2,1,0:T(8,128)S(1)}, bf16[8,240,128]{2,1,0:T(8,128)(2,1)S(1)}) custom-call(bf16[256,3072]{1,0:T(8,128)(2,1)S(1)} %get-tuple-element.64.own_ref.g_in_ref, bf16[256,3072]{1,0:T(8,128)(2,1)S(1)} %collective-permute-done.10.other_ref, ...), custom_call_target="tpu_custom_call" | custom-call | bytes 15000000 | tf_op jit(solution)/shard_map/pallas_call | solution.py:44
  62.0 1.6 %collective-permute-start.14 = (bf16[8,240,256]{2,1,0:T(8,128)(2,1)S(1)}, bf16[8,240,256]{2,1,0:T(8,128)(2,1)S(1)}, u32[]{:S(2)}, u32[]{:S(2)}) collective-permute-start(bf16[8,240,256]{2,1,0:T(8,128)(2,1)S(1)} %get-tuple-element.71), channel_id=1, source_target_pairs={{0,2},{1,5},{2,0},{3,7},{4,6},{5,1},{6,4},{7,3},{8,10},{9,13},{10,... | collective-permute-start | bytes 2949128 | tf_op jit(solution)/shard_map/ppermute | solution.py:65
  63.5 3.6 %shard_map.134 = (f32[256,768]{1,0:T(8,128)S(1)}, bf16[256,768]{1,0:T(8,128)(2,1)S(1)}) custom-call(bf16[256,3072]{1,0:T(8,128)(2,1)S(1)} %get-tuple-element.64.own_ref.g_in_ref, bf16[768,3072]{1,0:T(8,128)(2,1)S(1)} %get-tuple-element.62.w_in_ref, f32[256,768]{1,0:T(8,128)S(1)} %get-tuple-element.91.full_ref, f32[256,128]{1,0:T(8,128)S(1)} %get-tuple-element.92.inv_ref), custom_call_target="tpu_custom_call" | custom-call | bytes 12000000 | tf_op jit(solution)/shard_map/pallas_call | solution.py:44
  67.1 0.3 collective-permute-start.23
  67.4 0.8 collective-permute-start.18
  68.1 8.0 %collective-permute-done.14.got_ref = bf16[8,240,256]{2,1,0:T(8,128)(2,1)S(1)} collective-permute-done((bf16[8,240,256]{2,1,0:T(8,128)(2,1)S(1)}, bf16[8,240,256]{2,1,0:T(8,128)(2,1)S(1)}, u32[]{:S(2)}, u32[]{:S(2)}) %collective-permute-start.14) | collective-permute-done | bytes 983072 | tf_op jit(solution)/shard_map/ppermute | solution.py:65
  76.1 0.2 shard_map.126
  76.3 1.8 %collective-permute-start.15 = (bf16[4,240,256]{2,1,0:T(8,128)(2,1)S(1)}, bf16[4,240,256]{2,1,0:T(8,128)(2,1)S(1)}, u32[]{:S(2)}, u32[]{:S(2)}) collective-permute-start(bf16[4,240,256]{2,1,0:T(8,128)(2,1)S(1)} %get-tuple-element.73), channel_id=1, source_target_pairs={{0,4},{1,3},{2,6},{3,1},{4,0},{5,7},{6,2},{7,5},{8,12},{9,11},{10,... | collective-permute-start | bytes 1474568 | tf_op jit(solution)/shard_map/ppermute | solution.py:65
  78.2 0.7 collective-permute-start.24
  78.9 5.6 %shard_map.138 = (f32[32,768]{1,0:T(8,128)S(1)}, f32[32,768]{1,0:T(8,128)S(1)}) custom-call(f32[4,80,768]{2,1,0:T(8,128)S(1)} %get-tuple-element.99.pad_ref, f32[6,80,768]{2,1,0:T(8,128)S(1)} %get-tuple-element.100.edge_ref, f32[256,768]{1,0:T(8,128)S(1)} %get-tuple-element.94.refs_0_.dconv_ref), custom_call_target="tpu_custom_call" | custom-call | bytes 15000000 | tf_op jit(solution)/shard_map/pallas_call | solution.py:44
  84.6 1.6 %collective-permute-start.26 = (f32[32,768]{1,0:T(8,128)S(1)}, f32[32,768]{1,0:T(8,128)S(1)}, u32[]{:S(2)}, u32[]{:S(2)}) collective-permute-start(f32[32,768]{1,0:T(8,128)S(1)} %get-tuple-element.102), channel_id=1, source_target_pairs={{0,1},{1,0},{2,3},{3,2},{4,5},{5,4},{6,7},{7,6},{8,9},{9,8},{10,11... | collective-permute-start | bytes 294920 | tf_op jit(solution)/shard_map/ppermute | solution.py:65
  86.1 0.9 collective-permute-done.26
  87.1 1.7 %collective-permute-start.27 = (f32[32,768]{1,0:T(8,128)S(1)}, f32[32,768]{1,0:T(8,128)S(1)}, u32[]{:S(2)}, u32[]{:S(2)}) collective-permute-start(f32[32,768]{1,0:T(8,128)S(1)} %add.15), channel_id=1, source_target_pairs={{0,8},{1,9},{2,10},{3,11},{4,12},{5,13},{6,14},{7,15},{8,0},{9,1},... | collective-permute-start | bytes 294920 | tf_op jit(solution)/shard_map/ppermute | solution.py:65
  88.8 3.4 %collective-permute-done.27 = f32[32,768]{1,0:T(8,128)S(1)} collective-permute-done((f32[32,768]{1,0:T(8,128)S(1)}, f32[32,768]{1,0:T(8,128)S(1)}, u32[]{:S(2)}, u32[]{:S(2)}) %collective-permute-start.27) | collective-permute-done | bytes 98336 | tf_op jit(solution)/shard_map/ppermute | solution.py:65
  92.2 2.5 %collective-permute-start.28 = (f32[32,768]{1,0:T(8,128)S(1)}, f32[32,768]{1,0:T(8,128)S(1)}, u32[]{:S(2)}, u32[]{:S(2)}) collective-permute-start(f32[32,768]{1,0:T(8,128)S(1)} %add.16), channel_id=1, source_target_pairs={{0,16},{1,17},{2,18},{3,19},{4,20},{5,21},{6,22},{7,23},{8,24},{9,... | collective-permute-start | bytes 294920 | tf_op jit(solution)/shard_map/ppermute | solution.py:65
  94.7 0.2 shard_map.129
  94.9 0.5 collective-permute-start.19
  95.4 10.1 %collective-permute-done.28 = f32[32,768]{1,0:T(8,128)S(1)} collective-permute-done((f32[32,768]{1,0:T(8,128)S(1)}, f32[32,768]{1,0:T(8,128)S(1)}, u32[]{:S(2)}, u32[]{:S(2)}) %collective-permute-start.28) | collective-permute-done | bytes 98336 | tf_op jit(solution)/shard_map/ppermute | solution.py:65
  105.6 1.9 %collective-permute-start.29 = (f32[32,768]{1,0:T(8,128)S(1)}, f32[32,768]{1,0:T(8,128)S(1)}, u32[]{:S(2)}, u32[]{:S(2)}) collective-permute-start(f32[32,768]{1,0:T(8,128)S(1)} %add.17), channel_id=1, source_target_pairs={{0,2},{1,5},{2,0},{3,7},{4,6},{5,1},{6,4},{7,3},{8,10},{9,13},{10,... | collective-permute-start | bytes 294920 | tf_op jit(solution)/shard_map/ppermute | solution.py:65
  107.5 0.8 shard_map.127
  108.3 2.0 %collective-permute-done.29 = f32[32,768]{1,0:T(8,128)S(1)} collective-permute-done((f32[32,768]{1,0:T(8,128)S(1)}, f32[32,768]{1,0:T(8,128)S(1)}, u32[]{:S(2)}, u32[]{:S(2)}) %collective-permute-start.29) | collective-permute-done | bytes 98336 | tf_op jit(solution)/shard_map/ppermute | solution.py:65
  110.3 2.1 %collective-permute-start.30 = (f32[32,768]{1,0:T(8,128)S(1)}, f32[32,768]{1,0:T(8,128)S(1)}, u32[]{:S(2)}, u32[]{:S(2)}) collective-permute-start(f32[32,768]{1,0:T(8,128)S(1)} %add.18), channel_id=1, source_target_pairs={{0,4},{1,3},{2,6},{3,1},{4,0},{5,7},{6,2},{7,5},{8,12},{9,11},{10,... | collective-permute-start | bytes 294920 | tf_op jit(solution)/shard_map/ppermute | solution.py:65
  112.4 0.7 shard_map.130
  113.2 1.7 %collective-permute-start.20 = (bf16[2,240,128]{2,1,0:T(8,128)(2,1)}, bf16[2,240,128]{2,1,0:T(8,128)(2,1)S(1)}, u32[]{:S(2)}, u32[]{:S(2)}) collective-permute-start(bf16[2,240,128]{2,1,0:T(8,128)(2,1)} %get-tuple-element.83), channel_id=1, source_target_pairs={{0,2},{1,5},{2,0},{3,7},{4,6},{5,1},{6,4},{7,3},{8,10},{9,13},{10,... | collective-permute-start | bytes 368648 | tf_op jit(solution)/shard_map/ppermute | solution.py:65
  114.9 0.8 collective-permute-done.30
  115.7 0.6 add.19
  116.3 0.5 collective-permute-start.25
  116.8 4.1 %shard_map.136 = (f32[4,80,768]{2,1,0:T(8,128)}, f32[256,768]{1,0:T(8,128)S(1)}) custom-call(f32[256,768]{1,0:T(8,128)S(1)} %get-tuple-element.94.refs_0_.dconv_ref, bf16[4,64,768]{2,1,0:T(8,128)(2,1)S(1)} %collective-permute-done.23.other_ref.refs_1_, f32[49,768]{1,0:T(8,128)S(1)} %get-tuple-element.58.refs_2_.taps_ref), custom_call_target="tpu_custom_call" | custom-call | bytes 12000000 | tf_op jit(solution)/shard_map/pallas_call | solution.py:44
  120.9 0.9 copy-done.1
  121.9 2.4 %collective-permute-start.21 = (bf16[1,240,128]{2,1,0:T(8,128)(2,1)S(1)}, bf16[1,240,128]{2,1,0:T(8,128)(2,1)S(1)}, u32[]{:S(2)}, u32[]{:S(2)}) collective-permute-start(bf16[1,240,128]{2,1,0:T(8,128)(2,1)S(1)} %get-tuple-element.85), channel_id=1, source_target_pairs={{0,4},{1,3},{2,6},{3,1},{4,0},{5,7},{6,2},{7,5},{8,12},{9,11},{10,... | collective-permute-start | bytes 184328 | tf_op jit(solution)/shard_map/ppermute | solution.py:65
  124.3 1.0 shard_map.128
  125.3 1.0 collective-permute-start.17
  126.3 1.0 slice_select_fusion
  127.2 6.3 %collective-permute-done.17.refs_1_ = bf16[1,240,256]{2,1,0:T(8,128)(2,1)S(1)} collective-permute-done((bf16[1,240,256]{2,1,0:T(8,128)(2,1)S(1)}, bf16[1,240,256]{2,1,0:T(8,128)(2,1)S(1)}, u32[]{:S(2)}, u32[]{:S(2)}) %collective-permute-start.17) | collective-permute-done | bytes 122912 | tf_op jit(solution)/shard_map/ppermute | solution.py:65
  133.5 0.9 copy-done.3
  134.4 0.8 copy-done.5
  135.3 0.9 shard_map.132
  136.2 0.9 slice_select_fusion.1
  137.1 0.7 pad_maximum_fusion
  137.8 3.5 %shard_map.137 = bf16[4,64,768]{2,1,0:T(8,128)(2,1)} custom-call(bf16[3,128,768]{2,1,0:T(8,128)(2,1)S(1)} %collective-permute-done.24.near_ref, bf16[3,128,768]{2,1,0:T(8,128)(2,1)S(1)} %collective-permute-done.25.far_ref, f32[49,768]{1,0:T(8,128)S(1)} %get-tuple-element.58.refs_2_.taps_ref, f32[256,768]{1,0:T(8,128)S(1)} %get-tuple-element.95.sum_ref, ...), custom_call_target="tpu_custom_call" | custom-call | bytes 9000000 | tf_op jit(solution)/shard_map/pallas_call | solution.py:44
  141.3 0.7 shard_map.133
  (45 shorter events, 0.3 us)
Async XLA Ops:
  0.6 2.4 %collective-permute-start.7 = (bf16[4,64,768]{2,1,0:T(8,128)(2,1)}, bf16[4,64,768]{2,1,0:T(8,128)(2,1)S(1)}, u32[]{:S(2)}, u32[]{:S(2)}) collective-permute-start(bf16[4,64,768]{2,1,0:T(8,128)(2,1)} %image_ref.1), channel_id=1, source_target_pairs={{0,1},{1,0},{2,3},{3,2},{4,5},{5,4},{6,7},{7,6},{8,9},{9,8},{10,11... | collective-permute-start | bytes 1179656 | tf_op jit(solution)/shard_map/ppermute | solution.py:65
  3.1 4.7 %collective-permute-start.8 = (bf16[3,128,768]{2,1,0:T(8,128)(2,1)S(1)}, bf16[3,128,768]{2,1,0:T(8,128)(2,1)S(1)}, u32[]{:S(2)}, u32[]{:S(2)}) collective-permute-start(bf16[3,128,768]{2,1,0:T(8,128)(2,1)S(1)} %shard_map.121), channel_id=1, source_target_pairs={{1,2},{2,1},{3,4},{4,3},{5,6},{6,5},{7,8},{8,7},{9,10},{10,9},{11,... | collective-permute-start | bytes 1769480 | tf_op jit(solution)/shard_map/ppermute | solution.py:78
  3.8 17.0 %collective-permute-start = (bf16[8,768]{1,0:T(8,128)(2,1)S(1)}, bf16[8,768]{1,0:T(8,128)(2,1)S(1)}, u32[]{:S(2)}, u32[]{:S(2)}) collective-permute-start(bf16[8,768]{1,0:T(8,128)(2,1)S(1)} %get-tuple-element.54), channel_id=1, source_target_pairs={{0,1},{1,0},{2,3},{3,2},{4,5},{5,4},{6,7},{7,6},{8,9},{9,8},{10,11... | collective-permute-start | bytes 36872 | tf_op jit(solution)/shard_map/ppermute | solution.py:65
  7.7 29.4 %collective-permute-start.9 = (bf16[3,128,768]{2,1,0:T(8,128)(2,1)S(1)}, bf16[3,128,768]{2,1,0:T(8,128)(2,1)S(1)}, u32[]{:S(2)}, u32[]{:S(2)}) collective-permute-start(bf16[3,128,768]{2,1,0:T(8,128)(2,1)S(1)} %collective-permute-done.8.near_ref), channel_id=1, source_target_pairs={{0,1},{1,0},{2,3},{3,2},{4,5},{5,4},{6,7},{7,6},{8,9},{9,8},{10,11... | collective-permute-start | bytes 1769480 | tf_op jit(solution)/shard_map/ppermute | solution.py:65
  20.8 5.0 %collective-permute-start.1 = (bf16[16,768]{1,0:T(8,128)(2,1)S(1)}, bf16[16,768]{1,0:T(8,128)(2,1)S(1)}, u32[]{:S(2)}, u32[]{:S(2)}) collective-permute-start(bf16[16,768]{1,0:T(8,128)(2,1)S(1)} %get-tuple-element.103), channel_id=1, source_target_pairs={{0,2},{1,3},{2,0},{3,1},{4,6},{5,7},{6,4},{7,5},{8,10},{9,11},{10,... | collective-permute-start | bytes 73736 | tf_op jit(solution)/shard_map/ppermute | solution.py:65
  24.0 4.1 %collective-permute-start.2 = (bf16[16,768]{1,0:T(8,128)(2,1)S(1)}, bf16[16,768]{1,0:T(8,128)(2,1)S(1)}, u32[]{:S(2)}, u32[]{:S(2)}) collective-permute-start(bf16[16,768]{1,0:T(8,128)(2,1)S(1)} %get-tuple-element.103), channel_id=1, source_target_pairs={{0,4},{1,5},{2,6},{3,7},{4,0},{5,1},{6,2},{7,3},{8,12},{9,13},{10,... | collective-permute-start | bytes 73736 | tf_op jit(solution)/shard_map/ppermute | solution.py:65
  24.3 4.7 %collective-permute-start.3 = (bf16[16,768]{1,0:T(8,128)(2,1)S(1)}, bf16[16,768]{1,0:T(8,128)(2,1)S(1)}, u32[]{:S(2)}, u32[]{:S(2)}) collective-permute-start(bf16[16,768]{1,0:T(8,128)(2,1)S(1)} %get-tuple-element.103), channel_id=1, source_target_pairs={{0,6},{1,7},{2,4},{3,5},{4,2},{5,3},{6,0},{7,1},{8,14},{9,15},{10,... | collective-permute-start | bytes 73736 | tf_op jit(solution)/shard_map/ppermute | solution.py:65
  29.0 21.2 %collective-permute-start.4 = (bf16[64,768]{1,0:T(8,128)(2,1)S(1)}, bf16[64,768]{1,0:T(8,128)(2,1)S(1)}, u32[]{:S(2)}, u32[]{:S(2)}) collective-permute-start(bf16[64,768]{1,0:T(8,128)(2,1)S(1)} %constant_dynamic-update-slice_fusion.2.refs_0_), channel_id=1, source_target_pairs={{0,8},{1,9},{2,10},{3,11},{4,12},{5,13},{6,14},{7,15},{8,0},{9,1},... | collective-permute-start | bytes 294920 | tf_op jit(solution)/shard_map/ppermute | solution.py:65
  30.6 19.6 %collective-permute-start.5 = (bf16[64,768]{1,0:T(8,128)(2,1)S(1)}, bf16[64,768]{1,0:T(8,128)(2,1)S(1)}, u32[]{:S(2)}, u32[]{:S(2)}) collective-permute-start(bf16[64,768]{1,0:T(8,128)(2,1)S(1)} %constant_dynamic-update-slice_fusion.2.refs_0_), channel_id=1, source_target_pairs={{0,16},{1,17},{2,18},{3,19},{4,20},{5,21},{6,22},{7,23},{8,24},{9,... | collective-permute-start | bytes 294920 | tf_op jit(solution)/shard_map/ppermute | solution.py:65
  33.2 17.0 %collective-permute-start.6 = (bf16[64,768]{1,0:T(8,128)(2,1)S(1)}, bf16[64,768]{1,0:T(8,128)(2,1)S(1)}, u32[]{:S(2)}, u32[]{:S(2)}) collective-permute-start(bf16[64,768]{1,0:T(8,128)(2,1)S(1)} %constant_dynamic-update-slice_fusion.2.refs_0_), channel_id=1, source_target_pairs={{0,24},{1,25},{2,26},{3,27},{4,28},{5,29},{6,30},{7,31},{8,16},{9,... | collective-permute-start | bytes 294920 | tf_op jit(solution)/shard_map/ppermute | solution.py:65
  52.9 0.6 copy-start.4
  53.6 13.5 %copy-start.2 = (bf16[128,768]{1,0:T(8,128)(2,1)}, bf16[128,768]{1,0:T(8,128)(2,1)S(1)}, u32[]{:S(2)}) copy-start(bf16[128,768]{1,0:T(8,128)(2,1)S(1)} %get-tuple-element.86.refs_4_) | copy-start | bytes 589828
  53.6 4.5 %collective-permute-start.10 = (bf16[256,3072]{1,0:T(8,128)(2,1)S(1)}, bf16[256,3072]{1,0:T(8,128)(2,1)S(1)}, u32[]{:S(2)}, u32[]{:S(2)}) collective-permute-start(bf16[256,3072]{1,0:T(8,128)(2,1)S(1)} %get-tuple-element.64.own_ref.g_in_ref), channel_id=1, source_target_pairs={{0,1},{1,0},{2,3},{3,2},{4,5},{5,4},{6,7},{7,6},{8,9},{9,8},{10,11... | collective-permute-start | bytes 4718600 | tf_op jit(solution)/shard_map/ppermute | solution.py:65
  53.6 4.5 %collective-permute-start.12 = (bf16[16,32,384]{2,1,0:T(8,128)(2,1)S(1)}, bf16[16,32,384]{2,1,0:T(8,128)(2,1)S(1)}, u32[]{:S(2)}, u32[]{:S(2)}) collective-permute-start(bf16[16,32,384]{2,1,0:T(8,128)(2,1)S(1)} %get-tuple-element.67), channel_id=1, source_target_pairs={{0,1},{1,0},{2,3},{3,2},{4,5},{5,4},{6,7},{7,6},{8,9},{9,8},{10,11... | collective-permute-start | bytes 1179656 | tf_op jit(solution)/shard_map/ppermute | solution.py:65
  54.1 3.7 %collective-permute-start.13 = (f32[128,384]{1,0:T(8,128)S(1)}, f32[128,384]{1,0:T(8,128)S(1)}, u32[]{:S(2)}, u32[]{:S(2)}) collective-permute-start(f32[128,384]{1,0:T(8,128)S(1)} %get-tuple-element.69), channel_id=1, source_target_pairs={{0,1},{1,0},{2,3},{3,2},{4,5},{5,4},{6,7},{7,6},{8,9},{9,8},{10,11... | collective-permute-start | bytes 589832 | tf_op jit(solution)/shard_map/ppermute | solution.py:65
  54.1 4.0 %collective-permute-start.11 = (bf16[256,384]{1,0:T(8,128)(2,1)S(1)}, bf16[256,384]{1,0:T(8,128)(2,1)S(1)}, u32[]{:S(2)}, u32[]{:S(2)}) collective-permute-start(bf16[256,384]{1,0:T(8,128)(2,1)S(1)} %get-tuple-element.65), channel_id=1, source_target_pairs={{0,1},{1,0},{2,3},{3,2},{4,5},{5,4},{6,7},{7,6},{8,9},{9,8},{10,11... | collective-permute-start | bytes 589832 | tf_op jit(solution)/shard_map/ppermute | solution.py:65
  62.0 14.2 %collective-permute-start.14 = (bf16[8,240,256]{2,1,0:T(8,128)(2,1)S(1)}, bf16[8,240,256]{2,1,0:T(8,128)(2,1)S(1)}, u32[]{:S(2)}, u32[]{:S(2)}) collective-permute-start(bf16[8,240,256]{2,1,0:T(8,128)(2,1)S(1)} %get-tuple-element.71), channel_id=1, source_target_pairs={{0,2},{1,5},{2,0},{3,7},{4,6},{5,1},{6,4},{7,3},{8,10},{9,13},{10,... | collective-permute-start | bytes 2949128 | tf_op jit(solution)/shard_map/ppermute | solution.py:65
  67.1 11.1 %collective-permute-start.23 = (bf16[4,64,768]{2,1,0:T(8,128)(2,1)S(1)}, bf16[4,64,768]{2,1,0:T(8,128)(2,1)S(1)}, u32[]{:S(2)}, u32[]{:S(2)}) collective-permute-start(bf16[4,64,768]{2,1,0:T(8,128)(2,1)S(1)} %bitcast.5), channel_id=1, source_target_pairs={{0,1},{1,0},{2,3},{3,2},{4,5},{5,4},{6,7},{7,6},{8,9},{9,8},{10,11... | collective-permute-start | bytes 1179656 | tf_op jit(solution)/shard_map/ppermute | solution.py:65
  67.4 27.4 %collective-permute-start.18 = (bf16[8,240,128]{2,1,0:T(8,128)(2,1)S(1)}, bf16[8,240,128]{2,1,0:T(8,128)(2,1)S(1)}, u32[]{:S(2)}, u32[]{:S(2)}) collective-permute-start(bf16[8,240,128]{2,1,0:T(8,128)(2,1)S(1)} %get-tuple-element.79), channel_id=1, source_target_pairs={{0,8},{1,9},{2,10},{3,11},{4,12},{5,13},{6,14},{7,15},{8,0},{9,1},... | collective-permute-start | bytes 1474568 | tf_op jit(solution)/shard_map/ppermute | solution.py:65
  76.3 31.2 %collective-permute-start.15 = (bf16[4,240,256]{2,1,0:T(8,128)(2,1)S(1)}, bf16[4,240,256]{2,1,0:T(8,128)(2,1)S(1)}, u32[]{:S(2)}, u32[]{:S(2)}) collective-permute-start(bf16[4,240,256]{2,1,0:T(8,128)(2,1)S(1)} %get-tuple-element.73), channel_id=1, source_target_pairs={{0,4},{1,3},{2,6},{3,1},{4,0},{5,7},{6,2},{7,5},{8,12},{9,11},{10,... | collective-permute-start | bytes 1474568 | tf_op jit(solution)/shard_map/ppermute | solution.py:65
  78.2 38.1 %collective-permute-start.24 = (bf16[3,128,768]{2,1,0:T(8,128)(2,1)S(1)}, bf16[3,128,768]{2,1,0:T(8,128)(2,1)S(1)}, u32[]{:S(2)}, u32[]{:S(2)}) collective-permute-start(bf16[3,128,768]{2,1,0:T(8,128)(2,1)S(1)} %shard_map.135), channel_id=1, source_target_pairs={{1,2},{2,1},{3,4},{4,3},{5,6},{6,5},{7,8},{8,7},{9,10},{10,9},{11,... | collective-permute-start | bytes 1769480 | tf_op jit(solution)/shard_map/ppermute | solution.py:78
  84.6 2.5 %collective-permute-start.26 = (f32[32,768]{1,0:T(8,128)S(1)}, f32[32,768]{1,0:T(8,128)S(1)}, u32[]{:S(2)}, u32[]{:S(2)}) collective-permute-start(f32[32,768]{1,0:T(8,128)S(1)} %get-tuple-element.102), channel_id=1, source_target_pairs={{0,1},{1,0},{2,3},{3,2},{4,5},{5,4},{6,7},{7,6},{8,9},{9,8},{10,11... | collective-permute-start | bytes 294920 | tf_op jit(solution)/shard_map/ppermute | solution.py:65
  87.1 5.1 %collective-permute-start.27 = (f32[32,768]{1,0:T(8,128)S(1)}, f32[32,768]{1,0:T(8,128)S(1)}, u32[]{:S(2)}, u32[]{:S(2)}) collective-permute-start(f32[32,768]{1,0:T(8,128)S(1)} %add.15), channel_id=1, source_target_pairs={{0,8},{1,9},{2,10},{3,11},{4,12},{5,13},{6,14},{7,15},{8,0},{9,1},... | collective-permute-start | bytes 294920 | tf_op jit(solution)/shard_map/ppermute | solution.py:65
  92.2 13.4 %collective-permute-start.28 = (f32[32,768]{1,0:T(8,128)S(1)}, f32[32,768]{1,0:T(8,128)S(1)}, u32[]{:S(2)}, u32[]{:S(2)}) collective-permute-start(f32[32,768]{1,0:T(8,128)S(1)} %add.16), channel_id=1, source_target_pairs={{0,16},{1,17},{2,18},{3,19},{4,20},{5,21},{6,22},{7,23},{8,24},{9,... | collective-permute-start | bytes 294920 | tf_op jit(solution)/shard_map/ppermute | solution.py:65
  94.9 17.6 %collective-permute-start.19 = (bf16[4,240,128]{2,1,0:T(8,128)(2,1)S(1)}, bf16[4,240,128]{2,1,0:T(8,128)(2,1)S(1)}, u32[]{:S(2)}, u32[]{:S(2)}) collective-permute-start(bf16[4,240,128]{2,1,0:T(8,128)(2,1)S(1)} %get-tuple-element.81), channel_id=1, source_target_pairs={{0,16},{1,17},{2,18},{3,19},{4,20},{5,21},{6,22},{7,23},{8,24},{9,... | collective-permute-start | bytes 737288 | tf_op jit(solution)/shard_map/ppermute | solution.py:65
  105.6 4.7 %collective-permute-start.29 = (f32[32,768]{1,0:T(8,128)S(1)}, f32[32,768]{1,0:T(8,128)S(1)}, u32[]{:S(2)}, u32[]{:S(2)}) collective-permute-start(f32[32,768]{1,0:T(8,128)S(1)} %add.17), channel_id=1, source_target_pairs={{0,2},{1,5},{2,0},{3,7},{4,6},{5,1},{6,4},{7,3},{8,10},{9,13},{10,... | collective-permute-start | bytes 294920 | tf_op jit(solution)/shard_map/ppermute | solution.py:65
  108.3 15.9 %collective-permute-start.16 = (bf16[2,240,256]{2,1,0:T(8,128)(2,1)}, bf16[2,240,256]{2,1,0:T(8,128)(2,1)}, u32[]{:S(2)}, u32[]{:S(2)}) collective-permute-start(bf16[2,240,256]{2,1,0:T(8,128)(2,1)} %get-tuple-element.75), channel_id=1, source_target_pairs={{0,8},{1,9},{2,10},{3,11},{4,12},{5,13},{6,14},{7,15},{8,0},{9,1},... | collective-permute-start | bytes 737288 | tf_op jit(solution)/shard_map/ppermute | solution.py:65
  110.3 5.4 %collective-permute-start.30 = (f32[32,768]{1,0:T(8,128)S(1)}, f32[32,768]{1,0:T(8,128)S(1)}, u32[]{:S(2)}, u32[]{:S(2)}) collective-permute-start(f32[32,768]{1,0:T(8,128)S(1)} %add.18), channel_id=1, source_target_pairs={{0,4},{1,3},{2,6},{3,1},{4,0},{5,7},{6,2},{7,5},{8,12},{9,11},{10,... | collective-permute-start | bytes 294920 | tf_op jit(solution)/shard_map/ppermute | solution.py:65
  113.2 3.2 %copy-start = (f32[2,232,128]{2,1,0:T(8,128)}, f32[2,232,128]{2,1,0:T(8,128)S(1)}, u32[]{:S(2)}) copy-start(f32[2,232,128]{2,1,0:T(8,128)S(1)} %get-tuple-element.82.old_ref) | copy-start | bytes 712708
  113.2 7.7 %collective-permute-start.20 = (bf16[2,240,128]{2,1,0:T(8,128)(2,1)}, bf16[2,240,128]{2,1,0:T(8,128)(2,1)S(1)}, u32[]{:S(2)}, u32[]{:S(2)}) collective-permute-start(bf16[2,240,128]{2,1,0:T(8,128)(2,1)} %get-tuple-element.83), channel_id=1, source_target_pairs={{0,2},{1,5},{2,0},{3,7},{4,6},{5,1},{6,4},{7,3},{8,10},{9,13},{10,... | collective-permute-start | bytes 368648 | tf_op jit(solution)/shard_map/ppermute | solution.py:65
  116.3 9.9 %collective-permute-start.31 = (f32[32,768]{1,0:T(8,128)}, f32[32,768]{1,0:T(8,128)}, u32[]{:S(2)}, u32[]{:S(2)}) collective-permute-start(f32[32,768]{1,0:T(8,128)} %add.19), channel_id=1, source_target_pairs={{0,1},{1,0},{2,3},{3,2},{4,5},{5,4},{6,7},{7,6},{8,9},{9,8},{10,11... | collective-permute-start | bytes 294920 | tf_op jit(solution)/shard_map/ppermute | solution.py:65
  116.3 21.5 %collective-permute-start.25 = (bf16[3,128,768]{2,1,0:T(8,128)(2,1)S(1)}, bf16[3,128,768]{2,1,0:T(8,128)(2,1)S(1)}, u32[]{:S(2)}, u32[]{:S(2)}) collective-permute-start(bf16[3,128,768]{2,1,0:T(8,128)(2,1)S(1)} %collective-permute-done.24.near_ref), channel_id=1, source_target_pairs={{0,1},{1,0},{2,3},{3,2},{4,5},{5,4},{6,7},{7,6},{8,9},{9,8},{10,11... | collective-permute-start | bytes 1769480 | tf_op jit(solution)/shard_map/ppermute | solution.py:65
  120.9 0.9 copy-start.1
  121.9 5.3 %collective-permute-start.21 = (bf16[1,240,128]{2,1,0:T(8,128)(2,1)S(1)}, bf16[1,240,128]{2,1,0:T(8,128)(2,1)S(1)}, u32[]{:S(2)}, u32[]{:S(2)}) collective-permute-start(bf16[1,240,128]{2,1,0:T(8,128)(2,1)S(1)} %get-tuple-element.85), channel_id=1, source_target_pairs={{0,4},{1,3},{2,6},{3,1},{4,0},{5,7},{6,2},{7,5},{8,12},{9,11},{10,... | collective-permute-start | bytes 184328 | tf_op jit(solution)/shard_map/ppermute | solution.py:65
  125.3 8.2 %collective-permute-start.17 = (bf16[1,240,256]{2,1,0:T(8,128)(2,1)S(1)}, bf16[1,240,256]{2,1,0:T(8,128)(2,1)S(1)}, u32[]{:S(2)}, u32[]{:S(2)}) collective-permute-start(bf16[1,240,256]{2,1,0:T(8,128)(2,1)S(1)} %get-tuple-element.77), channel_id=1, source_target_pairs={{0,16},{1,17},{2,18},{3,19},{4,20},{5,21},{6,22},{7,23},{8,24},{9,... | collective-permute-start | bytes 368648 | tf_op jit(solution)/shard_map/ppermute | solution.py:65
  133.5 0.9 copy-start.3
  134.4 0.8 copy-start.5
  136.2 5.1 %collective-permute-start.22 = (f32[104,384]{1,0:T(8,128)S(1)}, f32[104,384]{1,0:T(8,128)S(1)}, u32[]{:S(2)}, u32[]{:S(2)}) collective-permute-start(f32[104,384]{1,0:T(8,128)S(1)} %get-tuple-element.89), channel_id=1, source_target_pairs={{0,1},{1,0},{2,3},{3,2},{4,5},{5,4},{6,7},{7,6},{8,9},{9,8},{10,11... | collective-permute-start | bytes 479240 | tf_op jit(solution)/shard_map/ppermute | solution.py:65

commit v2 on v1

--- a/solution.py
+++ b/solution.py
@@ -80,9 +80,11 @@
 
 def orders(bits, chunk):
     plain = list(range(bits))
-    mixed = [k ^ 1 if k < 2 and bits > 1 else k for k in range(bits)]
-    turn = chunk * (bits // 2)
-    return plain[turn:] + plain[:turn], mixed[turn:] + mixed[:turn]
+    if bits < 4:
+        return plain, plain
+    if chunk == 0:
+        return [1, 2, 0] + plain[3:], [2, 1, 3, 0] + plain[4:]
+    return plain, [0, 3, 1, 2] + plain[4:]
 
 
 def layout_place(chip, row, core, order):
@@ -241,8 +243,13 @@
     return [(ref, i, i) for i in range(3)] + [(ref, i + 3, i + height + 3) for i in range(3)]
 
 
-def lane_block(k):
-    return pl.ds(pl.multiple_of(k * 128, 128), 128)
+def over_lanes(width, block):
+    def step(k, carry):
+        for side in range(2):
+            block(pl.ds(pl.multiple_of(k * 256 + side * 128, 128), 128))
+        return carry
+
+    lax.fori_loop(0, width // 256, step, 0)
 
 
 def local_body(flipped, copied, *refs):
@@ -257,16 +264,14 @@
     height, breadth, width = other_ref.shape
     fill_center(pad_ref, own_ref, other_ref)
 
-    def block(k, carry):
-        lanes = lane_block(k)
+    def block(lanes):
         sums = convolve(
             center_lines(pad_ref), [None] * height, taps_ref, breadth, lanes, flipped
         )
         for i, row in enumerate(sums):
             sum_ref[i * breadth : (i + 1) * breadth, lanes] = row
-        return carry
-
-    lax.fori_loop(0, width // 128, block, 0)
+
+    over_lanes(width, block)
     for copy in copies:
         copy.wait()
 
@@ -294,18 +299,15 @@
     steps, half = width // 128, width // 2
     fill_edges(edge_ref, near_ref, far_ref)
 
-    def block(k, carry):
-        lanes = lane_block(k)
+    for k in range(0, width, 128):
+        lanes = slice(k, k + 128)
         sums = [sum_ref[i * breadth : (i + 1) * breadth, lanes] for i in range(height)]
         sums = convolve(edge_lines(edge_ref, height), sums, taps_ref, breadth, lanes, False)
         for i, row in enumerate(sums):
             full_ref[i * breadth : (i + 1) * breadth, lanes] = row
-        return carry
-
-    lax.fori_loop(0, steps, block, 0)
-
-    def chunk(i, carry):
-        rows = pl.ds(pl.multiple_of(i * 16, 16), 16)
+
+    for i in range(0, places, 16):
+        rows = slice(i, i + 16)
         parts = [full_ref[rows, s * 128 : (s + 1) * 128] for s in range(steps)]
         mean = jnp.sum(functools.reduce(jnp.add, parts), axis=1, keepdims=True) * (1.0 / width)
         parts = [p - mean for p in parts]
@@ -317,9 +319,6 @@
             value = p * inv
             full_ref[rows, s * 128 : (s + 1) * 128] = value
             normed_ref[rows, s * 128 : (s + 1) * 128] = value.astype(BF16)
-        return carry
-
-    lax.fori_loop(0, places // 16, chunk, 0, unroll=4)
     c = lax.axis_index("col")
     send_ref[...] = normed_ref[:, pl.ds(pl.multiple_of((1 - c) * half, 128), half)]
 
@@ -351,10 +350,6 @@
 
 
 UNITS = 768
-
-
-def unit_block(f):
-    return pl.ds(pl.multiple_of(f * UNITS, UNITS), UNITS)
 
 
 def forward_body(
@@ -370,36 +365,39 @@
     per_core = per_chip // 2
     slot = slot_ref[...]
     select = (slot == iota((places, regions), 1).astype(F32)).astype(BF16)
-    branch[...] = jnp.zeros_like(branch)
-
-    def units(f, carry):
-        at = unit_block(f)
-        pre[...] = dot(normed_ref[...], w_in_ref[:, at])
-
-        def chunk(i, inner):
-            line = pl.ds(pl.multiple_of(i * 16, 16), 16)
+    blocks = total // UNITS
+
+    def expand(f):
+        pre[f % 2] = dot(normed_ref[...], w_in_ref[:, f * UNITS : (f + 1) * UNITS])
+
+    def activate(f):
+        for row in range(0, places, 16):
+            line = slice(row, row + 16)
             for start in range(0, UNITS, 256):
-                lanes = slice(start, start + 256)
-                value = pre[line, lanes]
+                value = pre[f % 2, line, start : start + 256]
                 cdf = 0.5 * (1.0 + lax.erf(value * (1.0 / math.sqrt(2.0))))
                 density = jnp.exp(-0.5 * value * value) * (1.0 / math.sqrt(2.0 * math.pi))
-                hidden[line, lanes] = (value * cdf).astype(BF16)
-                out = pl.ds(pl.multiple_of(f * UNITS + start, 256), 256)
-                slope_ref[line, out] = cdf + value * density
-            return inner
-
-        lax.fori_loop(0, places // 16, chunk, 0)
-        branch[...] += dot(hidden[...], w_out_ref[at, :])
-        by_region = dot(hidden[...], select, CONTRACT_ROWS)
+                hidden[f % 2, line, start : start + 256] = (value * cdf).astype(BF16)
+                at = f * UNITS + start
+                slope_ref[line, at : at + 256] = cdf + value * density
+
+    def reduce(f):
+        part = dot(hidden[f % 2], w_out_ref[f * UNITS : (f + 1) * UNITS, :])
+        branch[...] = part if f == 0 else branch[...] + part
+        by_region = dot(hidden[f % 2], select, CONTRACT_ROWS)
         for t in range(UNITS // per_chip):
             q = f * (UNITS // per_chip) + t
             low = by_region[t * per_chip : t * per_chip + per_core]
             high = by_region[t * per_chip + per_core : (t + 1) * per_chip]
             h_mine_ref[q] = lane_pack(jnp.where(c == 0, low, high), half // 128)
             h_send_ref[q] = lane_pack(jnp.where(c == 0, high, low), half // 128).astype(BF16)
-        return carry
-
-    lax.fori_loop(0, total // UNITS, units, 0)
+
+    expand(0)
+    for f in range(blocks):
+        if f + 1 < blocks:
+            expand(f + 1)
+        activate(f)
+        reduce(f)
     block[...] = (image_ref[...].astype(F32) + scale_ref[...] * branch[...]).astype(BF16)
     for at, out in ((c, s_mine_ref), (1 - c, s_send_ref)):
         columns = block[:, pl.ds(pl.multiple_of(at * half, 128), half)]
@@ -418,8 +416,8 @@
         ((regions, half), F32),
     ]
     scratch = [
-        pltpu.VMEM((places, UNITS), F32),
-        pltpu.VMEM((places, UNITS), BF16),
+        pltpu.VMEM((2, places, UNITS), F32),
+        pltpu.VMEM((2, places, UNITS), BF16),
         pltpu.VMEM((places, width), F32),
         pltpu.VMEM((places, width), BF16),
     ]
@@ -448,7 +446,8 @@
     count = dot(known[:, :regions], is_count.astype(BF16), CONTRACT_ROWS)
     count_ref[...] = count
     line = iota((regions, total), 1)
-    source = (me ^ (line >> 3)) * owned + (line & 7)
+    bits = (total >> 4).bit_length() - 1
+    source = gathered_device(line >> 3, me, bits) * owned + (line & 7)
     place = ((line & 7) < owned) & (source == iota((regions, total), 0))
     pooled = dot(place.astype(BF16), known)
     region_grad = (pooled / (4.0 * count[:, :1])).astype(BF16)
@@ -458,13 +457,10 @@
     g_out[...] = dot(select, g_region).astype(BF16)
     dblock_ref[...] = dot(select, region_grad).astype(BF16)
 
-    def block(f, carry):
-        at = unit_block(f)
+    for f in range(0, units, UNITS):
+        at = slice(f, f + UNITS)
         dhidden = dot(g_out[...], w_out_ref[at, :], CONTRACT_LANES)
         g_in_ref[:, at] = (dhidden * slope_ref[:, at]).astype(BF16)
-        return carry
-
-    lax.fori_loop(0, units // UNITS, block, 0)
 
 
 def mlp_backward(known, slot, scale, w_out, slope, regions):
@@ -485,17 +481,10 @@
 
 def norm_backward_body(g_in_ref, w_in_ref, full_ref, inv_ref, dconv_ref, narrow_ref):
     places, width = dconv_ref.shape
-    dconv_ref[...] = dot(g_in_ref[:, :UNITS], w_in_ref[:, :UNITS], CONTRACT_LANES)
-
-    def block(f, carry):
-        at = unit_block(f)
-        dconv_ref[...] += dot(g_in_ref[:, at], w_in_ref[:, at], CONTRACT_LANES)
-        return carry
-
-    lax.fori_loop(1, w_in_ref.shape[1] // UNITS, block, 0)
-
-    def chunk(i, carry):
-        rows = pl.ds(pl.multiple_of(i * 16, 16), 16)
+    dconv_ref[...] = dot(g_in_ref[...], w_in_ref[...], CONTRACT_LANES)
+
+    for i in range(0, places, 16):
+        rows = slice(i, i + 16)
         lanes = [slice(s, s + 128) for s in range(0, width, 128)]
         grads = [dconv_ref[rows, at] for at in lanes]
         fulls = [full_ref[rows, at] for at in lanes]
@@ -507,9 +496,6 @@
             value = inv * (g - mean - n * along)
             dconv_ref[rows, at] = value
             narrow_ref[rows, at] = value.astype(BF16)
-        return carry
-
-    lax.fori_loop(0, places // 16, chunk, 0, unroll=4)
 
 
 def norm_backward(g_in, w_in, full, inv):
@@ -540,42 +526,28 @@
     per = s_mine_ref.shape[0] // rows
     columns = pl.ds(pl.multiple_of(c * half, 128), half)
 
-    def store(q, value, first, split):
+    def store(q, value, first):
         for k, (lane, wide) in enumerate(CHUNKS):
-            keep_ref, send_ref = out_refs[2 * k : 2 * k + 2]
-            j = layout_place(q, r, c, orders(bits, k))
-            part = value[:, lane : lane + wide]
-
-            @pl.when(j < count)
-            def _():
-                keep_ref[j, first : first + value.shape[0], :] = part
-
-            @pl.when(j >= count)
-            def _():
-                if split:
-                    tail = jnp.concatenate(split_high_low(part), axis=0)
-                else:
-                    tail = part.astype(BF16)
-                send_ref[j - count, first : first + tail.shape[0], :] = tail
-
-    def block(f, carry):
-        at = unit_block(f)
+            j = layout_place(jnp.int32(q), r, c, orders(bits, k))
+            out_refs[2 * k][j, first : first + value.shape[0], :] = value[:, lane : lane + wide]
+
+    for q in range(rows):
+        store(q, h_mine_ref[q] + h_got_ref[q].astype(F32), per_chip)
+        at = slice(q * per, (q + 1) * per)
+        store(q, s_mine_ref[at, :] + s_got_ref[at, :], per_chip + packed)
+    for f in range(0, total, UNITS):
+        at = slice(f, f + UNITS)
         grad = dot(own_ref[:, at], normed_ref[:, columns], CONTRACT_ROWS)
         grad += dot(other_ref[:, at], normed_other_ref[...], CONTRACT_ROWS)
         for t in range(UNITS // per_chip):
-            q = f * (UNITS // per_chip) + t
-            store(q, grad[t * per_chip : (t + 1) * per_chip], 0, False)
-        return carry
-
-    lax.fori_loop(0, total // UNITS, block, 0)
-
-    def chip(q, carry):
-        store(q, h_mine_ref[q] + h_got_ref[q].astype(F32), per_chip, False)
-        at = pl.ds(pl.multiple_of(q * per, per), per)
-        store(q, s_mine_ref[at, :] + s_got_ref[at, :], per_chip + packed, True)
-        return carry
-
-    lax.fori_loop(0, rows, chip, 0)
+            store((f + t * per_chip) // per_chip, grad[t * per_chip : (t + 1) * per_chip], 0)
+    body = per_chip + packed
+    for k in range(len(CHUNKS)):
+        all_ref, send_ref = out_refs[2 * k : 2 * k + 2]
+        for j in range(count):
+            send_ref[j, :body, :] = all_ref[count + j, :body, :].astype(BF16)
+            sums = all_ref[count + j, body:, :]
+            send_ref[j, body:, :] = jnp.concatenate(split_high_low(sums), axis=0)
 
 
 def weight_gradient(g_in, g_other, normed, normed_other, h_mine, h_got, s_mine, s_got):
@@ -585,7 +557,7 @@
     height = total // rows + packed + per
     outs = []
     for _, wide in CHUNKS:
-        outs.append(((rows // 2, height, wide), F32))
+        outs.append(((rows, height, wide), F32))
         outs.append(((rows // 2, height + per, wide), BF16))
     return call(functools.partial(weight_body, rows), outs, 5.0, room=12)(
         g_in, g_other, normed, normed_other, h_mine, h_got, s_mine, s_got
@@ -620,20 +592,91 @@
 
 
 def halving_round(keep, got, per):
-    count, height, wide = keep.shape
-    left = count // 2
+    _, height, wide = keep.shape
+    left = got.shape[0] // 2
     outs = [((left, height, wide), F32), ((left, height + per, wide), BF16)]
     return call(functools.partial(round_body, per), outs, 0.5)(keep, got)
 
 
+def taps_to_rows(taps):
+    return jnp.concatenate(
+        [taps[:, k : k + 128] for k in range(0, taps.shape[1], 128)], axis=0
+    )
+
+
+def rows_to_taps(rows, count):
+    pieces = [rows[k : k + count] for k in range(0, rows.shape[0], count)]
+    return jnp.concatenate(pieces, axis=1)
+
+
+def taps_received(got_ref, first, count):
+    rows = (got_ref.shape[0] - first) // 2
+    high = got_ref[first : first + rows, :].astype(F32)
+    return rows_to_taps(high + got_ref[first + rows :, :].astype(F32), count)
+
+
+def tapped_round_body(
+    per, carried, old_ref, got_ref, taps_ref, taps_got_ref, keep_ref, send_ref, taps_out_ref
+):
+    left = keep_ref.shape[0]
+    height = keep_ref.shape[1] + per
+    body = keep_ref.shape[1] - per
+
+    def block(i):
+        at = pl.ds(pl.multiple_of(i * height, 16), height)
+        return merged(old_ref[i], got_ref[at, :], per)
+
+    def near(i, carry):
+        plain, sums = block(i)
+        keep_ref[i, :body, :] = plain
+        keep_ref[i, body:, :] = sums
+        return carry
+
+    def far(i, carry):
+        plain, sums = block(i + left)
+        send_ref[pl.ds(pl.multiple_of(i * height, 16), body), :] = plain.astype(BF16)
+        tail = pl.ds(pl.multiple_of(i * height + body, 16), 2 * per)
+        send_ref[tail, :] = jnp.concatenate(split_high_low(sums), axis=0)
+        return carry
+
+    lax.fori_loop(0, left, far, 0)
+    count = taps_ref.shape[0]
+    if carried:
+        taps = taps_ref[...] + taps_received(got_ref, 2 * left * height, count)
+    else:
+        taps = taps_ref[...] + taps_got_ref[...]
+    high, low = split_high_low(taps)
+    taps_out_ref[...] = high.astype(F32) + low.astype(F32)
+    rows = taps_to_rows(taps).shape[0]
+    high, low = split_high_low(taps_to_rows(taps))
+    send_ref[left * height : left * height + rows, :] = high
+    send_ref[left * height + rows :, :] = low
+    lax.fori_loop(0, left, near, 0)
+
+
+def tapped_round(keep, got, taps, taps_got, left, per):
+    _, height, wide = keep.shape
+    rows = taps.size // wide
+    outs = [
+        ((left, height, wide), F32),
+        ((left * (height + per) + 2 * rows, wide), BF16),
+        (taps.shape, F32),
+    ]
+    carried = taps_got is None
+    body = functools.partial(tapped_round_body, per, carried)
+    return call(body, outs, 0.5)(keep, got.reshape(-1, wide), taps, taps if carried else taps_got)
+
+
 def finish_body(per, *refs):
-    parts = refs[: 2 * len(CHUNKS)]
-    region_ref, count_ref, out_ref, mine_ref, send_ref = refs[2 * len(CHUNKS) :]
+    keep_a, got_a, keep_b, got_b, taps_ref, region_ref, count_ref = refs[:7]
+    out_ref, mine_ref, send_ref = refs[7:]
     r, c = lax.axis_index("row"), lax.axis_index("col")
-    done = [merged(parts[2 * k][0], parts[2 * k + 1][0], per) for k in range(len(CHUNKS))]
+    height = keep_b.shape[1] + per
+    done = [merged(keep_a[0], got_a[0], per), merged(keep_b[0], got_b[:height, :], per)]
     plain = jnp.concatenate([d[0] for d in done], axis=1)
     sums = jnp.concatenate([d[1] for d in done], axis=1)
     per_core = out_ref.shape[0]
+    half = plain.shape[1]
     first, second = plain[:per_core], plain[per_core : 2 * per_core]
     high, low = split_high_low(lane_unpack(plain[2 * per_core :], per_core))
     out_ref[...] = dot(high, region_ref[...]) + dot(low, region_ref[...])
@@ -641,22 +684,30 @@
     send_ref[:per_core, :] = jnp.where(c == 0, second, first)
     start = pl.multiple_of(r * per, per)
     pooled = sums / (4.0 * count_ref[pl.ds(start, per), :1])
-    mine_ref[per_core:, :] = pooled
-    send_ref[per_core:, :] = pooled
-
-
-def finish(parts, region, count, per, per_core):
+    count = taps_ref.shape[0]
+    taps = taps_ref[...] + taps_received(got_b, height, count)
+    for ref in (mine_ref, send_ref):
+        ref[per_core : per_core + per, :] = pooled
+        ref[per_core + per : per_core + per + count, :] = taps[:, :half]
+        ref[per_core + per + count :, :] = taps[:, half:]
+
+
+def finish(parts, taps, region, count, per, per_core):
     width = region.shape[1]
-    part = ((per_core + per, width // 2), F32)
+    part = ((per_core + per + 2 * taps.shape[0], width // 2), F32)
     outs = [((per_core, width), F32), part, part]
-    return call(functools.partial(finish_body, per), outs, 1.0, far_out=(0,))(*parts, region, count)
-
-
-def place_body(mine_ref, got_ref, grad_ref, pool_ref):
+    return call(functools.partial(finish_body, per), outs, 1.0, far_out=(0,))(
+        *parts, taps, region, count
+    )
+
+
+def place_body(per, mine_ref, got_ref, grad_ref, pool_ref, taps_ref):
     c = lax.axis_index("col")
     per_core, width = grad_ref.shape
     half = width // 2
     owned = pool_ref.shape[0]
+    first = per_core + per
+    count = (mine_ref.shape[0] - first) // 2
     for core in range(2):
 
         @pl.when(c == core)
@@ -667,12 +718,17 @@
             rows = slice(per_core + core * owned, per_core + (core + 1) * owned)
             pool_ref[:, :half] = left[rows, :]
             pool_ref[:, half:] = right[rows, :]
-
-
-def place_outputs(mine, got, per_core, owned):
+            for k in range(2):
+                at = slice(k * half, (k + 1) * half)
+                low = first + k * count
+                taps_ref[:28, at] = left[low : low + 28, :]
+                taps_ref[28:, at] = right[low : low + 21, :]
+
+
+def place_outputs(mine, got, per_core, owned, per):
     width = 2 * mine.shape[1]
-    outs = [((per_core, width), F32), ((owned, width), F32)]
-    return call(place_body, outs, 0.5, far_out=(0, 1))(mine, got)
+    outs = [((per_core, width), F32), ((owned, width), F32), ((49, width), F32)]
+    return call(functools.partial(place_body, per), outs, 0.5, far_out=(0, 1, 2))(mine, got)
 
 
 def kernel_gradient_body(pad_ref, edge_ref, dconv_ref, mine_ref, send_ref):
@@ -680,8 +736,7 @@
     height, wide, width = pad_ref.shape
     breadth = wide - 16
 
-    def block(k, carry):
-        lanes = lane_block(k)
+    def block(lanes):
         sums = {}
         grads = [dconv_ref[i * breadth : (i + 1) * breadth, lanes] for i in range(height)]
         for b in range(7):
@@ -713,9 +768,7 @@
             put(mine_ref, 4, 7)
             put(send_ref, 0, 4)
 
-        return carry
-
-    lax.fori_loop(0, width // 128, block, 0)
+    over_lanes(width, block)
 
 
 def kernel_gradient(padded, edges, dconv):
@@ -728,16 +781,14 @@
     height, breadth, width = out_ref.shape
     fill_edges(edge_ref, near_ref, far_ref)
 
-    def block(k, carry):
-        lanes = lane_block(k)
+    def block(lanes):
         sums = [sum_ref[i * breadth : (i + 1) * breadth, lanes] for i in range(height)]
         sums = convolve(edge_lines(edge_ref, height), sums, taps_ref, breadth, lanes, True)
         for i, row in enumerate(sums):
             rows = slice(i * breadth, (i + 1) * breadth)
             out_ref[i, :, lanes] = (dblock_ref[rows, lanes].astype(F32) + row).astype(BF16)
-        return carry
-
-    lax.fori_loop(0, width // 128, block, 0)
+
+    over_lanes(width, block)
 
 
 def back_convolution(near, far, taps, sums, dblock):
@@ -749,10 +800,14 @@
     return out
 
 
+def gather_stages(bits):
+    return list(range((bits - 1) // 2 * 2, -1, -2))
+
+
 def gather_known(known):
     bits = lax.axis_size("row").bit_length() - 1
     pieces = [known, swap_core(known)]
-    for low in range(0, bits, 2):
+    for low in gather_stages(bits):
         known = jnp.concatenate(pieces, axis=0)
         pieces = [known]
         for mask in (1 << low, 2 << low, 3 << low):
@@ -760,12 +815,18 @@
     return pieces
 
 
+def gathered_device(block, me, bits):
+    mask = block & 1
+    for k, low in enumerate(gather_stages(bits)):
+        mask = mask | (((block >> (2 * k + 1)) & 3) << (low + 1))
+    return me ^ mask
+
+
 def compute(image, dw_kernel, w_in, w_out, layer_scale, region_ids, region_slot, pool_grad):
     height, breadth, width = image.shape
     total = w_in.shape[1]
     rows = lax.axis_size("row")
     bits = rows.bit_length() - 1
-    c = lax.axis_index("col")
     regions = region_slot.shape[0]
     owned = pool_grad.shape[0]
     known, slot, own, taps, scale = prepare(
@@ -787,29 +848,25 @@
     dconv, narrow = norm_backward(g_in, w_in, full, inv)
     halves = weight_gradient(g_in, g_other, normed, normed_other, h_mine, h_got, s_mine, s_got)
     per = regions // rows
+    part, part_send = kernel_gradient(padded, edges, dconv)
+    part = part + swap_core(part_send)
+    order = orders(bits, 1)
+    part_got = exchange(part, (1 << order[0][0], 1 << order[1][0]))
     parts = []
     for k in range(len(CHUNKS)):
         keep, send = halves[2 * k : 2 * k + 2]
         order = orders(bits, k)
         for step in range(bits):
             got = exchange(send, (1 << order[0][step], 1 << order[1][step]))
-            if step < bits - 1:
+            if step == bits - 1:
+                break
+            if k == 0:
                 keep, send = halving_round(keep, got, per)
+            else:
+                left = rows >> (step + 2)
+                keep, send, part = tapped_round(keep, got, part, part_got, left, per)
+                part_got = None
         parts += [keep, got]
-
-    part, part_send = kernel_gradient(padded, edges, dconv)
-    part = part + swap_core(part_send)
-    order = orders(bits, 1)
-    for step in range(bits):
-        part = part + exchange(part, (1 << order[0][step], 1 << order[1][step]))
-    part_other = swap_core(part)
-    grad_kernel = jnp.concatenate(
-        [
-            jnp.where(c == 0, part, part_other)[:28],
-            jnp.where(c == 0, part_other, part)[:21],
-        ],
-        axis=0,
-    )
 
     narrow = narrow.reshape(height, breadth, width)
     d_other, d_near, d_far = halo(narrow, narrow)
@@ -817,9 +874,9 @@
     grad_image = back_convolution(d_near, d_far, taps, back, dblock)
 
     per_core = total // rows // 2
-    grad_w_out, mine, send = finish(parts, g_region, count, per, per_core)
+    grad_w_out, mine, send = finish(parts, part, g_region, count, per, per_core)
     got = swap_core(send)
-    grad_w_in, region_pool = place_outputs(mine, got, per_core, owned)
+    grad_w_in, region_pool, grad_kernel = place_outputs(mine, got, per_core, owned, per)
     return (region_pool, grad_image, grad_w_in.T, grad_w_out, grad_kernel)
 
 

time: 142 us -> 122 us (0.86)
  Pallas kernels: 46.6 us -> 33.7 us
  starting transfers between devices: 49.5 us -> 42.7 us
  waiting for transfers between devices: 38.5 us -> 45 us
  local copies, waits for them, and re-layouts: 3.34 us -> 0.01 us
  other arithmetic: 3.27 us -> 0.01 us
    pallas_call x20, Pallas kernels: 46.6 us -> 33.7 us  [run(): pl.pallas_call(body, in_specs=specs, out_specs=[VMEM] * len(outs), out_sh...]
    ppermute x30 -> x26, starting transfers between devices: 48.1 us -> 41.3 us  [exchange(): return lax.ppermute(value, AXES, pairs)]
    ppermute x30 -> x26, waiting for transfers between devices: 38.5 us -> 45 us  [exchange(): return lax.ppermute(value, AXES, pairs)]
    unnamed x15 -> x3, local copies, waits for them, and re-layouts: 3.33 us -> 0.01 us
    select_n x2 -> x0, other arithmetic: 1.88 us -> none  [the longest x1 0.95 us: compute(): jnp.where(c == 0, part, part_other)[:28]]
  transfers between devices with their start and end apart: 32 -> 28, of which waited for: 12 -> 10; matrix products, arithmetic and copies ran while one was open for 2% -> 0% of each run, Pallas kernels for 28% -> 24%
where the time goes in v2:
time: 122 us
  waiting for transfers between devices  45 us (37%)
  starting transfers between devices  42.7 us (35%)
  Pallas kernels  33.7 us (28%)
    ppermute x26, waiting for transfers between devices, exchange(): return lax.ppermute(value, AXES, pairs)  45 us
    ppermute x26, starting transfers between devices, exchange(): return lax.ppermute(value, AXES, pairs)  41.3 us
    pallas_call x20, Pallas kernels, run(): pl.pallas_call(body, in_specs=specs, out_specs=[VMEM] * len(outs), out_sh...  33.7 us
  transfers between devices with their start and end apart: 28, of which 10 were waited for; matrix products, arithmetic and copies ran while one was open for 0% of the time, Pallas kernels for 24%

profile of v2, /device:TPU:0, one launch (start us, length us, event | category | flops | bytes accessed | tf_op | source)
XLA Modules:
  0.0 122.2 jit_solution(12033449114446374929)
XLA Ops:
  0.6 0.6 collective-permute-start.7
  1.2 1.8 %shard_map.119 = (bf16[8,768]{1,0:T(8,128)(2,1)S(1)}, f32[256,1]{1,0:T(8,128)S(1)}, bf16[4,64,768]{2,1,0:T(8,128)(2,1)S(1)}, f32[49,768]{1,0:T(8,128)S(1)}, f32[1,768]{1,0:T(1,128)S(1)}) custom-call(s32[2,32]{1,0:T(2,128)} %ids_ref.1, s32[1,128]{1,0:T(1,128)} %bitcast.9, bf16[4,768]{1,0:T(4,128)(2,1)} %grad_ref.1, bf16[4,64,768]{2,1,0:T(8,128)(2,1)} %image_ref.1, ...), custom_call_target="tpu_custom_call" | custom-call | bytes 4500000 | tf_op jit(solution)/shard_map/pallas_call | solution.py:44
  3.0 0.0 collective-permute-done.7.refs_1_.other_ref
  3.0 0.1 shard_map.121
  3.1 0.7 collective-permute-start.8
  3.8 4.0 %collective-permute-start = (bf16[8,768]{1,0:T(8,128)(2,1)S(1)}, bf16[8,768]{1,0:T(8,128)(2,1)S(1)}, u32[]{:S(2)}, u32[]{:S(2)}) collective-permute-start(bf16[8,768]{1,0:T(8,128)(2,1)S(1)} %get-tuple-element.58), channel_id=1, source_target_pairs={{0,1},{1,0},{2,3},{3,2},{4,5},{5,4},{6,7},{7,6},{8,9},{9,8},{10,11... | collective-permute-start | bytes 36872 | tf_op jit(solution)/shard_map/ppermute | solution.py:65
  7.7 13.1 %collective-permute-start.9 = (bf16[3,128,768]{2,1,0:T(8,128)(2,1)S(1)}, bf16[3,128,768]{2,1,0:T(8,128)(2,1)S(1)}, u32[]{:S(2)}, u32[]{:S(2)}) collective-permute-start(bf16[3,128,768]{2,1,0:T(8,128)(2,1)S(1)} %collective-permute-done.8.near_ref), channel_id=1, source_target_pairs={{0,1},{1,0},{2,3},{3,2},{4,5},{5,4},{6,7},{7,6},{8,9},{9,8},{10,11... | collective-permute-start | bytes 1769480 | tf_op jit(solution)/shard_map/ppermute | solution.py:65
  20.8 0.0 collective-permute-done
  20.8 2.5 %collective-permute-start.1 = (bf16[16,768]{1,0:T(8,128)(2,1)S(1)}, bf16[16,768]{1,0:T(8,128)(2,1)S(1)}, u32[]{:S(2)}, u32[]{:S(2)}) collective-permute-start(bf16[16,768]{1,0:T(8,128)(2,1)S(1)} %get-tuple-element.111), channel_id=1, source_target_pairs={{0,8},{1,9},{2,10},{3,11},{4,12},{5,13},{6,14},{7,15},{8,0},{9,1},... | collective-permute-start | bytes 73736 | tf_op jit(solution)/shard_map/ppermute | solution.py:65
  23.3 2.5 %collective-permute-start.3 = (bf16[16,768]{1,0:T(8,128)(2,1)S(1)}, bf16[16,768]{1,0:T(8,128)(2,1)S(1)}, u32[]{:S(2)}, u32[]{:S(2)}) collective-permute-start(bf16[16,768]{1,0:T(8,128)(2,1)S(1)} %get-tuple-element.111), channel_id=1, source_target_pairs={{0,24},{1,25},{2,26},{3,27},{4,28},{5,29},{6,30},{7,31},{8,16},{9,... | collective-permute-start | bytes 73736 | tf_op jit(solution)/shard_map/ppermute | solution.py:65
  25.8 0.1 collective-permute-start.2
  25.9 0.0 collective-permute-done.1
  25.9 4.9 %collective-permute-done.2 = bf16[16,768]{1,0:T(8,128)(2,1)S(1)} collective-permute-done((bf16[16,768]{1,0:T(8,128)(2,1)S(1)}, bf16[16,768]{1,0:T(8,128)(2,1)S(1)}, u32[]{:S(2)}, u32[]{:S(2)}) %collective-permute-start.2) | collective-permute-done | bytes 24608 | tf_op jit(solution)/shard_map/ppermute | solution.py:65
  30.8 2.0 %collective-permute-start.6 = (bf16[64,768]{1,0:T(8,128)(2,1)S(1)}, bf16[64,768]{1,0:T(8,128)(2,1)S(1)}, u32[]{:S(2)}, u32[]{:S(2)}) collective-permute-start(bf16[64,768]{1,0:T(8,128)(2,1)S(1)} %constant_dynamic-update-slice_fusion.2.refs_0_), channel_id=1, source_target_pairs={{0,6},{1,7},{2,4},{3,5},{4,2},{5,3},{6,0},{7,1},{8,14},{9,15},{10,... | collective-permute-start | bytes 294920 | tf_op jit(solution)/shard_map/ppermute | solution.py:65
  32.8 1.8 %collective-permute-start.5 = (bf16[64,768]{1,0:T(8,128)(2,1)S(1)}, bf16[64,768]{1,0:T(8,128)(2,1)S(1)}, u32[]{:S(2)}, u32[]{:S(2)}) collective-permute-start(bf16[64,768]{1,0:T(8,128)(2,1)S(1)} %constant_dynamic-update-slice_fusion.2.refs_0_), channel_id=1, source_target_pairs={{0,4},{1,5},{2,6},{3,7},{4,0},{5,1},{6,2},{7,3},{8,12},{9,13},{10,... | collective-permute-start | bytes 294920 | tf_op jit(solution)/shard_map/ppermute | solution.py:65
  34.6 0.0 collective-permute-start.4
  34.6 3.8 %shard_map.120 = (f32[4,80,768]{2,1,0:T(8,128)S(1)}, f32[256,768]{1,0:T(8,128)S(1)}, bf16[768,3072]{1,0:T(8,128)(2,1)S(1)}, bf16[3072,768]{1,0:T(8,128)(2,1)S(1)}) custom-call(bf16[4,64,768]{2,1,0:T(8,128)(2,1)S(1)} %get-tuple-element.61.refs_0_.own_ref, bf16[4,64,768]{2,1,0:T(8,128)(2,1)S(1)} %collective-permute-done.7.refs_1_.other_ref, ...), custom_call_target="tpu_custom_call" | custom-call | bytes 12000000 | tf_op jit(solution)/shard_map/pallas_call | solution.py:44
  38.4 0.0 collective-permute-done.9.far_ref
  38.4 3.5 %shard_map.122 = (f32[6,80,768]{2,1,0:T(8,128)S(1)}, bf16[256,768]{1,0:T(8,128)(2,1)S(1)}, bf16[256,384]{1,0:T(8,128)(2,1)S(1)}, f32[256,768]{1,0:T(8,128)S(1)}, f32[256,128]{1,0:T(8,128)S(1)}) custom-call(bf16[3,128,768]{2,1,0:T(8,128)(2,1)S(1)} %collective-permute-done.8.near_ref, bf16[3,128,768]{2,1,0:T(8,128)(2,1)S(1)} %collective-permute-done.9.far_ref, ...), custom_call_target="tpu_custom_call" | custom-call | bytes 15000000 | tf_op jit(solution)/shard_map/pallas_call | solution.py:44
  41.9 3.7 %shard_map.123 = (f32[256,3072]{1,0:T(8,128)S(1)}, f32[16,32,384]{2,1,0:T(8,128)S(1)}, bf16[16,32,384]{2,1,0:T(8,128)(2,1)S(1)}, f32[128,384]{1,0:T(8,128)S(1)}, f32[128,384]{1,0:T(8,128)S(1)}) custom-call(bf16[256,768]{1,0:T(8,128)(2,1)S(1)} %get-tuple-element.65.normed_ref, bf16[768,3072]{1,0:T(8,128)(2,1)S(1)} %get-tuple-element.66.w_in_ref, ...), custom_call_target="tpu_custom_call" | custom-call | bytes 27000000 | tf_op jit(solution)/shard_map/pallas_call | solution.py:44
  45.6 0.0 collective-permute-done.6.refs_3_
  45.7 1.9 %shard_map.124 = (bf16[256,3072]{1,0:T(8,128)(2,1)S(1)}, bf16[128,768]{1,0:T(8,128)(2,1)S(1)}, bf16[256,768]{1,0:T(8,128)(2,1)S(1)}, f32[128,128]{1,0:T(8,128)S(1)}) custom-call(bf16[64,768]{1,0:T(8,128)(2,1)S(1)} %constant_dynamic-update-slice_fusion.2.refs_0_, bf16[64,768]{1,0:T(8,128)(2,1)S(1)} %collective-permute-done.4.refs_1_, ...), custom_call_target="tpu_custom_call" | custom-call | bytes 12000000 | tf_op jit(solution)/shard_map/pallas_call | solution.py:44
  47.6 0.1 collective-permute-start.10
  47.6 0.5 collective-permute-start.12
  48.1 0.1 collective-permute-start.11
  48.2 0.4 collective-permute-start.13
  48.6 3.2 %collective-permute-done.11.normed_other_ref = bf16[256,384]{1,0:T(8,128)(2,1)S(1)} collective-permute-done((bf16[256,384]{1,0:T(8,128)(2,1)S(1)}, bf16[256,384]{1,0:T(8,128)(2,1)S(1)}, u32[]{:S(2)}, u32[]{:S(2)}) %collective-permute-start.11) | collective-permute-done | bytes 196640 | tf_op jit(solution)/shard_map/ppermute | solution.py:65
  51.9 0.3 collective-permute-done.13.s_got_ref
  52.2 2.1 %shard_map.125 = (f32[16,232,256]{2,1,0:T(8,128)S(1)}, bf16[8,240,256]{2,1,0:T(8,128)(2,1)S(1)}, f32[16,232,128]{2,1,0:T(8,128)S(1)}, bf16[8,240,128]{2,1,0:T(8,128)(2,1)S(1)}) custom-call(bf16[256,3072]{1,0:T(8,128)(2,1)S(1)} %get-tuple-element.68.own_ref.g_in_ref, bf16[256,3072]{1,0:T(8,128)(2,1)S(1)} %collective-permute-done.10.other_ref, ...), custom_call_target="tpu_custom_call" | custom-call | bytes 15000000 | tf_op jit(solution)/shard_map/pallas_call | solution.py:44
  54.2 2.0 %collective-permute-start.14 = (bf16[8,240,256]{2,1,0:T(8,128)(2,1)S(1)}, bf16[8,240,256]{2,1,0:T(8,128)(2,1)S(1)}, u32[]{:S(2)}, u32[]{:S(2)}) collective-permute-start(bf16[8,240,256]{2,1,0:T(8,128)(2,1)S(1)} %get-tuple-element.75), channel_id=1, source_target_pairs={{0,4},{1,9},{2,6},{3,11},{4,0},{5,13},{6,2},{7,15},{8,12},{9,1},{1... | collective-permute-start | bytes 2949128 | tf_op jit(solution)/shard_map/ppermute | solution.py:65
  56.2 1.6 %shard_map.129 = (f32[256,768]{1,0:T(8,128)S(1)}, bf16[256,768]{1,0:T(8,128)(2,1)S(1)}) custom-call(bf16[256,3072]{1,0:T(8,128)(2,1)S(1)} %get-tuple-element.68.own_ref.g_in_ref, bf16[768,3072]{1,0:T(8,128)(2,1)S(1)} %get-tuple-element.66.w_in_ref, f32[256,768]{1,0:T(8,128)S(1)} %get-tuple-element.86.full_ref, f32[256,128]{1,0:T(8,128)S(1)} %get-tuple-element.87.inv_ref), custom_call_target="tpu_custom_call" | custom-call | bytes 12000000 | tf_op jit(solution)/shard_map/pallas_call | solution.py:44
  57.8 0.1 collective-permute-start.25
  57.9 0.5 collective-permute-start.18
  58.4 5.6 %shard_map.130 = (f32[32,768]{1,0:T(8,128)S(1)}, f32[32,768]{1,0:T(8,128)S(1)}) custom-call(f32[4,80,768]{2,1,0:T(8,128)S(1)} %get-tuple-element.84.pad_ref, f32[6,80,768]{2,1,0:T(8,128)S(1)} %get-tuple-element.85.edge_ref, f32[256,768]{1,0:T(8,128)S(1)} %get-tuple-element.88.dconv_ref.refs_0_), custom_call_target="tpu_custom_call" | custom-call | bytes 15000000 | tf_op jit(solution)/shard_map/pallas_call | solution.py:44
  64.0 0.2 collective-permute-start.19
  64.3 0.7 collective-permute-start.26
  65.0 3.4 %collective-permute-done.14.got_ref = bf16[8,240,256]{2,1,0:T(8,128)(2,1)S(1)} collective-permute-done((bf16[8,240,256]{2,1,0:T(8,128)(2,1)S(1)}, bf16[8,240,256]{2,1,0:T(8,128)(2,1)S(1)}, u32[]{:S(2)}, u32[]{:S(2)}) %collective-permute-start.14) | collective-permute-done | bytes 983072 | tf_op jit(solution)/shard_map/ppermute | solution.py:65
  68.4 0.2 shard_map.126
  68.6 0.7 collective-permute-start.15
  69.3 2.0 %collective-permute-start.20 = (f32[32,768]{1,0:T(8,128)S(1)}, f32[32,768]{1,0:T(8,128)S(1)}, u32[]{:S(2)}, u32[]{:S(2)}) collective-permute-start(f32[32,768]{1,0:T(8,128)S(1)} %add.3.taps_ref), channel_id=1, source_target_pairs={{0,2},{1,3},{2,0},{3,1},{4,6},{5,7},{6,4},{7,5},{8,10},{9,11},{10,... | collective-permute-start | bytes 294920 | tf_op jit(solution)/shard_map/ppermute | solution.py:65
  71.3 15.0 %collective-permute-done.20.taps_got_ref = f32[32,768]{1,0:T(8,128)S(1)} collective-permute-done((f32[32,768]{1,0:T(8,128)S(1)}, f32[32,768]{1,0:T(8,128)S(1)}, u32[]{:S(2)}, u32[]{:S(2)}) %collective-permute-start.20) | collective-permute-done | bytes 98336 | tf_op jit(solution)/shard_map/ppermute | solution.py:65
  86.3 0.0 collective-permute-done.18
  86.3 0.2 shard_map.131
  86.4 0.1 collective-permute-start.21
  86.5 7.2 %collective-permute-done.21.got_ref = bf16[1344,128]{1,0:T(8,128)(2,1)S(1)} collective-permute-done((bf16[1344,128]{1,0:T(8,128)(2,1)S(1)}, bf16[1344,128]{1,0:T(8,128)(2,1)S(1)}, u32[]{:S(2)}, u32[]{:S(2)}) %collective-permute-start.21) | collective-permute-done | bytes 344096 | tf_op jit(solution)/shard_map/ppermute | solution.py:65
  93.7 0.1 shard_map.132
  93.8 0.6 collective-permute-start.22
  94.4 0.0 collective-permute-done.15.got_ref
  94.4 0.1 shard_map.127
  94.6 0.2 collective-permute-start.16
  94.8 2.4 %collective-permute-start.27 = (bf16[3,128,768]{2,1,0:T(8,128)(2,1)S(1)}, bf16[3,128,768]{2,1,0:T(8,128)(2,1)S(1)}, u32[]{:S(2)}, u32[]{:S(2)}) collective-permute-start(bf16[3,128,768]{2,1,0:T(8,128)(2,1)S(1)} %collective-permute-done.26.near_ref), channel_id=1, source_target_pairs={{0,1},{1,0},{2,3},{3,2},{4,5},{5,4},{6,7},{7,6},{8,9},{9,8},{10,11... | collective-permute-start | bytes 1769480 | tf_op jit(solution)/shard_map/ppermute | solution.py:65
  97.2 2.6 %collective-permute-done.22.got_ref = bf16[864,128]{1,0:T(8,128)(2,1)S(1)} collective-permute-done((bf16[864,128]{1,0:T(8,128)(2,1)S(1)}, bf16[864,128]{1,0:T(8,128)(2,1)S(1)}, u32[]{:S(2)}, u32[]{:S(2)}) %collective-permute-start.22) | collective-permute-done | bytes 221216 | tf_op jit(solution)/shard_map/ppermute | solution.py:65
  99.8 0.1 shard_map.133
  99.9 0.4 collective-permute-start.23
  100.3 0.6 collective-permute-done.16.got_ref
  100.8 0.1 shard_map.128
  100.9 2.1 %collective-permute-start.17 = (bf16[1,240,256]{2,1,0:T(8,128)(2,1)S(1)}, bf16[1,240,256]{2,1,0:T(8,128)(2,1)S(1)}, u32[]{:S(2)}, u32[]{:S(2)}) collective-permute-start(bf16[1,240,256]{2,1,0:T(8,128)(2,1)S(1)} %get-tuple-element.81), channel_id=1, source_target_pairs={{0,16},{1,3},{2,18},{3,1},{4,20},{5,7},{6,22},{7,5},{8,24},{9,11},... | collective-permute-start | bytes 368648 | tf_op jit(solution)/shard_map/ppermute | solution.py:65
  103.0 6.4 %collective-permute-done.23.refs_3_ = bf16[624,128]{1,0:T(8,128)(2,1)S(1)} collective-permute-done((bf16[624,128]{1,0:T(8,128)(2,1)S(1)}, bf16[624,128]{1,0:T(8,128)(2,1)S(1)}, u32[]{:S(2)}, u32[]{:S(2)}) %collective-permute-start.23) | collective-permute-done | bytes 159776 | tf_op jit(solution)/shard_map/ppermute | solution.py:65
  109.4 1.3 %collective-permute-done.17.refs_1_ = bf16[1,240,256]{2,1,0:T(8,128)(2,1)S(1)} collective-permute-done((bf16[1,240,256]{2,1,0:T(8,128)(2,1)S(1)}, bf16[1,240,256]{2,1,0:T(8,128)(2,1)S(1)}, u32[]{:S(2)}, u32[]{:S(2)}) %collective-permute-start.17) | collective-permute-done | bytes 122912 | tf_op jit(solution)/shard_map/ppermute | solution.py:65
  110.7 0.9 shard_map.134
  111.7 2.5 %collective-permute-start.24 = (f32[168,384]{1,0:T(8,128)S(1)}, f32[168,384]{1,0:T(8,128)S(1)}, u32[]{:S(2)}, u32[]{:S(2)}) collective-permute-start(f32[168,384]{1,0:T(8,128)S(1)} %get-tuple-element.103), channel_id=1, source_target_pairs={{0,1},{1,0},{2,3},{3,2},{4,5},{5,4},{6,7},{7,6},{8,9},{9,8},{10,11... | collective-permute-start | bytes 774152 | tf_op jit(solution)/shard_map/ppermute | solution.py:65
  114.2 3.7 %shard_map.137 = (f32[4,80,768]{2,1,0:T(8,128)}, f32[256,768]{1,0:T(8,128)S(1)}) custom-call(f32[256,768]{1,0:T(8,128)S(1)} %get-tuple-element.88.dconv_ref.refs_0_, bf16[4,64,768]{2,1,0:T(8,128)(2,1)S(1)} %collective-permute-done.25.other_ref.refs_1_, f32[49,768]{1,0:T(8,128)S(1)} %get-tuple-element.62.refs_2_.taps_ref), custom_call_target="tpu_custom_call" | custom-call | bytes 12000000 | tf_op jit(solution)/shard_map/pallas_call | solution.py:44
  117.9 3.5 %shard_map.138 = bf16[4,64,768]{2,1,0:T(8,128)(2,1)} custom-call(bf16[3,128,768]{2,1,0:T(8,128)(2,1)S(1)} %collective-permute-done.26.near_ref, bf16[3,128,768]{2,1,0:T(8,128)(2,1)S(1)} %collective-permute-done.27.far_ref, f32[49,768]{1,0:T(8,128)S(1)} %get-tuple-element.62.refs_2_.taps_ref, f32[256,768]{1,0:T(8,128)S(1)} %get-tuple-element.106.sum_ref, ...), custom_call_target="tpu_custom_call" | custom-call | bytes 9000000 | tf_op jit(solution)/shard_map/pallas_call | solution.py:44
  121.3 0.8 shard_map.135
  (18 shorter events, 0.1 us)
Async XLA Ops:
  0.6 2.4 %collective-permute-start.7 = (bf16[4,64,768]{2,1,0:T(8,128)(2,1)}, bf16[4,64,768]{2,1,0:T(8,128)(2,1)S(1)}, u32[]{:S(2)}, u32[]{:S(2)}) collective-permute-start(bf16[4,64,768]{2,1,0:T(8,128)(2,1)} %image_ref.1), channel_id=1, source_target_pairs={{0,1},{1,0},{2,3},{3,2},{4,5},{5,4},{6,7},{7,6},{8,9},{9,8},{10,11... | collective-permute-start | bytes 1179656 | tf_op jit(solution)/shard_map/ppermute | solution.py:65
  3.1 4.7 %collective-permute-start.8 = (bf16[3,128,768]{2,1,0:T(8,128)(2,1)S(1)}, bf16[3,128,768]{2,1,0:T(8,128)(2,1)S(1)}, u32[]{:S(2)}, u32[]{:S(2)}) collective-permute-start(bf16[3,128,768]{2,1,0:T(8,128)(2,1)S(1)} %shard_map.121), channel_id=1, source_target_pairs={{1,2},{2,1},{3,4},{4,3},{5,6},{6,5},{7,8},{8,7},{9,10},{10,9},{11,... | collective-permute-start | bytes 1769480 | tf_op jit(solution)/shard_map/ppermute | solution.py:78
  3.8 17.0 %collective-permute-start = (bf16[8,768]{1,0:T(8,128)(2,1)S(1)}, bf16[8,768]{1,0:T(8,128)(2,1)S(1)}, u32[]{:S(2)}, u32[]{:S(2)}) collective-permute-start(bf16[8,768]{1,0:T(8,128)(2,1)S(1)} %get-tuple-element.58), channel_id=1, source_target_pairs={{0,1},{1,0},{2,3},{3,2},{4,5},{5,4},{6,7},{7,6},{8,9},{9,8},{10,11... | collective-permute-start | bytes 36872 | tf_op jit(solution)/shard_map/ppermute | solution.py:65
  7.7 30.7 %collective-permute-start.9 = (bf16[3,128,768]{2,1,0:T(8,128)(2,1)S(1)}, bf16[3,128,768]{2,1,0:T(8,128)(2,1)S(1)}, u32[]{:S(2)}, u32[]{:S(2)}) collective-permute-start(bf16[3,128,768]{2,1,0:T(8,128)(2,1)S(1)} %collective-permute-done.8.near_ref), channel_id=1, source_target_pairs={{0,1},{1,0},{2,3},{3,2},{4,5},{5,4},{6,7},{7,6},{8,9},{9,8},{10,11... | collective-permute-start | bytes 1769480 | tf_op jit(solution)/shard_map/ppermute | solution.py:65
  20.8 5.1 %collective-permute-start.1 = (bf16[16,768]{1,0:T(8,128)(2,1)S(1)}, bf16[16,768]{1,0:T(8,128)(2,1)S(1)}, u32[]{:S(2)}, u32[]{:S(2)}) collective-permute-start(bf16[16,768]{1,0:T(8,128)(2,1)S(1)} %get-tuple-element.111), channel_id=1, source_target_pairs={{0,8},{1,9},{2,10},{3,11},{4,12},{5,13},{6,14},{7,15},{8,0},{9,1},... | collective-permute-start | bytes 73736 | tf_op jit(solution)/shard_map/ppermute | solution.py:65
  23.3 7.5 %collective-permute-start.3 = (bf16[16,768]{1,0:T(8,128)(2,1)S(1)}, bf16[16,768]{1,0:T(8,128)(2,1)S(1)}, u32[]{:S(2)}, u32[]{:S(2)}) collective-permute-start(bf16[16,768]{1,0:T(8,128)(2,1)S(1)} %get-tuple-element.111), channel_id=1, source_target_pairs={{0,24},{1,25},{2,26},{3,27},{4,28},{5,29},{6,30},{7,31},{8,16},{9,... | collective-permute-start | bytes 73736 | tf_op jit(solution)/shard_map/ppermute | solution.py:65
  25.8 5.0 %collective-permute-start.2 = (bf16[16,768]{1,0:T(8,128)(2,1)S(1)}, bf16[16,768]{1,0:T(8,128)(2,1)S(1)}, u32[]{:S(2)}, u32[]{:S(2)}) collective-permute-start(bf16[16,768]{1,0:T(8,128)(2,1)S(1)} %get-tuple-element.111), channel_id=1, source_target_pairs={{0,16},{1,17},{2,18},{3,19},{4,20},{5,21},{6,22},{7,23},{8,24},{9,... | collective-permute-start | bytes 73736 | tf_op jit(solution)/shard_map/ppermute | solution.py:65
  30.8 14.8 %collective-permute-start.6 = (bf16[64,768]{1,0:T(8,128)(2,1)S(1)}, bf16[64,768]{1,0:T(8,128)(2,1)S(1)}, u32[]{:S(2)}, u32[]{:S(2)}) collective-permute-start(bf16[64,768]{1,0:T(8,128)(2,1)S(1)} %constant_dynamic-update-slice_fusion.2.refs_0_), channel_id=1, source_target_pairs={{0,6},{1,7},{2,4},{3,5},{4,2},{5,3},{6,0},{7,1},{8,14},{9,15},{10,... | collective-permute-start | bytes 294920 | tf_op jit(solution)/shard_map/ppermute | solution.py:65
  32.8 12.8 %collective-permute-start.5 = (bf16[64,768]{1,0:T(8,128)(2,1)S(1)}, bf16[64,768]{1,0:T(8,128)(2,1)S(1)}, u32[]{:S(2)}, u32[]{:S(2)}) collective-permute-start(bf16[64,768]{1,0:T(8,128)(2,1)S(1)} %constant_dynamic-update-slice_fusion.2.refs_0_), channel_id=1, source_target_pairs={{0,4},{1,5},{2,6},{3,7},{4,0},{5,1},{6,2},{7,3},{8,12},{9,13},{10,... | collective-permute-start | bytes 294920 | tf_op jit(solution)/shard_map/ppermute | solution.py:65
  34.6 11.1 %collective-permute-start.4 = (bf16[64,768]{1,0:T(8,128)(2,1)S(1)}, bf16[64,768]{1,0:T(8,128)(2,1)S(1)}, u32[]{:S(2)}, u32[]{:S(2)}) collective-permute-start(bf16[64,768]{1,0:T(8,128)(2,1)S(1)} %constant_dynamic-update-slice_fusion.2.refs_0_), channel_id=1, source_target_pairs={{0,2},{1,3},{2,0},{3,1},{4,6},{5,7},{6,4},{7,5},{8,10},{9,11},{10,... | collective-permute-start | bytes 294920 | tf_op jit(solution)/shard_map/ppermute | solution.py:65
  47.6 4.6 %collective-permute-start.10 = (bf16[256,3072]{1,0:T(8,128)(2,1)S(1)}, bf16[256,3072]{1,0:T(8,128)(2,1)S(1)}, u32[]{:S(2)}, u32[]{:S(2)}) collective-permute-start(bf16[256,3072]{1,0:T(8,128)(2,1)S(1)} %get-tuple-element.68.own_ref.g_in_ref), channel_id=1, source_target_pairs={{0,1},{1,0},{2,3},{3,2},{4,5},{5,4},{6,7},{7,6},{8,9},{9,8},{10,11... | collective-permute-start | bytes 4718600 | tf_op jit(solution)/shard_map/ppermute | solution.py:65
  47.6 4.5 %collective-permute-start.12 = (bf16[16,32,384]{2,1,0:T(8,128)(2,1)S(1)}, bf16[16,32,384]{2,1,0:T(8,128)(2,1)S(1)}, u32[]{:S(2)}, u32[]{:S(2)}) collective-permute-start(bf16[16,32,384]{2,1,0:T(8,128)(2,1)S(1)} %get-tuple-element.71), channel_id=1, source_target_pairs={{0,1},{1,0},{2,3},{3,2},{4,5},{5,4},{6,7},{7,6},{8,9},{9,8},{10,11... | collective-permute-start | bytes 1179656 | tf_op jit(solution)/shard_map/ppermute | solution.py:65
  48.1 3.7 %collective-permute-start.11 = (bf16[256,384]{1,0:T(8,128)(2,1)S(1)}, bf16[256,384]{1,0:T(8,128)(2,1)S(1)}, u32[]{:S(2)}, u32[]{:S(2)}) collective-permute-start(bf16[256,384]{1,0:T(8,128)(2,1)S(1)} %get-tuple-element.69), channel_id=1, source_target_pairs={{0,1},{1,0},{2,3},{3,2},{4,5},{5,4},{6,7},{7,6},{8,9},{9,8},{10,11... | collective-permute-start | bytes 589832 | tf_op jit(solution)/shard_map/ppermute | solution.py:65
  48.2 3.9 %collective-permute-start.13 = (f32[128,384]{1,0:T(8,128)S(1)}, f32[128,384]{1,0:T(8,128)S(1)}, u32[]{:S(2)}, u32[]{:S(2)}) collective-permute-start(f32[128,384]{1,0:T(8,128)S(1)} %get-tuple-element.73), channel_id=1, source_target_pairs={{0,1},{1,0},{2,3},{3,2},{4,5},{5,4},{6,7},{7,6},{8,9},{9,8},{10,11... | collective-permute-start | bytes 589832 | tf_op jit(solution)/shard_map/ppermute | solution.py:65
  54.2 14.2 %collective-permute-start.14 = (bf16[8,240,256]{2,1,0:T(8,128)(2,1)S(1)}, bf16[8,240,256]{2,1,0:T(8,128)(2,1)S(1)}, u32[]{:S(2)}, u32[]{:S(2)}) collective-permute-start(bf16[8,240,256]{2,1,0:T(8,128)(2,1)S(1)} %get-tuple-element.75), channel_id=1, source_target_pairs={{0,4},{1,9},{2,6},{3,11},{4,0},{5,13},{6,2},{7,15},{8,12},{9,1},{1... | collective-permute-start | bytes 2949128 | tf_op jit(solution)/shard_map/ppermute | solution.py:65
  57.8 6.4 %collective-permute-start.25 = (bf16[4,64,768]{2,1,0:T(8,128)(2,1)S(1)}, bf16[4,64,768]{2,1,0:T(8,128)(2,1)S(1)}, u32[]{:S(2)}, u32[]{:S(2)}) collective-permute-start(bf16[4,64,768]{2,1,0:T(8,128)(2,1)S(1)} %bitcast.7), channel_id=1, source_target_pairs={{0,1},{1,0},{2,3},{3,2},{4,5},{5,4},{6,7},{7,6},{8,9},{9,8},{10,11... | collective-permute-start | bytes 1179656 | tf_op jit(solution)/shard_map/ppermute | solution.py:65
  57.9 28.4 %collective-permute-start.18 = (bf16[8,240,128]{2,1,0:T(8,128)(2,1)S(1)}, bf16[8,240,128]{2,1,0:T(8,128)(2,1)S(1)}, u32[]{:S(2)}, u32[]{:S(2)}) collective-permute-start(bf16[8,240,128]{2,1,0:T(8,128)(2,1)S(1)} %get-tuple-element.83), channel_id=1, source_target_pairs={{0,2},{1,3},{2,0},{3,1},{4,6},{5,7},{6,4},{7,5},{8,10},{9,11},{10,... | collective-permute-start | bytes 1474568 | tf_op jit(solution)/shard_map/ppermute | solution.py:65
  64.0 5.3 %collective-permute-start.19 = (f32[32,768]{1,0:T(8,128)S(1)}, f32[32,768]{1,0:T(8,128)S(1)}, u32[]{:S(2)}, u32[]{:S(2)}) collective-permute-start(f32[32,768]{1,0:T(8,128)S(1)} %get-tuple-element.90), channel_id=1, source_target_pairs={{0,1},{1,0},{2,3},{3,2},{4,5},{5,4},{6,7},{7,6},{8,9},{9,8},{10,11... | collective-permute-start | bytes 294920 | tf_op jit(solution)/shard_map/ppermute | solution.py:65
  64.3 30.5 %collective-permute-start.26 = (bf16[3,128,768]{2,1,0:T(8,128)(2,1)S(1)}, bf16[3,128,768]{2,1,0:T(8,128)(2,1)S(1)}, u32[]{:S(2)}, u32[]{:S(2)}) collective-permute-start(bf16[3,128,768]{2,1,0:T(8,128)(2,1)S(1)} %shard_map.136), channel_id=1, source_target_pairs={{1,2},{2,1},{3,4},{4,3},{5,6},{6,5},{7,8},{8,7},{9,10},{10,9},{11,... | collective-permute-start | bytes 1769480 | tf_op jit(solution)/shard_map/ppermute | solution.py:78
  68.6 25.8 %collective-permute-start.15 = (bf16[4,240,256]{2,1,0:T(8,128)(2,1)S(1)}, bf16[4,240,256]{2,1,0:T(8,128)(2,1)S(1)}, u32[]{:S(2)}, u32[]{:S(2)}) collective-permute-start(bf16[4,240,256]{2,1,0:T(8,128)(2,1)S(1)} %get-tuple-element.77), channel_id=1, source_target_pairs={{0,8},{1,5},{2,10},{3,7},{4,12},{5,1},{6,14},{7,3},{8,0},{9,13},{1... | collective-permute-start | bytes 1474568 | tf_op jit(solution)/shard_map/ppermute | solution.py:65
  69.3 16.9 %collective-permute-start.20 = (f32[32,768]{1,0:T(8,128)S(1)}, f32[32,768]{1,0:T(8,128)S(1)}, u32[]{:S(2)}, u32[]{:S(2)}) collective-permute-start(f32[32,768]{1,0:T(8,128)S(1)} %add.3.taps_ref), channel_id=1, source_target_pairs={{0,2},{1,3},{2,0},{3,1},{4,6},{5,7},{6,4},{7,5},{8,10},{9,11},{10,... | collective-permute-start | bytes 294920 | tf_op jit(solution)/shard_map/ppermute | solution.py:65
  86.4 7.3 %collective-permute-start.21 = (bf16[1344,128]{1,0:T(8,128)(2,1)S(1)}, bf16[1344,128]{1,0:T(8,128)(2,1)S(1)}, u32[]{:S(2)}, u32[]{:S(2)}) collective-permute-start(bf16[1344,128]{1,0:T(8,128)(2,1)S(1)} %get-tuple-element.92), channel_id=1, source_target_pairs={{0,4},{1,17},{2,6},{3,19},{4,0},{5,21},{6,2},{7,23},{8,12},{9,25},... | collective-permute-start | bytes 1032200 | tf_op jit(solution)/shard_map/ppermute | solution.py:65
  93.8 6.0 %collective-permute-start.22 = (bf16[864,128]{1,0:T(8,128)(2,1)S(1)}, bf16[864,128]{1,0:T(8,128)(2,1)S(1)}, u32[]{:S(2)}, u32[]{:S(2)}) collective-permute-start(bf16[864,128]{1,0:T(8,128)(2,1)S(1)} %get-tuple-element.95), channel_id=1, source_target_pairs={{0,8},{1,5},{2,10},{3,7},{4,12},{5,1},{6,14},{7,3},{8,0},{9,13},{1... | collective-permute-start | bytes 663560 | tf_op jit(solution)/shard_map/ppermute | solution.py:65
  94.6 6.3 %collective-permute-start.16 = (bf16[2,240,256]{2,1,0:T(8,128)(2,1)S(1)}, bf16[2,240,256]{2,1,0:T(8,128)(2,1)S(1)}, u32[]{:S(2)}, u32[]{:S(2)}) collective-permute-start(bf16[2,240,256]{2,1,0:T(8,128)(2,1)S(1)} %get-tuple-element.79), channel_id=1, source_target_pairs={{0,2},{1,17},{2,0},{3,19},{4,6},{5,21},{6,4},{7,23},{8,10},{9,25},... | collective-permute-start | bytes 737288 | tf_op jit(solution)/shard_map/ppermute | solution.py:65
  94.8 23.1 %collective-permute-start.27 = (bf16[3,128,768]{2,1,0:T(8,128)(2,1)S(1)}, bf16[3,128,768]{2,1,0:T(8,128)(2,1)S(1)}, u32[]{:S(2)}, u32[]{:S(2)}) collective-permute-start(bf16[3,128,768]{2,1,0:T(8,128)(2,1)S(1)} %collective-permute-done.26.near_ref), channel_id=1, source_target_pairs={{0,1},{1,0},{2,3},{3,2},{4,5},{5,4},{6,7},{7,6},{8,9},{9,8},{10,11... | collective-permute-start | bytes 1769480 | tf_op jit(solution)/shard_map/ppermute | solution.py:65
  99.9 9.5 %collective-permute-start.23 = (bf16[624,128]{1,0:T(8,128)(2,1)S(1)}, bf16[624,128]{1,0:T(8,128)(2,1)S(1)}, u32[]{:S(2)}, u32[]{:S(2)}) collective-permute-start(bf16[624,128]{1,0:T(8,128)(2,1)S(1)} %get-tuple-element.98), channel_id=1, source_target_pairs={{0,16},{1,9},{2,18},{3,11},{4,20},{5,13},{6,22},{7,15},{8,24},{9,1... | collective-permute-start | bytes 479240 | tf_op jit(solution)/shard_map/ppermute | solution.py:65
  100.9 9.8 %collective-permute-start.17 = (bf16[1,240,256]{2,1,0:T(8,128)(2,1)S(1)}, bf16[1,240,256]{2,1,0:T(8,128)(2,1)S(1)}, u32[]{:S(2)}, u32[]{:S(2)}) collective-permute-start(bf16[1,240,256]{2,1,0:T(8,128)(2,1)S(1)} %get-tuple-element.81), channel_id=1, source_target_pairs={{0,16},{1,3},{2,18},{3,1},{4,20},{5,7},{6,22},{7,5},{8,24},{9,11},... | collective-permute-start | bytes 368648 | tf_op jit(solution)/shard_map/ppermute | solution.py:65
  111.7 9.7 %collective-permute-start.24 = (f32[168,384]{1,0:T(8,128)S(1)}, f32[168,384]{1,0:T(8,128)S(1)}, u32[]{:S(2)}, u32[]{:S(2)}) collective-permute-start(f32[168,384]{1,0:T(8,128)S(1)} %get-tuple-element.103), channel_id=1, source_target_pairs={{0,1},{1,0},{2,3},{3,2},{4,5},{5,4},{6,7},{7,6},{8,9},{9,8},{10,11... | collective-permute-start | bytes 774152 | tf_op jit(solution)/shard_map/ppermute | solution.py:65

commit v3 on v2

--- a/solution.py
+++ b/solution.py
@@ -476,7 +476,9 @@
         pltpu.VMEM((places, width), BF16),
         pltpu.VMEM((4 * known[0].shape[0], width), BF16),
     ]
-    return call(backward_body, outs, 4.0, scratch)(*known, slot, scale, w_out, slope)
+    return call(backward_body, outs, 4.0, scratch)(
+        *known, slot, scale, w_out, slope
+    )
 
 
 def norm_backward_body(g_in_ref, w_in_ref, full_ref, inv_ref, dconv_ref, narrow_ref):
@@ -610,9 +612,7 @@
 
 
 def taps_received(got_ref, first, count):
-    rows = (got_ref.shape[0] - first) // 2
-    high = got_ref[first : first + rows, :].astype(F32)
-    return rows_to_taps(high + got_ref[first + rows :, :].astype(F32), count)
+    return rows_to_taps(got_ref[first:, :].astype(F32), count)
 
 
 def tapped_round_body(
@@ -645,12 +645,8 @@
         taps = taps_ref[...] + taps_received(got_ref, 2 * left * height, count)
     else:
         taps = taps_ref[...] + taps_got_ref[...]
-    high, low = split_high_low(taps)
-    taps_out_ref[...] = high.astype(F32) + low.astype(F32)
-    rows = taps_to_rows(taps).shape[0]
-    high, low = split_high_low(taps_to_rows(taps))
-    send_ref[left * height : left * height + rows, :] = high
-    send_ref[left * height + rows :, :] = low
+    taps_out_ref[...] = taps.astype(BF16).astype(F32)
+    send_ref[left * height :, :] = taps_to_rows(taps).astype(BF16)
     lax.fori_loop(0, left, near, 0)
 
 
@@ -659,7 +655,7 @@
     rows = taps.size // wide
     outs = [
         ((left, height, wide), F32),
-        ((left * (height + per) + 2 * rows, wide), BF16),
+        ((left * (height + per) + rows, wide), BF16),
         (taps.shape, F32),
     ]
     carried = taps_got is None

time: 122 us -> 121 us (level)
  waiting for transfers between devices: 45 us -> 39.3 us
  starting transfers between devices: 42.7 us -> 47 us
    ppermute x26, waiting for transfers between devices: 45 us -> 39.3 us  [exchange(): return lax.ppermute(value, AXES, pairs)]
    ppermute x26, starting transfers between devices: 41.3 us -> 45.4 us  [exchange(): return lax.ppermute(value, AXES, pairs)]
  transfers between devices with their start and end apart: 28 -> 28, of which waited for: 10 -> 11; matrix products, arithmetic and copies ran while one was open for 0% -> 0% of each run, Pallas kernels for 24% -> 24%
where the time goes in v3:
time: 121 us
  starting transfers between devices  47 us (39%)
  waiting for transfers between devices  39.3 us (32%)
  Pallas kernels  33.6 us (28%)
    ppermute x26, starting transfers between devices, exchange(): return lax.ppermute(value, AXES, pairs)  45.4 us
    ppermute x26, waiting for transfers between devices, exchange(): return lax.ppermute(value, AXES, pairs)  39.3 us
    pallas_call x20, Pallas kernels, run(): pl.pallas_call(body, in_specs=specs, out_specs=[VMEM] * len(outs), out_sh...  33.6 us
  transfers between devices with their start and end apart: 28, of which 11 were waited for; matrix products, arithmetic and copies ran while one was open for 0% of the time, Pallas kernels for 24%

profile of v3, /device:TPU:0, one launch (start us, length us, event | category | flops | bytes accessed | tf_op | source)
XLA Modules:
  0.0 120.8 jit_solution(4242346777573308680)
XLA Ops:
  0.6 0.6 collective-permute-start.7
  1.2 1.8 %shard_map.119 = (bf16[8,768]{1,0:T(8,128)(2,1)S(1)}, f32[256,1]{1,0:T(8,128)S(1)}, bf16[4,64,768]{2,1,0:T(8,128)(2,1)S(1)}, f32[49,768]{1,0:T(8,128)S(1)}, f32[1,768]{1,0:T(1,128)S(1)}) custom-call(s32[2,32]{1,0:T(2,128)} %ids_ref.1, s32[1,128]{1,0:T(1,128)} %bitcast.9, bf16[4,768]{1,0:T(4,128)(2,1)} %grad_ref.1, bf16[4,64,768]{2,1,0:T(8,128)(2,1)} %image_ref.1, ...), custom_call_target="tpu_custom_call" | custom-call | bytes 4500000 | tf_op jit(solution)/shard_map/pallas_call | solution.py:44
  3.0 0.0 collective-permute-done.7.refs_1_.other_ref
  3.0 0.1 shard_map.121
  3.1 0.7 collective-permute-start.8
  3.8 4.0 %collective-permute-start = (bf16[8,768]{1,0:T(8,128)(2,1)S(1)}, bf16[8,768]{1,0:T(8,128)(2,1)S(1)}, u32[]{:S(2)}, u32[]{:S(2)}) collective-permute-start(bf16[8,768]{1,0:T(8,128)(2,1)S(1)} %get-tuple-element.58), channel_id=1, source_target_pairs={{0,1},{1,0},{2,3},{3,2},{4,5},{5,4},{6,7},{7,6},{8,9},{9,8},{10,11... | collective-permute-start | bytes 36872 | tf_op jit(solution)/shard_map/ppermute | solution.py:65
  7.7 13.1 %collective-permute-start.9 = (bf16[3,128,768]{2,1,0:T(8,128)(2,1)S(1)}, bf16[3,128,768]{2,1,0:T(8,128)(2,1)S(1)}, u32[]{:S(2)}, u32[]{:S(2)}) collective-permute-start(bf16[3,128,768]{2,1,0:T(8,128)(2,1)S(1)} %collective-permute-done.8.near_ref), channel_id=1, source_target_pairs={{0,1},{1,0},{2,3},{3,2},{4,5},{5,4},{6,7},{7,6},{8,9},{9,8},{10,11... | collective-permute-start | bytes 1769480 | tf_op jit(solution)/shard_map/ppermute | solution.py:65
  20.8 0.0 collective-permute-done
  20.8 2.5 %collective-permute-start.1 = (bf16[16,768]{1,0:T(8,128)(2,1)S(1)}, bf16[16,768]{1,0:T(8,128)(2,1)S(1)}, u32[]{:S(2)}, u32[]{:S(2)}) collective-permute-start(bf16[16,768]{1,0:T(8,128)(2,1)S(1)} %get-tuple-element.111), channel_id=1, source_target_pairs={{0,8},{1,9},{2,10},{3,11},{4,12},{5,13},{6,14},{7,15},{8,0},{9,1},... | collective-permute-start | bytes 73736 | tf_op jit(solution)/shard_map/ppermute | solution.py:65
  23.3 2.5 %collective-permute-start.3 = (bf16[16,768]{1,0:T(8,128)(2,1)S(1)}, bf16[16,768]{1,0:T(8,128)(2,1)S(1)}, u32[]{:S(2)}, u32[]{:S(2)}) collective-permute-start(bf16[16,768]{1,0:T(8,128)(2,1)S(1)} %get-tuple-element.111), channel_id=1, source_target_pairs={{0,24},{1,25},{2,26},{3,27},{4,28},{5,29},{6,30},{7,31},{8,16},{9,... | collective-permute-start | bytes 73736 | tf_op jit(solution)/shard_map/ppermute | solution.py:65
  25.8 0.1 collective-permute-start.2
  25.9 0.0 collective-permute-done.1
  25.9 4.9 %collective-permute-done.2 = bf16[16,768]{1,0:T(8,128)(2,1)S(1)} collective-permute-done((bf16[16,768]{1,0:T(8,128)(2,1)S(1)}, bf16[16,768]{1,0:T(8,128)(2,1)S(1)}, u32[]{:S(2)}, u32[]{:S(2)}) %collective-permute-start.2) | collective-permute-done | bytes 24608 | tf_op jit(solution)/shard_map/ppermute | solution.py:65
  30.8 2.0 %collective-permute-start.6 = (bf16[64,768]{1,0:T(8,128)(2,1)S(1)}, bf16[64,768]{1,0:T(8,128)(2,1)S(1)}, u32[]{:S(2)}, u32[]{:S(2)}) collective-permute-start(bf16[64,768]{1,0:T(8,128)(2,1)S(1)} %constant_dynamic-update-slice_fusion.2.refs_0_), channel_id=1, source_target_pairs={{0,6},{1,7},{2,4},{3,5},{4,2},{5,3},{6,0},{7,1},{8,14},{9,15},{10,... | collective-permute-start | bytes 294920 | tf_op jit(solution)/shard_map/ppermute | solution.py:65
  32.8 1.8 %collective-permute-start.5 = (bf16[64,768]{1,0:T(8,128)(2,1)S(1)}, bf16[64,768]{1,0:T(8,128)(2,1)S(1)}, u32[]{:S(2)}, u32[]{:S(2)}) collective-permute-start(bf16[64,768]{1,0:T(8,128)(2,1)S(1)} %constant_dynamic-update-slice_fusion.2.refs_0_), channel_id=1, source_target_pairs={{0,4},{1,5},{2,6},{3,7},{4,0},{5,1},{6,2},{7,3},{8,12},{9,13},{10,... | collective-permute-start | bytes 294920 | tf_op jit(solution)/shard_map/ppermute | solution.py:65
  34.6 0.0 collective-permute-start.4
  34.6 3.8 %shard_map.120 = (f32[4,80,768]{2,1,0:T(8,128)S(1)}, f32[256,768]{1,0:T(8,128)S(1)}, bf16[768,3072]{1,0:T(8,128)(2,1)S(1)}, bf16[3072,768]{1,0:T(8,128)(2,1)S(1)}) custom-call(bf16[4,64,768]{2,1,0:T(8,128)(2,1)S(1)} %get-tuple-element.61.refs_0_.own_ref, bf16[4,64,768]{2,1,0:T(8,128)(2,1)S(1)} %collective-permute-done.7.refs_1_.other_ref, ...), custom_call_target="tpu_custom_call" | custom-call | bytes 12000000 | tf_op jit(solution)/shard_map/pallas_call | solution.py:44
  38.4 0.0 collective-permute-done.9.far_ref
  38.4 3.5 %shard_map.122 = (f32[6,80,768]{2,1,0:T(8,128)S(1)}, bf16[256,768]{1,0:T(8,128)(2,1)S(1)}, bf16[256,384]{1,0:T(8,128)(2,1)S(1)}, f32[256,768]{1,0:T(8,128)S(1)}, f32[256,128]{1,0:T(8,128)S(1)}) custom-call(bf16[3,128,768]{2,1,0:T(8,128)(2,1)S(1)} %collective-permute-done.8.near_ref, bf16[3,128,768]{2,1,0:T(8,128)(2,1)S(1)} %collective-permute-done.9.far_ref, ...), custom_call_target="tpu_custom_call" | custom-call | bytes 15000000 | tf_op jit(solution)/shard_map/pallas_call | solution.py:44
  41.9 3.7 %shard_map.123 = (f32[256,3072]{1,0:T(8,128)S(1)}, f32[16,32,384]{2,1,0:T(8,128)S(1)}, bf16[16,32,384]{2,1,0:T(8,128)(2,1)S(1)}, f32[128,384]{1,0:T(8,128)S(1)}, f32[128,384]{1,0:T(8,128)S(1)}) custom-call(bf16[256,768]{1,0:T(8,128)(2,1)S(1)} %get-tuple-element.65.normed_ref, bf16[768,3072]{1,0:T(8,128)(2,1)S(1)} %get-tuple-element.66.w_in_ref, ...), custom_call_target="tpu_custom_call" | custom-call | bytes 27000000 | tf_op jit(solution)/shard_map/pallas_call | solution.py:44
  45.6 0.0 collective-permute-done.6.refs_3_
  45.7 1.9 %shard_map.124 = (bf16[256,3072]{1,0:T(8,128)(2,1)S(1)}, bf16[128,768]{1,0:T(8,128)(2,1)S(1)}, bf16[256,768]{1,0:T(8,128)(2,1)S(1)}, f32[128,128]{1,0:T(8,128)S(1)}) custom-call(bf16[64,768]{1,0:T(8,128)(2,1)S(1)} %constant_dynamic-update-slice_fusion.2.refs_0_, bf16[64,768]{1,0:T(8,128)(2,1)S(1)} %collective-permute-done.4.refs_1_, ...), custom_call_target="tpu_custom_call" | custom-call | bytes 12000000 | tf_op jit(solution)/shard_map/pallas_call | solution.py:44
  47.6 0.1 collective-permute-start.10
  47.6 0.5 collective-permute-start.12
  48.1 0.1 collective-permute-start.11
  48.2 0.4 collective-permute-start.13
  48.6 3.2 %collective-permute-done.11.normed_other_ref = bf16[256,384]{1,0:T(8,128)(2,1)S(1)} collective-permute-done((bf16[256,384]{1,0:T(8,128)(2,1)S(1)}, bf16[256,384]{1,0:T(8,128)(2,1)S(1)}, u32[]{:S(2)}, u32[]{:S(2)}) %collective-permute-start.11) | collective-permute-done | bytes 196640 | tf_op jit(solution)/shard_map/ppermute | solution.py:65
  51.9 0.3 collective-permute-done.13.s_got_ref
  52.2 2.1 %shard_map.125 = (f32[16,232,256]{2,1,0:T(8,128)S(1)}, bf16[8,240,256]{2,1,0:T(8,128)(2,1)S(1)}, f32[16,232,128]{2,1,0:T(8,128)S(1)}, bf16[8,240,128]{2,1,0:T(8,128)(2,1)S(1)}) custom-call(bf16[256,3072]{1,0:T(8,128)(2,1)S(1)} %get-tuple-element.68.own_ref.g_in_ref, bf16[256,3072]{1,0:T(8,128)(2,1)S(1)} %collective-permute-done.10.other_ref, ...), custom_call_target="tpu_custom_call" | custom-call | bytes 15000000 | tf_op jit(solution)/shard_map/pallas_call | solution.py:44
  54.3 2.0 %collective-permute-start.14 = (bf16[8,240,256]{2,1,0:T(8,128)(2,1)S(1)}, bf16[8,240,256]{2,1,0:T(8,128)(2,1)S(1)}, u32[]{:S(2)}, u32[]{:S(2)}) collective-permute-start(bf16[8,240,256]{2,1,0:T(8,128)(2,1)S(1)} %get-tuple-element.75), channel_id=1, source_target_pairs={{0,4},{1,9},{2,6},{3,11},{4,0},{5,13},{6,2},{7,15},{8,12},{9,1},{1... | collective-permute-start | bytes 2949128 | tf_op jit(solution)/shard_map/ppermute | solution.py:65
  56.2 1.6 %shard_map.129 = (f32[256,768]{1,0:T(8,128)S(1)}, bf16[256,768]{1,0:T(8,128)(2,1)S(1)}) custom-call(bf16[256,3072]{1,0:T(8,128)(2,1)S(1)} %get-tuple-element.68.own_ref.g_in_ref, bf16[768,3072]{1,0:T(8,128)(2,1)S(1)} %get-tuple-element.66.w_in_ref, f32[256,768]{1,0:T(8,128)S(1)} %get-tuple-element.86.full_ref, f32[256,128]{1,0:T(8,128)S(1)} %get-tuple-element.87.inv_ref), custom_call_target="tpu_custom_call" | custom-call | bytes 12000000 | tf_op jit(solution)/shard_map/pallas_call | solution.py:44
  57.8 0.1 collective-permute-start.25
  57.9 0.4 collective-permute-start.18
  58.4 1.3 %collective-permute-done.25.other_ref.refs_1_ = bf16[4,64,768]{2,1,0:T(8,128)(2,1)S(1)} collective-permute-done((bf16[4,64,768]{2,1,0:T(8,128)(2,1)S(1)}, bf16[4,64,768]{2,1,0:T(8,128)(2,1)S(1)}, u32[]{:S(2)}, u32[]{:S(2)}) %collective-permute-start.25) | collective-permute-done | bytes 393248 | tf_op jit(solution)/shard_map/ppermute | solution.py:65
  59.7 0.9 collective-permute-start.26
  60.6 7.8 %collective-permute-done.14.got_ref = bf16[8,240,256]{2,1,0:T(8,128)(2,1)S(1)} collective-permute-done((bf16[8,240,256]{2,1,0:T(8,128)(2,1)S(1)}, bf16[8,240,256]{2,1,0:T(8,128)(2,1)S(1)}, u32[]{:S(2)}, u32[]{:S(2)}) %collective-permute-start.14) | collective-permute-done | bytes 983072 | tf_op jit(solution)/shard_map/ppermute | solution.py:65
  68.4 0.2 shard_map.126
  68.6 0.6 collective-permute-start.15
  69.2 5.6 %shard_map.130 = (f32[32,768]{1,0:T(8,128)S(1)}, f32[32,768]{1,0:T(8,128)S(1)}) custom-call(f32[4,80,768]{2,1,0:T(8,128)S(1)} %get-tuple-element.84.pad_ref, f32[6,80,768]{2,1,0:T(8,128)S(1)} %get-tuple-element.85.edge_ref, f32[256,768]{1,0:T(8,128)S(1)} %get-tuple-element.88.dconv_ref.refs_0_), custom_call_target="tpu_custom_call" | custom-call | bytes 15000000 | tf_op jit(solution)/shard_map/pallas_call | solution.py:44
  74.8 0.5 collective-permute-start.19
  75.4 0.9 collective-permute-done.19
  76.3 7.8 %collective-permute-start.20 = (f32[32,768]{1,0:T(8,128)S(1)}, f32[32,768]{1,0:T(8,128)S(1)}, u32[]{:S(2)}, u32[]{:S(2)}) collective-permute-start(f32[32,768]{1,0:T(8,128)S(1)} %add.3.taps_ref), channel_id=1, source_target_pairs={{0,2},{1,3},{2,0},{3,1},{4,6},{5,7},{6,4},{7,5},{8,10},{9,11},{10,... | collective-permute-start | bytes 294920 | tf_op jit(solution)/shard_map/ppermute | solution.py:65
  84.2 3.1 %collective-permute-done.20.taps_got_ref = f32[32,768]{1,0:T(8,128)S(1)} collective-permute-done((f32[32,768]{1,0:T(8,128)S(1)}, f32[32,768]{1,0:T(8,128)S(1)}, u32[]{:S(2)}, u32[]{:S(2)}) %collective-permute-start.20) | collective-permute-done | bytes 98336 | tf_op jit(solution)/shard_map/ppermute | solution.py:65
  87.3 0.0 collective-permute-done.18
  87.3 0.1 shard_map.131
  87.5 2.5 %collective-permute-start.21 = (bf16[1152,128]{1,0:T(8,128)(2,1)S(1)}, bf16[1152,128]{1,0:T(8,128)(2,1)S(1)}, u32[]{:S(2)}, u32[]{:S(2)}) collective-permute-start(bf16[1152,128]{1,0:T(8,128)(2,1)S(1)} %get-tuple-element.92), channel_id=1, source_target_pairs={{0,4},{1,17},{2,6},{3,19},{4,0},{5,21},{6,2},{7,23},{8,12},{9,25},... | collective-permute-start | bytes 884744 | tf_op jit(solution)/shard_map/ppermute | solution.py:65
  90.0 0.0 collective-permute-done.15.got_ref
  90.0 0.1 shard_map.127
  90.1 1.8 %collective-permute-start.16 = (bf16[2,240,256]{2,1,0:T(8,128)(2,1)S(1)}, bf16[2,240,256]{2,1,0:T(8,128)(2,1)S(1)}, u32[]{:S(2)}, u32[]{:S(2)}) collective-permute-start(bf16[2,240,256]{2,1,0:T(8,128)(2,1)S(1)} %get-tuple-element.79), channel_id=1, source_target_pairs={{0,2},{1,17},{2,0},{3,19},{4,6},{5,21},{6,4},{7,23},{8,10},{9,25},... | collective-permute-start | bytes 737288 | tf_op jit(solution)/shard_map/ppermute | solution.py:65
  91.9 2.8 %collective-permute-done.21.got_ref = bf16[1152,128]{1,0:T(8,128)(2,1)S(1)} collective-permute-done((bf16[1152,128]{1,0:T(8,128)(2,1)S(1)}, bf16[1152,128]{1,0:T(8,128)(2,1)S(1)}, u32[]{:S(2)}, u32[]{:S(2)}) %collective-permute-start.21) | collective-permute-done | bytes 294944 | tf_op jit(solution)/shard_map/ppermute | solution.py:65
  94.7 0.1 shard_map.132
  94.8 0.1 collective-permute-start.22
  94.9 1.5 %collective-permute-done.16.got_ref = bf16[2,240,256]{2,1,0:T(8,128)(2,1)S(1)} collective-permute-done((bf16[2,240,256]{2,1,0:T(8,128)(2,1)S(1)}, bf16[2,240,256]{2,1,0:T(8,128)(2,1)S(1)}, u32[]{:S(2)}, u32[]{:S(2)}) %collective-permute-start.16) | collective-permute-done | bytes 245792 | tf_op jit(solution)/shard_map/ppermute | solution.py:65
  96.4 1.6 %collective-permute-start.17 = (bf16[1,240,256]{2,1,0:T(8,128)(2,1)S(1)}, bf16[1,240,256]{2,1,0:T(8,128)(2,1)S(1)}, u32[]{:S(2)}, u32[]{:S(2)}) collective-permute-start(bf16[1,240,256]{2,1,0:T(8,128)(2,1)S(1)} %get-tuple-element.81), channel_id=1, source_target_pairs={{0,16},{1,3},{2,18},{3,1},{4,20},{5,7},{6,22},{7,5},{8,24},{9,11},... | collective-permute-start | bytes 368648 | tf_op jit(solution)/shard_map/ppermute | solution.py:65
  98.0 7.3 %collective-permute-done.22.got_ref = bf16[672,128]{1,0:T(8,128)(2,1)S(1)} collective-permute-done((bf16[672,128]{1,0:T(8,128)(2,1)S(1)}, bf16[672,128]{1,0:T(8,128)(2,1)S(1)}, u32[]{:S(2)}, u32[]{:S(2)}) %collective-permute-start.22) | collective-permute-done | bytes 172064 | tf_op jit(solution)/shard_map/ppermute | solution.py:65
  105.4 0.3 collective-permute-start.23
  105.7 6.1 %collective-permute-done.23.refs_3_ = bf16[432,128]{1,0:T(8,128)(2,1)S(1)} collective-permute-done((bf16[432,128]{1,0:T(8,128)(2,1)S(1)}, bf16[432,128]{1,0:T(8,128)(2,1)S(1)}, u32[]{:S(2)}, u32[]{:S(2)}) %collective-permute-start.23) | collective-permute-done | bytes 110624 | tf_op jit(solution)/shard_map/ppermute | solution.py:65
  111.9 0.0 collective-permute-done.17.refs_1_
  111.9 0.9 shard_map.134
  112.8 0.0 collective-permute-start.24
  112.8 3.7 %shard_map.137 = (f32[4,80,768]{2,1,0:T(8,128)}, f32[256,768]{1,0:T(8,128)S(1)}) custom-call(f32[256,768]{1,0:T(8,128)S(1)} %get-tuple-element.88.dconv_ref.refs_0_, bf16[4,64,768]{2,1,0:T(8,128)(2,1)S(1)} %collective-permute-done.25.other_ref.refs_1_, f32[49,768]{1,0:T(8,128)S(1)} %get-tuple-element.62.refs_2_.taps_ref), custom_call_target="tpu_custom_call" | custom-call | bytes 12000000 | tf_op jit(solution)/shard_map/pallas_call | solution.py:44
  116.5 0.0 collective-permute-done.27.far_ref
  116.5 3.5 %shard_map.138 = bf16[4,64,768]{2,1,0:T(8,128)(2,1)} custom-call(bf16[3,128,768]{2,1,0:T(8,128)(2,1)S(1)} %collective-permute-done.26.near_ref, bf16[3,128,768]{2,1,0:T(8,128)(2,1)S(1)} %collective-permute-done.27.far_ref, f32[49,768]{1,0:T(8,128)S(1)} %get-tuple-element.62.refs_2_.taps_ref, f32[256,768]{1,0:T(8,128)S(1)} %get-tuple-element.106.sum_ref, ...), custom_call_target="tpu_custom_call" | custom-call | bytes 9000000 | tf_op jit(solution)/shard_map/pallas_call | solution.py:44
  119.9 0.8 shard_map.135
  (18 shorter events, 0.2 us)
Async XLA Ops:
  0.6 2.4 %collective-permute-start.7 = (bf16[4,64,768]{2,1,0:T(8,128)(2,1)}, bf16[4,64,768]{2,1,0:T(8,128)(2,1)S(1)}, u32[]{:S(2)}, u32[]{:S(2)}) collective-permute-start(bf16[4,64,768]{2,1,0:T(8,128)(2,1)} %image_ref.1), channel_id=1, source_target_pairs={{0,1},{1,0},{2,3},{3,2},{4,5},{5,4},{6,7},{7,6},{8,9},{9,8},{10,11... | collective-permute-start | bytes 1179656 | tf_op jit(solution)/shard_map/ppermute | solution.py:65
  3.1 4.7 %collective-permute-start.8 = (bf16[3,128,768]{2,1,0:T(8,128)(2,1)S(1)}, bf16[3,128,768]{2,1,0:T(8,128)(2,1)S(1)}, u32[]{:S(2)}, u32[]{:S(2)}) collective-permute-start(bf16[3,128,768]{2,1,0:T(8,128)(2,1)S(1)} %shard_map.121), channel_id=1, source_target_pairs={{1,2},{2,1},{3,4},{4,3},{5,6},{6,5},{7,8},{8,7},{9,10},{10,9},{11,... | collective-permute-start | bytes 1769480 | tf_op jit(solution)/shard_map/ppermute | solution.py:78
  3.8 17.0 %collective-permute-start = (bf16[8,768]{1,0:T(8,128)(2,1)S(1)}, bf16[8,768]{1,0:T(8,128)(2,1)S(1)}, u32[]{:S(2)}, u32[]{:S(2)}) collective-permute-start(bf16[8,768]{1,0:T(8,128)(2,1)S(1)} %get-tuple-element.58), channel_id=1, source_target_pairs={{0,1},{1,0},{2,3},{3,2},{4,5},{5,4},{6,7},{7,6},{8,9},{9,8},{10,11... | collective-permute-start | bytes 36872 | tf_op jit(solution)/shard_map/ppermute | solution.py:65
  7.7 30.7 %collective-permute-start.9 = (bf16[3,128,768]{2,1,0:T(8,128)(2,1)S(1)}, bf16[3,128,768]{2,1,0:T(8,128)(2,1)S(1)}, u32[]{:S(2)}, u32[]{:S(2)}) collective-permute-start(bf16[3,128,768]{2,1,0:T(8,128)(2,1)S(1)} %collective-permute-done.8.near_ref), channel_id=1, source_target_pairs={{0,1},{1,0},{2,3},{3,2},{4,5},{5,4},{6,7},{7,6},{8,9},{9,8},{10,11... | collective-permute-start | bytes 1769480 | tf_op jit(solution)/shard_map/ppermute | solution.py:65
  20.8 5.1 %collective-permute-start.1 = (bf16[16,768]{1,0:T(8,128)(2,1)S(1)}, bf16[16,768]{1,0:T(8,128)(2,1)S(1)}, u32[]{:S(2)}, u32[]{:S(2)}) collective-permute-start(bf16[16,768]{1,0:T(8,128)(2,1)S(1)} %get-tuple-element.111), channel_id=1, source_target_pairs={{0,8},{1,9},{2,10},{3,11},{4,12},{5,13},{6,14},{7,15},{8,0},{9,1},... | collective-permute-start | bytes 73736 | tf_op jit(solution)/shard_map/ppermute | solution.py:65
  23.3 7.5 %collective-permute-start.3 = (bf16[16,768]{1,0:T(8,128)(2,1)S(1)}, bf16[16,768]{1,0:T(8,128)(2,1)S(1)}, u32[]{:S(2)}, u32[]{:S(2)}) collective-permute-start(bf16[16,768]{1,0:T(8,128)(2,1)S(1)} %get-tuple-element.111), channel_id=1, source_target_pairs={{0,24},{1,25},{2,26},{3,27},{4,28},{5,29},{6,30},{7,31},{8,16},{9,... | collective-permute-start | bytes 73736 | tf_op jit(solution)/shard_map/ppermute | solution.py:65
  25.8 5.0 %collective-permute-start.2 = (bf16[16,768]{1,0:T(8,128)(2,1)S(1)}, bf16[16,768]{1,0:T(8,128)(2,1)S(1)}, u32[]{:S(2)}, u32[]{:S(2)}) collective-permute-start(bf16[16,768]{1,0:T(8,128)(2,1)S(1)} %get-tuple-element.111), channel_id=1, source_target_pairs={{0,16},{1,17},{2,18},{3,19},{4,20},{5,21},{6,22},{7,23},{8,24},{9,... | collective-permute-start | bytes 73736 | tf_op jit(solution)/shard_map/ppermute | solution.py:65
  30.8 14.8 %collective-permute-start.6 = (bf16[64,768]{1,0:T(8,128)(2,1)S(1)}, bf16[64,768]{1,0:T(8,128)(2,1)S(1)}, u32[]{:S(2)}, u32[]{:S(2)}) collective-permute-start(bf16[64,768]{1,0:T(8,128)(2,1)S(1)} %constant_dynamic-update-slice_fusion.2.refs_0_), channel_id=1, source_target_pairs={{0,6},{1,7},{2,4},{3,5},{4,2},{5,3},{6,0},{7,1},{8,14},{9,15},{10,... | collective-permute-start | bytes 294920 | tf_op jit(solution)/shard_map/ppermute | solution.py:65
  32.8 12.8 %collective-permute-start.5 = (bf16[64,768]{1,0:T(8,128)(2,1)S(1)}, bf16[64,768]{1,0:T(8,128)(2,1)S(1)}, u32[]{:S(2)}, u32[]{:S(2)}) collective-permute-start(bf16[64,768]{1,0:T(8,128)(2,1)S(1)} %constant_dynamic-update-slice_fusion.2.refs_0_), channel_id=1, source_target_pairs={{0,4},{1,5},{2,6},{3,7},{4,0},{5,1},{6,2},{7,3},{8,12},{9,13},{10,... | collective-permute-start | bytes 294920 | tf_op jit(solution)/shard_map/ppermute | solution.py:65
  34.6 11.1 %collective-permute-start.4 = (bf16[64,768]{1,0:T(8,128)(2,1)S(1)}, bf16[64,768]{1,0:T(8,128)(2,1)S(1)}, u32[]{:S(2)}, u32[]{:S(2)}) collective-permute-start(bf16[64,768]{1,0:T(8,128)(2,1)S(1)} %constant_dynamic-update-slice_fusion.2.refs_0_), channel_id=1, source_target_pairs={{0,2},{1,3},{2,0},{3,1},{4,6},{5,7},{6,4},{7,5},{8,10},{9,11},{10,... | collective-permute-start | bytes 294920 | tf_op jit(solution)/shard_map/ppermute | solution.py:65
  47.6 4.6 %collective-permute-start.10 = (bf16[256,3072]{1,0:T(8,128)(2,1)S(1)}, bf16[256,3072]{1,0:T(8,128)(2,1)S(1)}, u32[]{:S(2)}, u32[]{:S(2)}) collective-permute-start(bf16[256,3072]{1,0:T(8,128)(2,1)S(1)} %get-tuple-element.68.own_ref.g_in_ref), channel_id=1, source_target_pairs={{0,1},{1,0},{2,3},{3,2},{4,5},{5,4},{6,7},{7,6},{8,9},{9,8},{10,11... | collective-permute-start | bytes 4718600 | tf_op jit(solution)/shard_map/ppermute | solution.py:65
  47.6 4.5 %collective-permute-start.12 = (bf16[16,32,384]{2,1,0:T(8,128)(2,1)S(1)}, bf16[16,32,384]{2,1,0:T(8,128)(2,1)S(1)}, u32[]{:S(2)}, u32[]{:S(2)}) collective-permute-start(bf16[16,32,384]{2,1,0:T(8,128)(2,1)S(1)} %get-tuple-element.71), channel_id=1, source_target_pairs={{0,1},{1,0},{2,3},{3,2},{4,5},{5,4},{6,7},{7,6},{8,9},{9,8},{10,11... | collective-permute-start | bytes 1179656 | tf_op jit(solution)/shard_map/ppermute | solution.py:65
  48.1 3.7 %collective-permute-start.11 = (bf16[256,384]{1,0:T(8,128)(2,1)S(1)}, bf16[256,384]{1,0:T(8,128)(2,1)S(1)}, u32[]{:S(2)}, u32[]{:S(2)}) collective-permute-start(bf16[256,384]{1,0:T(8,128)(2,1)S(1)} %get-tuple-element.69), channel_id=1, source_target_pairs={{0,1},{1,0},{2,3},{3,2},{4,5},{5,4},{6,7},{7,6},{8,9},{9,8},{10,11... | collective-permute-start | bytes 589832 | tf_op jit(solution)/shard_map/ppermute | solution.py:65
  48.2 3.9 %collective-permute-start.13 = (f32[128,384]{1,0:T(8,128)S(1)}, f32[128,384]{1,0:T(8,128)S(1)}, u32[]{:S(2)}, u32[]{:S(2)}) collective-permute-start(f32[128,384]{1,0:T(8,128)S(1)} %get-tuple-element.73), channel_id=1, source_target_pairs={{0,1},{1,0},{2,3},{3,2},{4,5},{5,4},{6,7},{7,6},{8,9},{9,8},{10,11... | collective-permute-start | bytes 589832 | tf_op jit(solution)/shard_map/ppermute | solution.py:65
  54.3 14.2 %collective-permute-start.14 = (bf16[8,240,256]{2,1,0:T(8,128)(2,1)S(1)}, bf16[8,240,256]{2,1,0:T(8,128)(2,1)S(1)}, u32[]{:S(2)}, u32[]{:S(2)}) collective-permute-start(bf16[8,240,256]{2,1,0:T(8,128)(2,1)S(1)} %get-tuple-element.75), channel_id=1, source_target_pairs={{0,4},{1,9},{2,6},{3,11},{4,0},{5,13},{6,2},{7,15},{8,12},{9,1},{1... | collective-permute-start | bytes 2949128 | tf_op jit(solution)/shard_map/ppermute | solution.py:65
  57.8 1.8 %collective-permute-start.25 = (bf16[4,64,768]{2,1,0:T(8,128)(2,1)S(1)}, bf16[4,64,768]{2,1,0:T(8,128)(2,1)S(1)}, u32[]{:S(2)}, u32[]{:S(2)}) collective-permute-start(bf16[4,64,768]{2,1,0:T(8,128)(2,1)S(1)} %bitcast.7), channel_id=1, source_target_pairs={{0,1},{1,0},{2,3},{3,2},{4,5},{5,4},{6,7},{7,6},{8,9},{9,8},{10,11... | collective-permute-start | bytes 1179656 | tf_op jit(solution)/shard_map/ppermute | solution.py:65
  57.9 29.4 %collective-permute-start.18 = (bf16[8,240,128]{2,1,0:T(8,128)(2,1)S(1)}, bf16[8,240,128]{2,1,0:T(8,128)(2,1)S(1)}, u32[]{:S(2)}, u32[]{:S(2)}) collective-permute-start(bf16[8,240,128]{2,1,0:T(8,128)(2,1)S(1)} %get-tuple-element.83), channel_id=1, source_target_pairs={{0,2},{1,3},{2,0},{3,1},{4,6},{5,7},{6,4},{7,5},{8,10},{9,11},{10,... | collective-permute-start | bytes 1474568 | tf_op jit(solution)/shard_map/ppermute | solution.py:65
  59.7 32.2 %collective-permute-start.26 = (bf16[3,128,768]{2,1,0:T(8,128)(2,1)S(1)}, bf16[3,128,768]{2,1,0:T(8,128)(2,1)S(1)}, u32[]{:S(2)}, u32[]{:S(2)}) collective-permute-start(bf16[3,128,768]{2,1,0:T(8,128)(2,1)S(1)} %shard_map.136), channel_id=1, source_target_pairs={{1,2},{2,1},{3,4},{4,3},{5,6},{6,5},{7,8},{8,7},{9,10},{10,9},{11,... | collective-permute-start | bytes 1769480 | tf_op jit(solution)/shard_map/ppermute | solution.py:78
  68.6 21.4 %collective-permute-start.15 = (bf16[4,240,256]{2,1,0:T(8,128)(2,1)S(1)}, bf16[4,240,256]{2,1,0:T(8,128)(2,1)S(1)}, u32[]{:S(2)}, u32[]{:S(2)}) collective-permute-start(bf16[4,240,256]{2,1,0:T(8,128)(2,1)S(1)} %get-tuple-element.77), channel_id=1, source_target_pairs={{0,8},{1,5},{2,10},{3,7},{4,12},{5,1},{6,14},{7,3},{8,0},{9,13},{1... | collective-permute-start | bytes 1474568 | tf_op jit(solution)/shard_map/ppermute | solution.py:65
  74.8 1.5 %collective-permute-start.19 = (f32[32,768]{1,0:T(8,128)S(1)}, f32[32,768]{1,0:T(8,128)S(1)}, u32[]{:S(2)}, u32[]{:S(2)}) collective-permute-start(f32[32,768]{1,0:T(8,128)S(1)} %get-tuple-element.90), channel_id=1, source_target_pairs={{0,1},{1,0},{2,3},{3,2},{4,5},{5,4},{6,7},{7,6},{8,9},{9,8},{10,11... | collective-permute-start | bytes 294920 | tf_op jit(solution)/shard_map/ppermute | solution.py:65
  76.3 11.0 %collective-permute-start.20 = (f32[32,768]{1,0:T(8,128)S(1)}, f32[32,768]{1,0:T(8,128)S(1)}, u32[]{:S(2)}, u32[]{:S(2)}) collective-permute-start(f32[32,768]{1,0:T(8,128)S(1)} %add.3.taps_ref), channel_id=1, source_target_pairs={{0,2},{1,3},{2,0},{3,1},{4,6},{5,7},{6,4},{7,5},{8,10},{9,11},{10,... | collective-permute-start | bytes 294920 | tf_op jit(solution)/shard_map/ppermute | solution.py:65
  87.5 7.2 %collective-permute-start.21 = (bf16[1152,128]{1,0:T(8,128)(2,1)S(1)}, bf16[1152,128]{1,0:T(8,128)(2,1)S(1)}, u32[]{:S(2)}, u32[]{:S(2)}) collective-permute-start(bf16[1152,128]{1,0:T(8,128)(2,1)S(1)} %get-tuple-element.92), channel_id=1, source_target_pairs={{0,4},{1,17},{2,6},{3,19},{4,0},{5,21},{6,2},{7,23},{8,12},{9,25},... | collective-permute-start | bytes 884744 | tf_op jit(solution)/shard_map/ppermute | solution.py:65
  90.1 6.3 %collective-permute-start.16 = (bf16[2,240,256]{2,1,0:T(8,128)(2,1)S(1)}, bf16[2,240,256]{2,1,0:T(8,128)(2,1)S(1)}, u32[]{:S(2)}, u32[]{:S(2)}) collective-permute-start(bf16[2,240,256]{2,1,0:T(8,128)(2,1)S(1)} %get-tuple-element.79), channel_id=1, source_target_pairs={{0,2},{1,17},{2,0},{3,19},{4,6},{5,21},{6,4},{7,23},{8,10},{9,25},... | collective-permute-start | bytes 737288 | tf_op jit(solution)/shard_map/ppermute | solution.py:65
  91.9 24.5 %collective-permute-start.27 = (bf16[3,128,768]{2,1,0:T(8,128)(2,1)S(1)}, bf16[3,128,768]{2,1,0:T(8,128)(2,1)S(1)}, u32[]{:S(2)}, u32[]{:S(2)}) collective-permute-start(bf16[3,128,768]{2,1,0:T(8,128)(2,1)S(1)} %collective-permute-done.26.near_ref), channel_id=1, source_target_pairs={{0,1},{1,0},{2,3},{3,2},{4,5},{5,4},{6,7},{7,6},{8,9},{9,8},{10,11... | collective-permute-start | bytes 1769480 | tf_op jit(solution)/shard_map/ppermute | solution.py:65
  94.8 10.6 %collective-permute-start.22 = (bf16[672,128]{1,0:T(8,128)(2,1)S(1)}, bf16[672,128]{1,0:T(8,128)(2,1)S(1)}, u32[]{:S(2)}, u32[]{:S(2)}) collective-permute-start(bf16[672,128]{1,0:T(8,128)(2,1)S(1)} %get-tuple-element.95), channel_id=1, source_target_pairs={{0,8},{1,5},{2,10},{3,7},{4,12},{5,1},{6,14},{7,3},{8,0},{9,13},{1... | collective-permute-start | bytes 516104 | tf_op jit(solution)/shard_map/ppermute | solution.py:65
  96.4 15.4 %collective-permute-start.17 = (bf16[1,240,256]{2,1,0:T(8,128)(2,1)S(1)}, bf16[1,240,256]{2,1,0:T(8,128)(2,1)S(1)}, u32[]{:S(2)}, u32[]{:S(2)}) collective-permute-start(bf16[1,240,256]{2,1,0:T(8,128)(2,1)S(1)} %get-tuple-element.81), channel_id=1, source_target_pairs={{0,16},{1,3},{2,18},{3,1},{4,20},{5,7},{6,22},{7,5},{8,24},{9,11},... | collective-permute-start | bytes 368648 | tf_op jit(solution)/shard_map/ppermute | solution.py:65
  105.4 6.5 %collective-permute-start.23 = (bf16[432,128]{1,0:T(8,128)(2,1)S(1)}, bf16[432,128]{1,0:T(8,128)(2,1)S(1)}, u32[]{:S(2)}, u32[]{:S(2)}) collective-permute-start(bf16[432,128]{1,0:T(8,128)(2,1)S(1)} %get-tuple-element.98), channel_id=1, source_target_pairs={{0,16},{1,9},{2,18},{3,11},{4,20},{5,13},{6,22},{7,15},{8,24},{9,1... | collective-permute-start | bytes 331784 | tf_op jit(solution)/shard_map/ppermute | solution.py:65
  112.8 7.1 %collective-permute-start.24 = (f32[168,384]{1,0:T(8,128)S(1)}, f32[168,384]{1,0:T(8,128)S(1)}, u32[]{:S(2)}, u32[]{:S(2)}) collective-permute-start(f32[168,384]{1,0:T(8,128)S(1)} %get-tuple-element.103), channel_id=1, source_target_pairs={{0,1},{1,0},{2,3},{3,2},{4,5},{5,4},{6,7},{7,6},{8,9},{9,8},{10,11... | collective-permute-start | bytes 774152 | tf_op jit(solution)/shard_map/ppermute | solution.py:65

commit v4 on v3

--- a/solution.py
+++ b/solution.py
@@ -290,6 +290,39 @@
     )(own, other, taps, *copied)
 
 
+def conv_near_body(near_ref, taps_ref, sum_ref, out_ref, pad_ref):
+    c = lax.axis_index("col")
+    places, width = sum_ref.shape
+    breadth = near_ref.shape[1] // 2
+    height, stop = places // breadth, LEFT + breadth
+    for core in range(2):
+
+        @pl.when(c == core)
+        def _():
+            if core == 0:
+                pad_ref[:, LEFT : stop + 8, :] = near_ref[:, : breadth + 8, :].astype(F32)
+                pad_ref[:, :LEFT, :] = jnp.zeros((3, LEFT, width), F32)
+            else:
+                pad_ref[:, :stop, :] = near_ref[:, breadth - 8 :, :].astype(F32)
+                pad_ref[:, stop : stop + 8, :] = jnp.zeros((3, 8, width), F32)
+            first = 0 if core == 0 else height + 3
+            lines = [(pad_ref, i, i + first) for i in range(3)]
+            for k in range(0, width, 128):
+                lanes = slice(k, k + 128)
+                sums = [sum_ref[i * breadth : (i + 1) * breadth, lanes] for i in range(height)]
+                sums = convolve(lines, sums, taps_ref, breadth, lanes, False)
+                for i, row in enumerate(sums):
+                    out_ref[i * breadth : (i + 1) * breadth, lanes] = row
+
+
+def conv_near(near, taps, sums):
+    width = sums.shape[1]
+    scratch = [pltpu.VMEM((3, near.shape[1] // 2 + 16, width), F32)]
+    outs = [(sums.shape, F32)]
+    (out,) = call(conv_near_body, outs, 1.5, scratch)(near, taps, sums)
+    return out
+
+
 def conv_norm_body(
     near_ref, far_ref, taps_ref, sum_ref, edge_ref, normed_ref, send_ref, full_ref, inv_ref
 ):
@@ -299,12 +332,18 @@
     steps, half = width // 128, width // 2
     fill_edges(edge_ref, near_ref, far_ref)
 
-    for k in range(0, width, 128):
-        lanes = slice(k, k + 128)
-        sums = [sum_ref[i * breadth : (i + 1) * breadth, lanes] for i in range(height)]
-        sums = convolve(edge_lines(edge_ref, height), sums, taps_ref, breadth, lanes, False)
-        for i, row in enumerate(sums):
-            full_ref[i * breadth : (i + 1) * breadth, lanes] = row
+    c = lax.axis_index("col")
+    for core in range(2):
+        lines = edge_lines(edge_ref, height)[3:] if core == 0 else edge_lines(edge_ref, height)[:3]
+
+        @pl.when(c == core)
+        def _():
+            for k in range(0, width, 128):
+                lanes = slice(k, k + 128)
+                sums = [sum_ref[i * breadth : (i + 1) * breadth, lanes] for i in range(height)]
+                sums = convolve(lines, sums, taps_ref, breadth, lanes, False)
+                for i, row in enumerate(sums):
+                    full_ref[i * breadth : (i + 1) * breadth, lanes] = row
 
     for i in range(0, places, 16):
         rows = slice(i, i + 16)
@@ -548,8 +587,7 @@
         all_ref, send_ref = out_refs[2 * k : 2 * k + 2]
         for j in range(count):
             send_ref[j, :body, :] = all_ref[count + j, :body, :].astype(BF16)
-            sums = all_ref[count + j, body:, :]
-            send_ref[j, body:, :] = jnp.concatenate(split_high_low(sums), axis=0)
+            send_ref[j, body:, :] = all_ref[count + j, body:, :].astype(BF16)
 
 
 def weight_gradient(g_in, g_other, normed, normed_other, h_mine, h_got, s_mine, s_got):
@@ -560,7 +598,7 @@
     outs = []
     for _, wide in CHUNKS:
         outs.append(((rows, height, wide), F32))
-        outs.append(((rows // 2, height + per, wide), BF16))
+        outs.append(((rows // 2, height, wide), BF16))
     return call(functools.partial(weight_body, rows), outs, 5.0, room=12)(
         g_in, g_other, normed, normed_other, h_mine, h_got, s_mine, s_got
     )
@@ -569,7 +607,7 @@
 def merged(keep, got, per):
     body = keep.shape[0] - per
     plain = keep[:body] + got[:body].astype(F32)
-    sums = keep[body:] + (got[body : body + per].astype(F32) + got[body + per :].astype(F32))
+    sums = keep[body:] + got[body:].astype(F32)
     return plain, sums
 
 
@@ -586,7 +624,7 @@
     def far(i, carry):
         plain, sums = merged(old_ref[i + left], got_ref[i + left], per)
         send_ref[i, :body, :] = plain.astype(BF16)
-        send_ref[i, body:, :] = jnp.concatenate(split_high_low(sums), axis=0)
+        send_ref[i, body:, :] = sums.astype(BF16)
         return carry
 
     lax.fori_loop(0, left, far, 0)
@@ -596,7 +634,7 @@
 def halving_round(keep, got, per):
     _, height, wide = keep.shape
     left = got.shape[0] // 2
-    outs = [((left, height, wide), F32), ((left, height + per, wide), BF16)]
+    outs = [((left, height, wide), F32), ((left, height, wide), BF16)]
     return call(functools.partial(round_body, per), outs, 0.5)(keep, got)
 
 
@@ -619,11 +657,11 @@
     per, carried, old_ref, got_ref, taps_ref, taps_got_ref, keep_ref, send_ref, taps_out_ref
 ):
     left = keep_ref.shape[0]
-    height = keep_ref.shape[1] + per
-    body = keep_ref.shape[1] - per
+    height = keep_ref.shape[1]
+    body = height - per
 
     def block(i):
-        at = pl.ds(pl.multiple_of(i * height, 16), height)
+        at = pl.ds(pl.multiple_of(i * height, 8), height)
         return merged(old_ref[i], got_ref[at, :], per)
 
     def near(i, carry):
@@ -634,9 +672,9 @@
 
     def far(i, carry):
         plain, sums = block(i + left)
-        send_ref[pl.ds(pl.multiple_of(i * height, 16), body), :] = plain.astype(BF16)
-        tail = pl.ds(pl.multiple_of(i * height + body, 16), 2 * per)
-        send_ref[tail, :] = jnp.concatenate(split_high_low(sums), axis=0)
+        send_ref[pl.ds(pl.multiple_of(i * height, 8), body), :] = plain.astype(BF16)
+        tail = pl.ds(pl.multiple_of(i * height + body, 8), per)
+        send_ref[tail, :] = sums.astype(BF16)
         return carry
 
     lax.fori_loop(0, left, far, 0)
@@ -644,7 +682,7 @@
     if carried:
         taps = taps_ref[...] + taps_received(got_ref, 2 * left * height, count)
     else:
-        taps = taps_ref[...] + taps_got_ref[...]
+        taps = taps_ref[...].astype(F32) + taps_got_ref[...].astype(F32)
     taps_out_ref[...] = taps.astype(BF16).astype(F32)
     send_ref[left * height :, :] = taps_to_rows(taps).astype(BF16)
     lax.fori_loop(0, left, near, 0)
@@ -655,7 +693,7 @@
     rows = taps.size // wide
     outs = [
         ((left, height, wide), F32),
-        ((left * (height + per) + rows, wide), BF16),
+        ((left * height + rows, wide), BF16),
         (taps.shape, F32),
     ]
     carried = taps_got is None
@@ -667,7 +705,7 @@
     keep_a, got_a, keep_b, got_b, taps_ref, region_ref, count_ref = refs[:7]
     out_ref, mine_ref, send_ref = refs[7:]
     r, c = lax.axis_index("row"), lax.axis_index("col")
-    height = keep_b.shape[1] + per
+    height = keep_b.shape[1]
     done = [merged(keep_a[0], got_a[0], per), merged(keep_b[0], got_b[:height, :], per)]
     plain = jnp.concatenate([d[0] for d in done], axis=1)
     sums = jnp.concatenate([d[1] for d in done], axis=1)
@@ -832,6 +870,7 @@
     known = gather_known(known)
 
     padded, sums, w_in, w_out = local_convolution(own, other, taps, copied=(w_in, w_out))
+    sums = conv_near(near, taps, sums)
     edges, normed, normed_send, full, inv = conv_norm(near, far, taps, sums)
     normed_other = swap_core(normed_send)
     slope, h_mine, h_send, s_mine, s_send = mlp_forward(
@@ -845,7 +884,7 @@
     halves = weight_gradient(g_in, g_other, normed, normed_other, h_mine, h_got, s_mine, s_got)
     per = regions // rows
     part, part_send = kernel_gradient(padded, edges, dconv)
-    part = part + swap_core(part_send)
+    part = (part + swap_core(part_send)).astype(BF16)
     order = orders(bits, 1)
     part_got = exchange(part, (1 << order[0][0], 1 << order[1][0]))
     parts = []

time: 121 us -> 117 us (0.967)
  starting transfers between devices: 47 us -> 38.7 us
  waiting for transfers between devices: 39.3 us -> 43.7 us
    ppermute x26, starting transfers between devices: 45.4 us -> 37.3 us  [exchange(): return lax.ppermute(value, AXES, pairs)]
    ppermute x26, waiting for transfers between devices: 39.3 us -> 43.7 us  [exchange(): return lax.ppermute(value, AXES, pairs)]
    pallas_call x20 -> x21, Pallas kernels: 33.6 us -> 33.3 us  [run(): pl.pallas_call(body, in_specs=specs, out_specs=[VMEM] * len(outs), out_sh...]
  transfers between devices with their start and end apart: 28 -> 28, of which waited for: 11 -> 8; matrix products, arithmetic and copies ran while one was open for 0% -> 0% of each run, Pallas kernels for 24% -> 24%
where the time goes in v4:
time: 117 us
  waiting for transfers between devices  43.7 us (37%)
  starting transfers between devices  38.7 us (33%)
  Pallas kernels  33.3 us (28%)
    ppermute x26, waiting for transfers between devices, exchange(): return lax.ppermute(value, AXES, pairs)  43.7 us
    ppermute x26, starting transfers between devices, exchange(): return lax.ppermute(value, AXES, pairs)  37.3 us
    pallas_call x21, Pallas kernels, run(): pl.pallas_call(body, in_specs=specs, out_specs=[VMEM] * len(outs), out_sh...  33.3 us
  transfers between devices with their start and end apart: 28, of which 8 were waited for; matrix products, arithmetic and copies ran while one was open for 0% of the time, Pallas kernels for 24%

profile of v4, /device:TPU:0, one launch (start us, length us, event | category | flops | bytes accessed | tf_op | source)
XLA Modules:
  0.0 116.7 jit_solution(245205744682802362)
XLA Ops:
  0.6 0.6 collective-permute-start.7
  1.2 1.8 %shard_map.119 = (bf16[8,768]{1,0:T(8,128)(2,1)S(1)}, f32[256,1]{1,0:T(8,128)S(1)}, bf16[4,64,768]{2,1,0:T(8,128)(2,1)S(1)}, f32[49,768]{1,0:T(8,128)S(1)}, f32[1,768]{1,0:T(1,128)S(1)}) custom-call(s32[2,32]{1,0:T(2,128)} %ids_ref.1, s32[1,128]{1,0:T(1,128)} %bitcast.9, bf16[4,768]{1,0:T(4,128)(2,1)} %grad_ref.1, bf16[4,64,768]{2,1,0:T(8,128)(2,1)} %image_ref.1, ...), custom_call_target="tpu_custom_call" | custom-call | bytes 4500000 | tf_op jit(solution)/shard_map/pallas_call | solution.py:44
  3.0 0.0 collective-permute-done.7.refs_1_.other_ref
  3.0 0.1 shard_map.121
  3.1 0.7 collective-permute-start.8
  3.8 4.0 %collective-permute-start = (bf16[8,768]{1,0:T(8,128)(2,1)S(1)}, bf16[8,768]{1,0:T(8,128)(2,1)S(1)}, u32[]{:S(2)}, u32[]{:S(2)}) collective-permute-start(bf16[8,768]{1,0:T(8,128)(2,1)S(1)} %get-tuple-element.58), channel_id=1, source_target_pairs={{0,1},{1,0},{2,3},{3,2},{4,5},{5,4},{6,7},{7,6},{8,9},{9,8},{10,11... | collective-permute-start | bytes 36872 | tf_op jit(solution)/shard_map/ppermute | solution.py:65
  7.7 13.1 %collective-permute-start.9 = (bf16[3,128,768]{2,1,0:T(8,128)(2,1)S(1)}, bf16[3,128,768]{2,1,0:T(8,128)(2,1)S(1)}, u32[]{:S(2)}, u32[]{:S(2)}) collective-permute-start(bf16[3,128,768]{2,1,0:T(8,128)(2,1)S(1)} %collective-permute-done.8.near_ref), channel_id=1, source_target_pairs={{0,1},{1,0},{2,3},{3,2},{4,5},{5,4},{6,7},{7,6},{8,9},{9,8},{10,11... | collective-permute-start | bytes 1769480 | tf_op jit(solution)/shard_map/ppermute | solution.py:65
  20.8 0.0 collective-permute-done
  20.8 2.5 %collective-permute-start.1 = (bf16[16,768]{1,0:T(8,128)(2,1)S(1)}, bf16[16,768]{1,0:T(8,128)(2,1)S(1)}, u32[]{:S(2)}, u32[]{:S(2)}) collective-permute-start(bf16[16,768]{1,0:T(8,128)(2,1)S(1)} %get-tuple-element.111), channel_id=1, source_target_pairs={{0,8},{1,9},{2,10},{3,11},{4,12},{5,13},{6,14},{7,15},{8,0},{9,1},... | collective-permute-start | bytes 73736 | tf_op jit(solution)/shard_map/ppermute | solution.py:65
  23.3 2.5 %collective-permute-start.3 = (bf16[16,768]{1,0:T(8,128)(2,1)S(1)}, bf16[16,768]{1,0:T(8,128)(2,1)S(1)}, u32[]{:S(2)}, u32[]{:S(2)}) collective-permute-start(bf16[16,768]{1,0:T(8,128)(2,1)S(1)} %get-tuple-element.111), channel_id=1, source_target_pairs={{0,24},{1,25},{2,26},{3,27},{4,28},{5,29},{6,30},{7,31},{8,16},{9,... | collective-permute-start | bytes 73736 | tf_op jit(solution)/shard_map/ppermute | solution.py:65
  25.8 0.1 collective-permute-start.2
  25.9 0.0 collective-permute-done.1
  25.9 4.9 %collective-permute-done.2 = bf16[16,768]{1,0:T(8,128)(2,1)S(1)} collective-permute-done((bf16[16,768]{1,0:T(8,128)(2,1)S(1)}, bf16[16,768]{1,0:T(8,128)(2,1)S(1)}, u32[]{:S(2)}, u32[]{:S(2)}) %collective-permute-start.2) | collective-permute-done | bytes 24608 | tf_op jit(solution)/shard_map/ppermute | solution.py:65
  30.8 2.0 %collective-permute-start.6 = (bf16[64,768]{1,0:T(8,128)(2,1)S(1)}, bf16[64,768]{1,0:T(8,128)(2,1)S(1)}, u32[]{:S(2)}, u32[]{:S(2)}) collective-permute-start(bf16[64,768]{1,0:T(8,128)(2,1)S(1)} %constant_dynamic-update-slice_fusion.2.refs_0_), channel_id=1, source_target_pairs={{0,6},{1,7},{2,4},{3,5},{4,2},{5,3},{6,0},{7,1},{8,14},{9,15},{10,... | collective-permute-start | bytes 294920 | tf_op jit(solution)/shard_map/ppermute | solution.py:65
  32.8 1.8 %collective-permute-start.5 = (bf16[64,768]{1,0:T(8,128)(2,1)S(1)}, bf16[64,768]{1,0:T(8,128)(2,1)S(1)}, u32[]{:S(2)}, u32[]{:S(2)}) collective-permute-start(bf16[64,768]{1,0:T(8,128)(2,1)S(1)} %constant_dynamic-update-slice_fusion.2.refs_0_), channel_id=1, source_target_pairs={{0,4},{1,5},{2,6},{3,7},{4,0},{5,1},{6,2},{7,3},{8,12},{9,13},{10,... | collective-permute-start | bytes 294920 | tf_op jit(solution)/shard_map/ppermute | solution.py:65
  34.6 0.0 collective-permute-start.4
  34.6 3.8 %shard_map.120 = (f32[4,80,768]{2,1,0:T(8,128)S(1)}, f32[256,768]{1,0:T(8,128)S(1)}, bf16[768,3072]{1,0:T(8,128)(2,1)S(1)}, bf16[3072,768]{1,0:T(8,128)(2,1)S(1)}) custom-call(bf16[4,64,768]{2,1,0:T(8,128)(2,1)S(1)} %get-tuple-element.61.refs_0_.own_ref, bf16[4,64,768]{2,1,0:T(8,128)(2,1)S(1)} %collective-permute-done.7.refs_1_.other_ref, ...), custom_call_target="tpu_custom_call" | custom-call | bytes 12000000 | tf_op jit(solution)/shard_map/pallas_call | solution.py:44
  38.4 1.1 shard_map.122.sum_ref
  39.5 0.0 collective-permute-done.9.far_ref
  39.5 1.9 %shard_map.123 = (f32[6,80,768]{2,1,0:T(8,128)S(1)}, bf16[256,768]{1,0:T(8,128)(2,1)S(1)}, bf16[256,384]{1,0:T(8,128)(2,1)S(1)}, f32[256,768]{1,0:T(8,128)S(1)}, f32[256,128]{1,0:T(8,128)S(1)}) custom-call(bf16[3,128,768]{2,1,0:T(8,128)(2,1)S(1)} %collective-permute-done.8.near_ref, bf16[3,128,768]{2,1,0:T(8,128)(2,1)S(1)} %collective-permute-done.9.far_ref, ...), custom_call_target="tpu_custom_call" | custom-call | bytes 15000000 | tf_op jit(solution)/shard_map/pallas_call | solution.py:44
  41.4 3.8 %shard_map.124 = (f32[256,3072]{1,0:T(8,128)S(1)}, f32[16,32,384]{2,1,0:T(8,128)S(1)}, bf16[16,32,384]{2,1,0:T(8,128)(2,1)S(1)}, f32[128,384]{1,0:T(8,128)S(1)}, f32[128,384]{1,0:T(8,128)S(1)}) custom-call(bf16[256,768]{1,0:T(8,128)(2,1)S(1)} %get-tuple-element.65.normed_ref, bf16[768,3072]{1,0:T(8,128)(2,1)S(1)} %get-tuple-element.66.w_in_ref, ...), custom_call_target="tpu_custom_call" | custom-call | bytes 27000000 | tf_op jit(solution)/shard_map/pallas_call | solution.py:44
  45.2 0.0 collective-permute-done.6.refs_3_
  45.2 0.0 collective-permute-done.4.refs_1_
  45.2 1.9 %shard_map.125 = (bf16[256,3072]{1,0:T(8,128)(2,1)S(1)}, bf16[128,768]{1,0:T(8,128)(2,1)S(1)}, bf16[256,768]{1,0:T(8,128)(2,1)S(1)}, f32[128,128]{1,0:T(8,128)S(1)}) custom-call(bf16[64,768]{1,0:T(8,128)(2,1)S(1)} %constant_dynamic-update-slice_fusion.2.refs_0_, bf16[64,768]{1,0:T(8,128)(2,1)S(1)} %collective-permute-done.4.refs_1_, ...), custom_call_target="tpu_custom_call" | custom-call | bytes 12000000 | tf_op jit(solution)/shard_map/pallas_call | solution.py:44
  47.1 0.1 collective-permute-start.10
  47.2 0.5 collective-permute-start.12
  47.7 0.1 collective-permute-start.11
  47.8 0.4 collective-permute-start.13
  48.2 3.2 %collective-permute-done.11.normed_other_ref = bf16[256,384]{1,0:T(8,128)(2,1)S(1)} collective-permute-done((bf16[256,384]{1,0:T(8,128)(2,1)S(1)}, bf16[256,384]{1,0:T(8,128)(2,1)S(1)}, u32[]{:S(2)}, u32[]{:S(2)}) %collective-permute-start.11) | collective-permute-done | bytes 196640 | tf_op jit(solution)/shard_map/ppermute | solution.py:65
  51.4 0.3 collective-permute-done.13.s_got_ref
  51.7 0.0 collective-permute-done.12.h_got_ref
  51.7 0.0 collective-permute-done.10.other_ref
  51.7 2.0 %shard_map.126 = (f32[16,232,256]{2,1,0:T(8,128)S(1)}, bf16[8,232,256]{2,1,0:T(8,128)(2,1)S(1)}, f32[16,232,128]{2,1,0:T(8,128)S(1)}, bf16[8,232,128]{2,1,0:T(8,128)(2,1)S(1)}) custom-call(bf16[256,3072]{1,0:T(8,128)(2,1)S(1)} %get-tuple-element.68.own_ref.g_in_ref, bf16[256,3072]{1,0:T(8,128)(2,1)S(1)} %collective-permute-done.10.other_ref, ...), custom_call_target="tpu_custom_call" | custom-call | bytes 15000000 | tf_op jit(solution)/shard_map/pallas_call | solution.py:44
  53.8 2.0 %collective-permute-start.14 = (bf16[8,232,256]{2,1,0:T(8,128)(2,1)S(1)}, bf16[8,232,256]{2,1,0:T(8,128)(2,1)S(1)}, u32[]{:S(2)}, u32[]{:S(2)}) collective-permute-start(bf16[8,232,256]{2,1,0:T(8,128)(2,1)S(1)} %get-tuple-element.75), channel_id=1, source_target_pairs={{0,4},{1,9},{2,6},{3,11},{4,0},{5,13},{6,2},{7,15},{8,12},{9,1},{1... | collective-permute-start | bytes 2850824 | tf_op jit(solution)/shard_map/ppermute | solution.py:65
  55.8 1.6 %shard_map.130 = (f32[256,768]{1,0:T(8,128)S(1)}, bf16[256,768]{1,0:T(8,128)(2,1)S(1)}) custom-call(bf16[256,3072]{1,0:T(8,128)(2,1)S(1)} %get-tuple-element.68.own_ref.g_in_ref, bf16[768,3072]{1,0:T(8,128)(2,1)S(1)} %get-tuple-element.66.w_in_ref, f32[256,768]{1,0:T(8,128)S(1)} %get-tuple-element.86.full_ref, f32[256,128]{1,0:T(8,128)S(1)} %get-tuple-element.87.inv_ref), custom_call_target="tpu_custom_call" | custom-call | bytes 12000000 | tf_op jit(solution)/shard_map/pallas_call | solution.py:44
  57.3 0.1 collective-permute-start.25
  57.4 0.5 collective-permute-start.18
  57.9 5.6 %shard_map.131 = (f32[32,768]{1,0:T(8,128)S(1)}, f32[32,768]{1,0:T(8,128)S(1)}) custom-call(f32[4,80,768]{2,1,0:T(8,128)S(1)} %get-tuple-element.84.pad_ref, f32[6,80,768]{2,1,0:T(8,128)S(1)} %get-tuple-element.85.edge_ref, f32[256,768]{1,0:T(8,128)S(1)} %get-tuple-element.88.dconv_ref.refs_0_), custom_call_target="tpu_custom_call" | custom-call | bytes 15000000 | tf_op jit(solution)/shard_map/pallas_call | solution.py:44
  63.5 0.2 collective-permute-start.19
  63.8 0.7 collective-permute-start.26
  64.5 3.1 %collective-permute-done.14.got_ref = bf16[8,232,256]{2,1,0:T(8,128)(2,1)S(1)} collective-permute-done((bf16[8,232,256]{2,1,0:T(8,128)(2,1)S(1)}, bf16[8,232,256]{2,1,0:T(8,128)(2,1)S(1)}, u32[]{:S(2)}, u32[]{:S(2)}) %collective-permute-start.14) | collective-permute-done | bytes 950304 | tf_op jit(solution)/shard_map/ppermute | solution.py:65
  67.6 0.2 shard_map.127
  67.8 0.9 collective-permute-start.15
  68.7 0.0 collective-permute-done.19
  68.8 1.7 %collective-permute-start.20 = (bf16[32,768]{1,0:T(8,128)(2,1)S(1)}, bf16[32,768]{1,0:T(8,128)(2,1)S(1)}, u32[]{:S(2)}, u32[]{:S(2)}) collective-permute-start(bf16[32,768]{1,0:T(8,128)(2,1)S(1)} %add_convert_fusion.taps_ref), channel_id=1, source_target_pairs={{0,2},{1,3},{2,0},{3,1},{4,6},{5,7},{6,4},{7,5},{8,10},{9,11},{10,... | collective-permute-start | bytes 147464 | tf_op jit(solution)/shard_map/ppermute | solution.py:65
  70.5 13.9 %collective-permute-done.20.taps_got_ref = bf16[32,768]{1,0:T(8,128)(2,1)S(1)} collective-permute-done((bf16[32,768]{1,0:T(8,128)(2,1)S(1)}, bf16[32,768]{1,0:T(8,128)(2,1)S(1)}, u32[]{:S(2)}, u32[]{:S(2)}) %collective-permute-start.20) | collective-permute-done | bytes 49184 | tf_op jit(solution)/shard_map/ppermute | solution.py:65
  84.4 0.0 collective-permute-done.18
  84.4 0.1 shard_map.132
  84.5 0.1 collective-permute-start.21
  84.6 0.1 shard_map.128
  84.7 2.2 %collective-permute-start.16 = (bf16[2,232,256]{2,1,0:T(8,128)(2,1)S(1)}, bf16[2,232,256]{2,1,0:T(8,128)(2,1)S(1)}, u32[]{:S(2)}, u32[]{:S(2)}) collective-permute-start(bf16[2,232,256]{2,1,0:T(8,128)(2,1)S(1)} %get-tuple-element.79), channel_id=1, source_target_pairs={{0,2},{1,17},{2,0},{3,19},{4,6},{5,21},{6,4},{7,23},{8,10},{9,25},... | collective-permute-start | bytes 712712 | tf_op jit(solution)/shard_map/ppermute | solution.py:65
  86.9 0.0 collective-permute-done.26.near_ref
  86.9 4.3 %collective-permute-done.21.got_ref = bf16[1120,128]{1,0:T(8,128)(2,1)S(1)} collective-permute-done((bf16[1120,128]{1,0:T(8,128)(2,1)S(1)}, bf16[1120,128]{1,0:T(8,128)(2,1)S(1)}, u32[]{:S(2)}, u32[]{:S(2)}) %collective-permute-start.21) | collective-permute-done | bytes 286752 | tf_op jit(solution)/shard_map/ppermute | solution.py:65
  91.2 0.1 shard_map.133
  91.3 0.6 collective-permute-start.22
  91.9 0.1 shard_map.129
  92.0 1.5 %collective-permute-start.17 = (bf16[1,232,256]{2,1,0:T(8,128)(2,1)S(1)}, bf16[1,232,256]{2,1,0:T(8,128)(2,1)S(1)}, u32[]{:S(2)}, u32[]{:S(2)}) collective-permute-start(bf16[1,232,256]{2,1,0:T(8,128)(2,1)S(1)} %get-tuple-element.81), channel_id=1, source_target_pairs={{0,16},{1,3},{2,18},{3,1},{4,20},{5,7},{6,22},{7,5},{8,24},{9,11},... | collective-permute-start | bytes 356360 | tf_op jit(solution)/shard_map/ppermute | solution.py:65
  93.4 8.2 %collective-permute-done.22.got_ref = bf16[656,128]{1,0:T(8,128)(2,1)S(1)} collective-permute-done((bf16[656,128]{1,0:T(8,128)(2,1)S(1)}, bf16[656,128]{1,0:T(8,128)(2,1)S(1)}, u32[]{:S(2)}, u32[]{:S(2)}) %collective-permute-start.22) | collective-permute-done | bytes 167968 | tf_op jit(solution)/shard_map/ppermute | solution.py:65
  101.7 0.1 collective-permute-start.23
  101.7 5.8 %collective-permute-done.23.refs_3_ = bf16[424,128]{1,0:T(8,128)(2,1)S(1)} collective-permute-done((bf16[424,128]{1,0:T(8,128)(2,1)S(1)}, bf16[424,128]{1,0:T(8,128)(2,1)S(1)}, u32[]{:S(2)}, u32[]{:S(2)}) %collective-permute-start.23) | collective-permute-done | bytes 108576 | tf_op jit(solution)/shard_map/ppermute | solution.py:65
  107.5 1.0 shard_map.135
  108.5 3.9 %shard_map.138 = (f32[4,80,768]{2,1,0:T(8,128)}, f32[256,768]{1,0:T(8,128)S(1)}) custom-call(f32[256,768]{1,0:T(8,128)S(1)} %get-tuple-element.88.dconv_ref.refs_0_, bf16[4,64,768]{2,1,0:T(8,128)(2,1)S(1)} %collective-permute-done.25.other_ref.refs_1_, f32[49,768]{1,0:T(8,128)S(1)} %get-tuple-element.62.refs_2_.taps_ref), custom_call_target="tpu_custom_call" | custom-call | bytes 12000000 | tf_op jit(solution)/shard_map/pallas_call | solution.py:44
  112.4 3.5 %shard_map.139 = bf16[4,64,768]{2,1,0:T(8,128)(2,1)} custom-call(bf16[3,128,768]{2,1,0:T(8,128)(2,1)S(1)} %collective-permute-done.26.near_ref, bf16[3,128,768]{2,1,0:T(8,128)(2,1)S(1)} %collective-permute-done.27.far_ref, f32[49,768]{1,0:T(8,128)S(1)} %get-tuple-element.62.refs_2_.taps_ref, f32[256,768]{1,0:T(8,128)S(1)} %get-tuple-element.106.sum_ref, ...), custom_call_target="tpu_custom_call" | custom-call | bytes 9000000 | tf_op jit(solution)/shard_map/pallas_call | solution.py:44
  115.9 0.8 shard_map.136
  (19 shorter events, 0.1 us)
Async XLA Ops:
  0.6 2.4 %collective-permute-start.7 = (bf16[4,64,768]{2,1,0:T(8,128)(2,1)}, bf16[4,64,768]{2,1,0:T(8,128)(2,1)S(1)}, u32[]{:S(2)}, u32[]{:S(2)}) collective-permute-start(bf16[4,64,768]{2,1,0:T(8,128)(2,1)} %image_ref.1), channel_id=1, source_target_pairs={{0,1},{1,0},{2,3},{3,2},{4,5},{5,4},{6,7},{7,6},{8,9},{9,8},{10,11... | collective-permute-start | bytes 1179656 | tf_op jit(solution)/shard_map/ppermute | solution.py:65
  3.1 4.7 %collective-permute-start.8 = (bf16[3,128,768]{2,1,0:T(8,128)(2,1)S(1)}, bf16[3,128,768]{2,1,0:T(8,128)(2,1)S(1)}, u32[]{:S(2)}, u32[]{:S(2)}) collective-permute-start(bf16[3,128,768]{2,1,0:T(8,128)(2,1)S(1)} %shard_map.121), channel_id=1, source_target_pairs={{1,2},{2,1},{3,4},{4,3},{5,6},{6,5},{7,8},{8,7},{9,10},{10,9},{11,... | collective-permute-start | bytes 1769480 | tf_op jit(solution)/shard_map/ppermute | solution.py:78
  3.8 17.0 %collective-permute-start = (bf16[8,768]{1,0:T(8,128)(2,1)S(1)}, bf16[8,768]{1,0:T(8,128)(2,1)S(1)}, u32[]{:S(2)}, u32[]{:S(2)}) collective-permute-start(bf16[8,768]{1,0:T(8,128)(2,1)S(1)} %get-tuple-element.58), channel_id=1, source_target_pairs={{0,1},{1,0},{2,3},{3,2},{4,5},{5,4},{6,7},{7,6},{8,9},{9,8},{10,11... | collective-permute-start | bytes 36872 | tf_op jit(solution)/shard_map/ppermute | solution.py:65
  7.7 31.8 %collective-permute-start.9 = (bf16[3,128,768]{2,1,0:T(8,128)(2,1)S(1)}, bf16[3,128,768]{2,1,0:T(8,128)(2,1)S(1)}, u32[]{:S(2)}, u32[]{:S(2)}) collective-permute-start(bf16[3,128,768]{2,1,0:T(8,128)(2,1)S(1)} %collective-permute-done.8.near_ref), channel_id=1, source_target_pairs={{0,1},{1,0},{2,3},{3,2},{4,5},{5,4},{6,7},{7,6},{8,9},{9,8},{10,11... | collective-permute-start | bytes 1769480 | tf_op jit(solution)/shard_map/ppermute | solution.py:65
  20.8 5.1 %collective-permute-start.1 = (bf16[16,768]{1,0:T(8,128)(2,1)S(1)}, bf16[16,768]{1,0:T(8,128)(2,1)S(1)}, u32[]{:S(2)}, u32[]{:S(2)}) collective-permute-start(bf16[16,768]{1,0:T(8,128)(2,1)S(1)} %get-tuple-element.111), channel_id=1, source_target_pairs={{0,8},{1,9},{2,10},{3,11},{4,12},{5,13},{6,14},{7,15},{8,0},{9,1},... | collective-permute-start | bytes 73736 | tf_op jit(solution)/shard_map/ppermute | solution.py:65
  23.3 7.5 %collective-permute-start.3 = (bf16[16,768]{1,0:T(8,128)(2,1)S(1)}, bf16[16,768]{1,0:T(8,128)(2,1)S(1)}, u32[]{:S(2)}, u32[]{:S(2)}) collective-permute-start(bf16[16,768]{1,0:T(8,128)(2,1)S(1)} %get-tuple-element.111), channel_id=1, source_target_pairs={{0,24},{1,25},{2,26},{3,27},{4,28},{5,29},{6,30},{7,31},{8,16},{9,... | collective-permute-start | bytes 73736 | tf_op jit(solution)/shard_map/ppermute | solution.py:65
  25.8 5.0 %collective-permute-start.2 = (bf16[16,768]{1,0:T(8,128)(2,1)S(1)}, bf16[16,768]{1,0:T(8,128)(2,1)S(1)}, u32[]{:S(2)}, u32[]{:S(2)}) collective-permute-start(bf16[16,768]{1,0:T(8,128)(2,1)S(1)} %get-tuple-element.111), channel_id=1, source_target_pairs={{0,16},{1,17},{2,18},{3,19},{4,20},{5,21},{6,22},{7,23},{8,24},{9,... | collective-permute-start | bytes 73736 | tf_op jit(solution)/shard_map/ppermute | solution.py:65
  30.8 14.4 %collective-permute-start.6 = (bf16[64,768]{1,0:T(8,128)(2,1)S(1)}, bf16[64,768]{1,0:T(8,128)(2,1)S(1)}, u32[]{:S(2)}, u32[]{:S(2)}) collective-permute-start(bf16[64,768]{1,0:T(8,128)(2,1)S(1)} %constant_dynamic-update-slice_fusion.2.refs_0_), channel_id=1, source_target_pairs={{0,6},{1,7},{2,4},{3,5},{4,2},{5,3},{6,0},{7,1},{8,14},{9,15},{10,... | collective-permute-start | bytes 294920 | tf_op jit(solution)/shard_map/ppermute | solution.py:65
  32.8 12.4 %collective-permute-start.5 = (bf16[64,768]{1,0:T(8,128)(2,1)S(1)}, bf16[64,768]{1,0:T(8,128)(2,1)S(1)}, u32[]{:S(2)}, u32[]{:S(2)}) collective-permute-start(bf16[64,768]{1,0:T(8,128)(2,1)S(1)} %constant_dynamic-update-slice_fusion.2.refs_0_), channel_id=1, source_target_pairs={{0,4},{1,5},{2,6},{3,7},{4,0},{5,1},{6,2},{7,3},{8,12},{9,13},{10,... | collective-permute-start | bytes 294920 | tf_op jit(solution)/shard_map/ppermute | solution.py:65
  34.6 10.6 %collective-permute-start.4 = (bf16[64,768]{1,0:T(8,128)(2,1)S(1)}, bf16[64,768]{1,0:T(8,128)(2,1)S(1)}, u32[]{:S(2)}, u32[]{:S(2)}) collective-permute-start(bf16[64,768]{1,0:T(8,128)(2,1)S(1)} %constant_dynamic-update-slice_fusion.2.refs_0_), channel_id=1, source_target_pairs={{0,2},{1,3},{2,0},{3,1},{4,6},{5,7},{6,4},{7,5},{8,10},{9,11},{10,... | collective-permute-start | bytes 294920 | tf_op jit(solution)/shard_map/ppermute | solution.py:65
  47.1 4.6 %collective-permute-start.10 = (bf16[256,3072]{1,0:T(8,128)(2,1)S(1)}, bf16[256,3072]{1,0:T(8,128)(2,1)S(1)}, u32[]{:S(2)}, u32[]{:S(2)}) collective-permute-start(bf16[256,3072]{1,0:T(8,128)(2,1)S(1)} %get-tuple-element.68.own_ref.g_in_ref), channel_id=1, source_target_pairs={{0,1},{1,0},{2,3},{3,2},{4,5},{5,4},{6,7},{7,6},{8,9},{9,8},{10,11... | collective-permute-start | bytes 4718600 | tf_op jit(solution)/shard_map/ppermute | solution.py:65
  47.2 4.5 %collective-permute-start.12 = (bf16[16,32,384]{2,1,0:T(8,128)(2,1)S(1)}, bf16[16,32,384]{2,1,0:T(8,128)(2,1)S(1)}, u32[]{:S(2)}, u32[]{:S(2)}) collective-permute-start(bf16[16,32,384]{2,1,0:T(8,128)(2,1)S(1)} %get-tuple-element.71), channel_id=1, source_target_pairs={{0,1},{1,0},{2,3},{3,2},{4,5},{5,4},{6,7},{7,6},{8,9},{9,8},{10,11... | collective-permute-start | bytes 1179656 | tf_op jit(solution)/shard_map/ppermute | solution.py:65
  47.7 3.7 %collective-permute-start.11 = (bf16[256,384]{1,0:T(8,128)(2,1)S(1)}, bf16[256,384]{1,0:T(8,128)(2,1)S(1)}, u32[]{:S(2)}, u32[]{:S(2)}) collective-permute-start(bf16[256,384]{1,0:T(8,128)(2,1)S(1)} %get-tuple-element.69), channel_id=1, source_target_pairs={{0,1},{1,0},{2,3},{3,2},{4,5},{5,4},{6,7},{7,6},{8,9},{9,8},{10,11... | collective-permute-start | bytes 589832 | tf_op jit(solution)/shard_map/ppermute | solution.py:65
  47.8 3.9 %collective-permute-start.13 = (f32[128,384]{1,0:T(8,128)S(1)}, f32[128,384]{1,0:T(8,128)S(1)}, u32[]{:S(2)}, u32[]{:S(2)}) collective-permute-start(f32[128,384]{1,0:T(8,128)S(1)} %get-tuple-element.73), channel_id=1, source_target_pairs={{0,1},{1,0},{2,3},{3,2},{4,5},{5,4},{6,7},{7,6},{8,9},{9,8},{10,11... | collective-permute-start | bytes 589832 | tf_op jit(solution)/shard_map/ppermute | solution.py:65
  53.8 13.8 %collective-permute-start.14 = (bf16[8,232,256]{2,1,0:T(8,128)(2,1)S(1)}, bf16[8,232,256]{2,1,0:T(8,128)(2,1)S(1)}, u32[]{:S(2)}, u32[]{:S(2)}) collective-permute-start(bf16[8,232,256]{2,1,0:T(8,128)(2,1)S(1)} %get-tuple-element.75), channel_id=1, source_target_pairs={{0,4},{1,9},{2,6},{3,11},{4,0},{5,13},{6,2},{7,15},{8,12},{9,1},{1... | collective-permute-start | bytes 2850824 | tf_op jit(solution)/shard_map/ppermute | solution.py:65
  57.3 6.4 %collective-permute-start.25 = (bf16[4,64,768]{2,1,0:T(8,128)(2,1)S(1)}, bf16[4,64,768]{2,1,0:T(8,128)(2,1)S(1)}, u32[]{:S(2)}, u32[]{:S(2)}) collective-permute-start(bf16[4,64,768]{2,1,0:T(8,128)(2,1)S(1)} %bitcast.7), channel_id=1, source_target_pairs={{0,1},{1,0},{2,3},{3,2},{4,5},{5,4},{6,7},{7,6},{8,9},{9,8},{10,11... | collective-permute-start | bytes 1179656 | tf_op jit(solution)/shard_map/ppermute | solution.py:65
  57.4 27.0 %collective-permute-start.18 = (bf16[8,232,128]{2,1,0:T(8,128)(2,1)S(1)}, bf16[8,232,128]{2,1,0:T(8,128)(2,1)S(1)}, u32[]{:S(2)}, u32[]{:S(2)}) collective-permute-start(bf16[8,232,128]{2,1,0:T(8,128)(2,1)S(1)} %get-tuple-element.83), channel_id=1, source_target_pairs={{0,2},{1,3},{2,0},{3,1},{4,6},{5,7},{6,4},{7,5},{8,10},{9,11},{10,... | collective-permute-start | bytes 1425416 | tf_op jit(solution)/shard_map/ppermute | solution.py:65
  63.5 5.3 %collective-permute-start.19 = (f32[32,768]{1,0:T(8,128)S(1)}, f32[32,768]{1,0:T(8,128)S(1)}, u32[]{:S(2)}, u32[]{:S(2)}) collective-permute-start(f32[32,768]{1,0:T(8,128)S(1)} %get-tuple-element.90), channel_id=1, source_target_pairs={{0,1},{1,0},{2,3},{3,2},{4,5},{5,4},{6,7},{7,6},{8,9},{9,8},{10,11... | collective-permute-start | bytes 294920 | tf_op jit(solution)/shard_map/ppermute | solution.py:65
  63.8 23.2 %collective-permute-start.26 = (bf16[3,128,768]{2,1,0:T(8,128)(2,1)S(1)}, bf16[3,128,768]{2,1,0:T(8,128)(2,1)S(1)}, u32[]{:S(2)}, u32[]{:S(2)}) collective-permute-start(bf16[3,128,768]{2,1,0:T(8,128)(2,1)S(1)} %shard_map.137), channel_id=1, source_target_pairs={{1,2},{2,1},{3,4},{4,3},{5,6},{6,5},{7,8},{8,7},{9,10},{10,9},{11,... | collective-permute-start | bytes 1769480 | tf_op jit(solution)/shard_map/ppermute | solution.py:78
  67.8 16.8 %collective-permute-start.15 = (bf16[4,232,256]{2,1,0:T(8,128)(2,1)S(1)}, bf16[4,232,256]{2,1,0:T(8,128)(2,1)S(1)}, u32[]{:S(2)}, u32[]{:S(2)}) collective-permute-start(bf16[4,232,256]{2,1,0:T(8,128)(2,1)S(1)} %get-tuple-element.77), channel_id=1, source_target_pairs={{0,8},{1,5},{2,10},{3,7},{4,12},{5,1},{6,14},{7,3},{8,0},{9,13},{1... | collective-permute-start | bytes 1425416 | tf_op jit(solution)/shard_map/ppermute | solution.py:65
  68.8 15.6 %collective-permute-start.20 = (bf16[32,768]{1,0:T(8,128)(2,1)S(1)}, bf16[32,768]{1,0:T(8,128)(2,1)S(1)}, u32[]{:S(2)}, u32[]{:S(2)}) collective-permute-start(bf16[32,768]{1,0:T(8,128)(2,1)S(1)} %add_convert_fusion.taps_ref), channel_id=1, source_target_pairs={{0,2},{1,3},{2,0},{3,1},{4,6},{5,7},{6,4},{7,5},{8,10},{9,11},{10,... | collective-permute-start | bytes 147464 | tf_op jit(solution)/shard_map/ppermute | solution.py:65
  84.5 6.7 %collective-permute-start.21 = (bf16[1120,128]{1,0:T(8,128)(2,1)S(1)}, bf16[1120,128]{1,0:T(8,128)(2,1)S(1)}, u32[]{:S(2)}, u32[]{:S(2)}) collective-permute-start(bf16[1120,128]{1,0:T(8,128)(2,1)S(1)} %get-tuple-element.92), channel_id=1, source_target_pairs={{0,4},{1,17},{2,6},{3,19},{4,0},{5,21},{6,2},{7,23},{8,12},{9,25},... | collective-permute-start | bytes 860168 | tf_op jit(solution)/shard_map/ppermute | solution.py:65
  84.7 7.1 %collective-permute-start.16 = (bf16[2,232,256]{2,1,0:T(8,128)(2,1)S(1)}, bf16[2,232,256]{2,1,0:T(8,128)(2,1)S(1)}, u32[]{:S(2)}, u32[]{:S(2)}) collective-permute-start(bf16[2,232,256]{2,1,0:T(8,128)(2,1)S(1)} %get-tuple-element.79), channel_id=1, source_target_pairs={{0,2},{1,17},{2,0},{3,19},{4,6},{5,21},{6,4},{7,23},{8,10},{9,25},... | collective-permute-start | bytes 712712 | tf_op jit(solution)/shard_map/ppermute | solution.py:65
  86.9 25.4 %collective-permute-start.27 = (bf16[3,128,768]{2,1,0:T(8,128)(2,1)S(1)}, bf16[3,128,768]{2,1,0:T(8,128)(2,1)S(1)}, u32[]{:S(2)}, u32[]{:S(2)}) collective-permute-start(bf16[3,128,768]{2,1,0:T(8,128)(2,1)S(1)} %collective-permute-done.26.near_ref), channel_id=1, source_target_pairs={{0,1},{1,0},{2,3},{3,2},{4,5},{5,4},{6,7},{7,6},{8,9},{9,8},{10,11... | collective-permute-start | bytes 1769480 | tf_op jit(solution)/shard_map/ppermute | solution.py:65
  91.3 10.3 %collective-permute-start.22 = (bf16[656,128]{1,0:T(8,128)(2,1)S(1)}, bf16[656,128]{1,0:T(8,128)(2,1)S(1)}, u32[]{:S(2)}, u32[]{:S(2)}) collective-permute-start(bf16[656,128]{1,0:T(8,128)(2,1)S(1)} %get-tuple-element.95), channel_id=1, source_target_pairs={{0,8},{1,5},{2,10},{3,7},{4,12},{5,1},{6,14},{7,3},{8,0},{9,13},{1... | collective-permute-start | bytes 503816 | tf_op jit(solution)/shard_map/ppermute | solution.py:65
  92.0 15.6 %collective-permute-start.17 = (bf16[1,232,256]{2,1,0:T(8,128)(2,1)S(1)}, bf16[1,232,256]{2,1,0:T(8,128)(2,1)S(1)}, u32[]{:S(2)}, u32[]{:S(2)}) collective-permute-start(bf16[1,232,256]{2,1,0:T(8,128)(2,1)S(1)} %get-tuple-element.81), channel_id=1, source_target_pairs={{0,16},{1,3},{2,18},{3,1},{4,20},{5,7},{6,22},{7,5},{8,24},{9,11},... | collective-permute-start | bytes 356360 | tf_op jit(solution)/shard_map/ppermute | solution.py:65
  101.7 5.9 %collective-permute-start.23 = (bf16[424,128]{1,0:T(8,128)(2,1)S(1)}, bf16[424,128]{1,0:T(8,128)(2,1)S(1)}, u32[]{:S(2)}, u32[]{:S(2)}) collective-permute-start(bf16[424,128]{1,0:T(8,128)(2,1)S(1)} %get-tuple-element.98), channel_id=1, source_target_pairs={{0,16},{1,9},{2,18},{3,11},{4,20},{5,13},{6,22},{7,15},{8,24},{9,1... | collective-permute-start | bytes 325640 | tf_op jit(solution)/shard_map/ppermute | solution.py:65
  108.5 7.4 %collective-permute-start.24 = (f32[168,384]{1,0:T(8,128)S(1)}, f32[168,384]{1,0:T(8,128)S(1)}, u32[]{:S(2)}, u32[]{:S(2)}) collective-permute-start(f32[168,384]{1,0:T(8,128)S(1)} %get-tuple-element.103), channel_id=1, source_target_pairs={{0,1},{1,0},{2,3},{3,2},{4,5},{5,4},{6,7},{7,6},{8,9},{9,8},{10,11... | collective-permute-start | bytes 774152 | tf_op jit(solution)/shard_map/ppermute | solution.py:65
